TPU v7x, 32 devices: a whole 2x2x4 slice. The times are simulated.
32 devices in a mesh: fsdp: 8 (over z, x), ctx: 4 (over y, core).
Axes of the slice: x: 2, y: 2, z: 4, core: 2. Of those that a mesh axis runs over, the one named last changes fastest.
Arguments:
- inputs: bfloat16 [8, 1024, 2048], P('fsdp', 'ctx'), may hold values from -6 to 6
- cotangent: bfloat16 [8, 1024, 2048], P('fsdp', 'ctx'), may hold values from -6 to 6
- lengths: int32 [8], P('fsdp'), may hold values from 1024 to 1024, as said below
- qkv_weight: bfloat16 [2048, 1536], P('fsdp'), may hold values from -0.125 to 0.125
- out_weight: bfloat16 [1024, 2048], P('fsdp'), may hold values from -3 to 3
- gate_up: bfloat16 [2048, 2, 4096], P('fsdp'), may hold values from -0.125 to 0.125
- down_weight: bfloat16 [4096, 2048], P('fsdp'), may hold values from -0.09375 to 0.09375
- attn_gain: bfloat16 [2048], P('fsdp'), may hold values from 0.5 to 1.5
- ffn_gain: bfloat16 [2048], P('fsdp'), may hold values from 0.5 to 1.5
- qk_gain: bfloat16 [2, 64], replicated, may hold values from 0.5 to 1.5
Outputs:
- layer_out: bfloat16 [8, 1024, 2048], P('fsdp', 'ctx')
- input_grad: bfloat16 [8, 1024, 2048], P('fsdp', 'ctx')
- qkv_grad: float32 [2048, 1536], P('fsdp')
- out_grad: float32 [1024, 2048], P('fsdp')
- gate_up_grad: float32 [2048, 2, 4096], P('fsdp')
- down_grad: float32 [4096, 2048], P('fsdp')
- attn_gain_grad: float32 [2048], P('fsdp')
- ffn_gain_grad: float32 [2048], P('fsdp')
- qk_gain_grad: float32 [2, 64], replicated
Inputs may be any that keep to these rules, and one draw needn't show every extreme that they name: `lengths`: valid length of each slot; some slot is full, of length 1024.
All inputs are finite; a program needn't handle non-finite values.
Results may differ from a plain program's by a relative error of at most 0.02.
Values may be sent and summed in bfloat16 or wider, within the bound.
A program may use at most 384 MiB of HBM per device.

v0:
```python
import math

import jax
import jax.numpy as jnp
from jax import lax
from jax.sharding import PartitionSpec as P

HEADS = 16
KV_HEADS = 4
HEAD_DIM = 64


EPSILON = 1e-06


def root_norm(values, norm_gain):
    factor = lax.rsqrt(jnp.mean(values * values, axis=-1, keepdims=True) + EPSILON)
    return values * factor * norm_gain


def rotation_tables(positions):
    half_dim = HEAD_DIM // 2
    frequency = 10000.0 ** (-(2.0 * jnp.arange(half_dim, dtype=jnp.float32)) / HEAD_DIM)
    angles = positions.astype(jnp.float32)[:, None] * frequency[None, :]
    return (jnp.cos(angles), jnp.sin(angles))


def rotate(values, cos_table, sin_table):
    half_dim = values.shape[-1] // 2
    lower_half = values[..., :half_dim]
    upper_half = values[..., half_dim:]
    cos_part = cos_table[:, None, :]
    sin_part = sin_table[:, None, :]
    return jnp.concatenate(
        [
            lower_half * cos_part - upper_half * sin_part,
            upper_half * cos_part + lower_half * sin_part,
        ],
        axis=-1,
    )


def prepare_heads(qkv_out, head_gain, cos_table, sin_table):
    row_count = qkv_out.shape[0]
    query_cols = HEADS * HEAD_DIM
    key_cols = KV_HEADS * HEAD_DIM
    queries = qkv_out[:, :query_cols].reshape(row_count, HEADS, HEAD_DIM)
    key_part = qkv_out[:, query_cols : query_cols + key_cols].reshape(row_count, KV_HEADS, HEAD_DIM)
    value_part = qkv_out[:, query_cols + key_cols :]
    queries = rotate(root_norm(queries, head_gain[0]), cos_table, sin_table).reshape(
        row_count, query_cols
    )
    key_part = rotate(root_norm(key_part, head_gain[1]), cos_table, sin_table).reshape(
        row_count, key_cols
    )
    return (queries, key_part, value_part)


def activate(projected):
    gate_part = projected[:, 0]
    return gate_part * jax.nn.sigmoid(gate_part) * projected[:, 1]


def contract_rows(left, right):
    return lax.dot_general(
        left, right, (((0,), (0,)), ((), ())), preferred_element_type=jnp.float32
    )


def contract_cols(left, right):
    return lax.dot_general(
        left, right, (((1,), (1,)), ((), ())), preferred_element_type=jnp.float32
    )


def on_device(
    inputs,
    cotangent,
    lengths,
    qkv_weight,
    out_weight,
    gate_up,
    down_weight,
    attn_gain,
    ffn_gain,
    qk_gain,
):
    token_count = inputs.shape[1]
    group = HEADS // KV_HEADS
    key_cols = KV_HEADS * HEAD_DIM
    seq_len = token_count * lax.axis_size("ctx")
    positions = lax.axis_index("ctx") * token_count + jnp.arange(token_count, dtype=jnp.int32)
    length = lengths[0]
    row_keep = (positions < length).astype(jnp.float32)[:, None]
    inv_root = 1.0 / math.sqrt(HEAD_DIM)
    source = inputs[0].astype(jnp.float32)
    qkv_full, out_full, attn_full, ffn_full = (
        lax.all_gather(qkv_weight, "fsdp", axis=0, tiled=True),
        lax.all_gather(out_weight, "fsdp", axis=0, tiled=True),
        lax.all_gather(attn_gain, "fsdp", axis=0, tiled=True),
        lax.all_gather(ffn_gain, "fsdp", axis=0, tiled=True),
    )
    attn_norm = attn_full.astype(jnp.float32)
    ffn_norm = ffn_full.astype(jnp.float32)
    normed = root_norm(source, attn_norm).astype(jnp.bfloat16)
    qkv_out = jnp.dot(normed, qkv_full, preferred_element_type=jnp.float32)
    cos_table, sin_table = rotation_tables(positions)
    head_gain = qk_gain.astype(jnp.float32)

    def head_pieces(qkv_values, gain_values):
        return prepare_heads(qkv_values, gain_values, cos_table, sin_table)

    head_values, head_pull = jax.vjp(head_pieces, qkv_out, head_gain)
    queries, key_part, value_part = head_values
    query_low = queries.astype(jnp.bfloat16).reshape(token_count, KV_HEADS, group, HEAD_DIM)
    kv_local = jnp.concatenate([key_part, value_part], axis=1).astype(jnp.bfloat16)
    kv_whole = lax.all_gather(kv_local, "ctx", axis=0, tiled=True)
    block = 512
    block_total = seq_len // block
    kv_blocks = kv_whole.reshape(block_total, block, 2, KV_HEADS, HEAD_DIM)
    starts = jnp.arange(block_total, dtype=jnp.int32) * block

    def block_scores(key_block, block_start):
        scores = (
            jnp.einsum("bhgd,thd->hgbt", query_low, key_block, preferred_element_type=jnp.float32)
            * inv_root
        )
        key_pos = block_start + jnp.arange(key_block.shape[0], dtype=jnp.int32)
        visible = (key_pos[None, :] <= positions[:, None]) & (key_pos[None, :] < length)
        return (scores, visible)

    def max_step(state, item):
        running_max, running_sum = state
        kv_block, block_start = item
        scores, visible = block_scores(kv_block[:, 0], block_start)
        new_max = jnp.maximum(running_max, jnp.max(jnp.where(visible, scores, -1e30), axis=-1))
        expanded = jnp.where(visible, jnp.exp(scores - new_max[..., None]), 0.0)
        running_sum = running_sum * jnp.exp(running_max - new_max) + jnp.sum(expanded, axis=-1)
        return ((new_max, running_sum), None)

    stat_shape = (KV_HEADS, group, token_count)
    start_state = (jnp.full(stat_shape, -1e30, jnp.float32), jnp.zeros(stat_shape, jnp.float32))
    final_state, unused_out = lax.scan(max_step, start_state, (kv_blocks, starts))
    log_total = final_state[0] + jnp.log(final_state[1])

    def block_probs(kv_block, block_start):
        scores, visible = block_scores(kv_block[:, 0], block_start)
        return jnp.where(visible, jnp.exp(scores - log_total[..., None]), 0.0)

    def value_step(totals, item):
        kv_block, block_start = item
        probs_low = block_probs(kv_block, block_start).astype(jnp.bfloat16)
        return (
            totals
            + jnp.einsum(
                "hgbt,thd->bhgd", probs_low, kv_block[:, 1], preferred_element_type=jnp.float32
            ),
            None,
        )

    attended, unused_out = lax.scan(
        value_step,
        jnp.zeros((token_count, KV_HEADS, group, HEAD_DIM), jnp.float32),
        (kv_blocks, starts),
    )
    attended_low = attended.reshape(token_count, HEADS * HEAD_DIM).astype(jnp.bfloat16)
    middle = source + jnp.dot(attended_low, out_full, preferred_element_type=jnp.float32)
    normed_mid = root_norm(middle, ffn_norm).astype(jnp.bfloat16)
    columns = normed_mid
    projected = jnp.einsum(
        "td,dgf->tgf",
        columns,
        lax.all_gather(gate_up, "fsdp", axis=0, tiled=True),
        preferred_element_type=jnp.float32,
    )
    act_value, act_pull = jax.vjp(activate, projected)
    hidden = act_value.astype(jnp.bfloat16)
    columns = hidden
    ffn_out = jnp.dot(
        columns,
        lax.all_gather(down_weight, "fsdp", axis=0, tiled=True),
        preferred_element_type=jnp.float32,
    )
    layer_out = (row_keep * (middle + ffn_out)).astype(jnp.bfloat16)[None]
    d_out = row_keep * cotangent[0].astype(jnp.float32)
    d_out_low = d_out.astype(jnp.bfloat16)
    down_shard = lax.psum_scatter(
        contract_rows(hidden, d_out_low).astype(jnp.bfloat16),
        "fsdp",
        scatter_dimension=0,
        tiled=True,
    )
    d_hidden = contract_cols(d_out_low, lax.all_gather(down_weight, "fsdp", axis=0, tiled=True))
    d_proj_low = act_pull(d_hidden)[0].astype(jnp.bfloat16)
    columns = normed_mid
    gate_up_shard = lax.psum_scatter(
        jnp.einsum("td,tgf->dgf", columns, d_proj_low, preferred_element_type=jnp.float32).astype(
            jnp.bfloat16
        ),
        "fsdp",
        scatter_dimension=0,
        tiled=True,
    )
    d_normed_mid = jnp.einsum(
        "tgf,dgf->td",
        d_proj_low,
        lax.all_gather(gate_up, "fsdp", axis=0, tiled=True),
        preferred_element_type=jnp.float32,
    )
    mid_value, mid_pull = jax.vjp(root_norm, middle, ffn_norm)
    d_mid_norm, ffn_gain_part = mid_pull(d_normed_mid)
    d_middle = d_out + d_mid_norm
    d_branch = d_middle.astype(jnp.bfloat16)
    out_term = contract_rows(attended_low, d_branch)
    d_attended = (
        contract_cols(d_branch, out_full)
        .astype(jnp.bfloat16)
        .reshape(token_count, KV_HEADS, group, HEAD_DIM)
    )
    delta = jnp.transpose(jnp.sum(d_attended.astype(jnp.float32) * attended, axis=-1), (1, 2, 0))

    def block_grads(kv_block, block_start):
        probs = block_probs(kv_block, block_start)
        d_probs = jnp.einsum(
            "bhgd,thd->hgbt", d_attended, kv_block[:, 1], preferred_element_type=jnp.float32
        )
        d_scores = (probs * (d_probs - delta[..., None])).astype(jnp.bfloat16)
        return (probs.astype(jnp.bfloat16), d_scores)

    def query_step(totals, item):
        kv_block, block_start = item
        probs_low, d_scores = block_grads(kv_block, block_start)
        return (
            totals
            + jnp.einsum(
                "hgbt,thd->bhgd", d_scores, kv_block[:, 0], preferred_element_type=jnp.float32
            ),
            None,
        )

    d_query_sum, unused_out = lax.scan(
        query_step,
        jnp.zeros((token_count, KV_HEADS, group, HEAD_DIM), jnp.float32),
        (kv_blocks, starts),
    )
    d_query = (d_query_sum * inv_root).reshape(token_count, HEADS * HEAD_DIM).astype(jnp.bfloat16)
    sub_block = 512
    sub_total = token_count * lax.axis_size("ctx") // sub_block
    pieces = kv_whole.reshape(sub_total, sub_block, 2, KV_HEADS, HEAD_DIM)
    sub_starts = jnp.arange(sub_total, dtype=jnp.int32) * sub_block

    def key_grads(item):
        kv_block, block_start = item
        probs_low, d_scores = block_grads(kv_block, block_start)
        d_keys = (
            jnp.einsum("hgbt,bhgd->thd", d_scores, query_low, preferred_element_type=jnp.float32)
            * inv_root
        )
        d_values = jnp.einsum(
            "hgbt,bhgd->thd", probs_low, d_attended, preferred_element_type=jnp.float32
        )
        return jnp.concatenate(
            [d_keys.reshape(sub_block, key_cols), d_values.reshape(sub_block, key_cols)], axis=1
        )

    kv_grad = lax.psum_scatter(
        lax.map(key_grads, (pieces, sub_starts))
        .reshape(token_count * lax.axis_size("ctx"), 2 * key_cols)
        .astype(jnp.bfloat16),
        "ctx",
        scatter_dimension=0,
        tiled=True,
    ).astype(jnp.float32)
    d_key_low = kv_grad[:, :key_cols].astype(jnp.bfloat16).astype(jnp.float32)
    d_value_low = kv_grad[:, key_cols:].astype(jnp.bfloat16).astype(jnp.float32)
    d_qkv_out, qk_part = head_pull((d_query.astype(jnp.float32), d_key_low, d_value_low))
    d_qkv = d_qkv_out.astype(jnp.bfloat16)
    qkv_term = contract_rows(normed, d_qkv)
    d_normed = contract_cols(d_qkv, qkv_full)
    first_value, first_pull = jax.vjp(root_norm, source, attn_norm)
    d_source_norm, attn_gain_part = first_pull(d_normed)
    input_grad = (d_middle + d_source_norm).astype(jnp.bfloat16)[None]
    qkv_shard, out_shard, attn_shard, ffn_shard = (
        lax.psum_scatter(
            qkv_term.astype(jnp.bfloat16), "fsdp", scatter_dimension=0, tiled=True
        ).astype(jnp.float32),
        lax.psum_scatter(
            out_term.astype(jnp.bfloat16), "fsdp", scatter_dimension=0, tiled=True
        ).astype(jnp.float32),
        lax.psum_scatter(
            attn_gain_part.astype(jnp.bfloat16), "fsdp", scatter_dimension=0, tiled=True
        ).astype(jnp.float32),
        lax.psum_scatter(
            ffn_gain_part.astype(jnp.bfloat16), "fsdp", scatter_dimension=0, tiled=True
        ).astype(jnp.float32),
    )
    summed = (
        lax.psum(qkv_shard.astype(jnp.bfloat16), "ctx").astype(jnp.float32),
        lax.psum(out_shard.astype(jnp.bfloat16), "ctx").astype(jnp.float32),
        lax.psum(gate_up_shard, "ctx").astype(jnp.float32),
        lax.psum(down_shard, "ctx").astype(jnp.float32),
        lax.psum(attn_shard.astype(jnp.bfloat16), "ctx").astype(jnp.float32),
        lax.psum(ffn_shard.astype(jnp.bfloat16), "ctx").astype(jnp.float32),
    )
    qk_total = lax.psum(qk_part, ("fsdp", "ctx"))
    return (
        layer_out,
        input_grad,
        summed[0],
        summed[1],
        summed[2],
        summed[3],
        summed[4],
        summed[5],
        qk_total,
    )


def solution(mesh):
    return jax.shard_map(
        on_device,
        mesh=mesh,
        in_specs=(
            P("fsdp", "ctx", None),
            P("fsdp", "ctx", None),
            P("fsdp"),
            P("fsdp", None),
            P("fsdp", None),
            P("fsdp", None, None),
            P("fsdp", None),
            P("fsdp"),
            P("fsdp"),
            P(),
        ),
        out_specs=(
            P("fsdp", "ctx", None),
            P("fsdp", "ctx", None),
            P("fsdp", None),
            P("fsdp", None),
            P("fsdp", None, None),
            P("fsdp", None),
            P("fsdp"),
            P("fsdp"),
            P(),
        ),
        check_vma=False,
    )
```

profile of v0, /device:TPU:13, one launch (start us, length us, event | category | flops | bytes accessed | tf_op | source)
XLA Modules:
  0.0 2383.8 jit_solution(13541562072520986390)
XLA Ops:
  8.6 14.2 all-gather
  25.8 82.3 %all-gather.8.cloned.1.call-done = bf16[2048,1536]{1,0:T(8,128)(2,1)} async-done(((bf16[256,1536]{1,0:T(8,128)(2,1)}), bf16[2048,1536]{1,0:T(8,128)(2,1)}) %all-gather.8.cloned.1.call-update) | async-done | bytes 6291472 | tf_op jit(solution)/shard_map/all_gather | solution.py:98
  116.7 7.1 copy.65
  124.6 13.9 all-gather.1
  149.8 25.7 %while.47 = (s32[]{:T(128)}, f32[4,4,256]{2,1,0:T(4,128)S(1)}, f32[4,4,256]{2,1,0:T(4,128)S(1)}, s32[2]{0:T(128)S(1)}, s32[]{:T(128)}, /*index=5*/bf16[2,512,2,4...) while((s32[]{:T(128)}, f32[4,4,256]{2,1,0:T(4,128)S(1)}, ...), condition=%wide.region_6.7_spmd.clone, body=%wide.region_3.6_spmd.clone.sunk | while | flops 283399936 | bytes 19225752 | solution.py:143
  170.2 5.2 fusion.175
  175.5 13.6 while.48
  190.3 16.9 all-gather.12.cloned.1.call-done
  212.0 635.0 %all-gather.14.cloned.1.call-done = bf16[2048,2,4096]{2,0,1:T(8,128)(2,1)} async-done(((bf16[256,2,4096]{2,0,1:T(8,128)(2,1)}), bf16[2048,2,4096]{2,0,1:T(8,128)(2,1)}) %all-gather.14.cloned.1.call-update) | async-done | bytes 33554448 | tf_op jit(solution)/shard_map/all_gather | solution.py:173
  847.0 19.7 fusion.110
  866.8 207.4 %all-gather.16.cloned.1.call-done = bf16[4096,2048]{1,0:T(8,128)(2,1)} async-done(((bf16[512,2048]{1,0:T(8,128)(2,1)}), bf16[4096,2048]{1,0:T(8,128)(2,1)}) %all-gather.16.cloned.1.call-update) | async-done | bytes 16777232 | tf_op jit(solution)/shard_map/all_gather | solution.py:181
  1074.2 13.3 multiply_bitcast_fusion
  1087.5 18.9 multiply_reduce_fusion
  1115.6 29.1 %while.46 = (s32[]{:T(128)}, bf16[2,512,512]{2,1,0:T(8,128)(2,1)}, s32[2]{0:T(128)S(1)}, s32[]{:T(128)}, bf16[2,512,2,4,64]{1,4,3,2,0:T(8,128)(2,1)S(1)}, /*inde...) while((s32[]{:T(128)}, bf16[2,512,512]{2,1,0:T(8,128)(2,1)}, ...), condition=%wide.region_13.14_spmd.clone, body=%wide.region_12.13_spmd.clone.sunk | while | flops 1096288000 | bytes 68607184 | solution.py:267
  1122.1 7.1 fusion.172
  1136.4 7.1 fusion.172
  1150.6 30.0 %while.49 = (s32[]{:T(128)}, f32[256,4,4,64]{0,3,2,1:T(8,128)}, bf16[2,512,2,4,64]{1,4,3,2,0:T(8,128)(2,1)S(1)}, s32[2]{0:T(128)S(1)}, s32[]{:T(128)}, /*index=5...) while((s32[]{:T(128)}, f32[256,4,4,64]{0,3,2,1:T(8,128)}, ...), condition=%wide.region_17.18_spmd.clone, body=%wide.region_16.17_spmd.clone.sunk | while | flops 818677504 | bytes 22060200 | solution.py:241
  1158.0 7.6 fusion.184
  1172.8 7.8 fusion.184
  1194.6 12.4 convolution_convert_fusion.1
  1208.6 17.9 convolution_convert_fusion
  1226.6 35.8 %reduce-scatter.10.cloned.1.call-done = bf16[128,2048]{1,0:T(8,128)(2,1)} async-done(((bf16[1024,2048]{1,0:T(8,128)(2,1)}), bf16[128,2048]{1,0:T(8,128)(2,1)}) %reduce-scatter.10.cloned.1.call-update) | async-done | bytes 524304 | tf_op jit(solution)/shard_map/reduce_scatter | solution.py:287
  1262.4 120.4 %reduce-scatter.8.cloned.1.call-done = bf16[256,1536]{1,0:T(8,128)(2,1)} async-done(((bf16[2048,1536]{1,0:T(8,128)(2,1)}), bf16[256,1536]{1,0:T(8,128)(2,1)}) %reduce-scatter.8.cloned.1.call-update) | async-done | bytes 786448 | tf_op jit(solution)/shard_map/reduce_scatter | solution.py:284
  1382.7 284.8 %reduce-scatter.14.cloned.1.call-done = bf16[512,2048]{1,0:T(8,128)(2,1)} async-done(((bf16[4096,2048]{1,0:T(8,128)(2,1)}), bf16[512,2048]{1,0:T(8,128)(2,1)}) %reduce-scatter.14.cloned.1.call-update) | async-done | bytes 2097168 | tf_op jit(solution)/shard_map/reduce_scatter | solution.py:187
  1667.6 545.8 %reduce-scatter.12.cloned.1.call-done = bf16[256,2,4096]{2,0,1:T(8,128)(2,1)} async-done(((bf16[2048,2,4096]{2,0,1:T(8,128)(2,1)}), bf16[256,2,4096]{2,0,1:T(8,128)(2,1)}) %reduce-scatter.12.cloned.1.call-update) | async-done | bytes 4194320 | tf_op jit(solution)/shard_map/reduce_scatter | solution.py:196
  2214.7 13.9 fusion.83
  2228.6 7.0 fusion.85
  2235.6 16.5 all-reduce.13
  2252.2 9.2 all-reduce.14
  2263.2 43.1 %psum.55 = f32[2,64]{1,0:T(2,128)} all-reduce(f32[2,64]{1,0:T(2,128)S(1)} %pad_add_fusion.2), channel_id=1, replica_groups=mesh['fsdp'=8,'ctx'=4] {'fsdp','ctx'}, use_global_device_ids=true, to_apply=%region_36.37 | all-reduce | flops 128 | bytes 1024 | tf_op jit(solution)/shard_map/psum | solution.py:305
  2310.1 49.7 %all-reduce.18.cloned.1.call-done = (bf16[256,2,4096]{2,0,1:T(8,128)(2,1)}, bf16[256,1536]{1,0:T(8,128)(2,1)}, bf16[128,2048]{1,0:T(8,128)(2,1)}, bf16[512,2048]{1,0:T(8,128)(2,1)}) async-done(((bf16[256,2,4096]{2,0,1:T(8,128)(2,1)}, bf16[256,1536]{1,0:T(8,128)(2,1)}, bf16[128,2048]{1,0:T(8,128)(2,1)}, bf16[512,2048]{1,0:T(8,128)(2,1)}), (bf16[256,2,4096]{2,0,1:T(8,128)(2,1)}, bf16[256,1536]{1,0:T(8,128)(2,1)}, ...) | async-done | bytes 7602192 | tf_op jit(solution)/shard_map/psum | solution.py:300
  2364.4 10.1 copy.74
  (273 shorter events, 136.6 us)
Async XLA Ops:
  7.2 100.9 %all-gather.8.cloned.1.call-start = ((), (), s32[]{:S(2)}) async-start(), calls=%async_computation.5 | async-start | bytes 7077888 | tf_op jit(solution)/shard_map/all_gather | solution.py:98
  7.9 134.2 %all-gather.10.cloned.1.call-start = ((), (), s32[]{:S(2)}) async-start(), calls=%async_computation.6 | async-start | bytes 1310720 | tf_op jit(solution)/shard_map/all_gather | solution.py:117
  22.8 90.2 %copy-start.27 = (f32[8,1,256]{2,1,0:T(1,128)}, f32[8,1,256]{2,1,0:T(1,128)S(1)}, u32[]{:S(2)}) copy-start(f32[8,1,256]{2,1,0:T(1,128)S(1)} %convert_element_type.220) | copy-start | bytes 24580
  25.6 87.5 %copy-start.36 = (f32[256]{0:T(256)}, f32[256]{0:T(256)S(1)}, u32[]{:S(2)}) copy-start(f32[256]{0:T(256)S(1)} %fusion.115) | copy-start | bytes 3076
  25.6 88.9 %copy-start.41 = (f32[64]{0:T(128)}, f32[64]{0:T(128)S(1)}, u32[]{:S(2)}) copy-start(f32[64]{0:T(128)S(1)} %get-tuple-element.562) | copy-start | bytes 772
  25.6 115.3 %copy-start.43 = (f32[64]{0:T(128)}, f32[64]{0:T(128)S(1)}, u32[]{:S(2)}) copy-start(f32[64]{0:T(128)S(1)} %get-tuple-element.561) | copy-start | bytes 772
  25.8 116.1 %copy-start.21 = (f32[256,32]{0,1:T(8,128)}, f32[256,32]{0,1:T(8,128)S(1)}, u32[]{:S(2)}) copy-start(f32[256,32]{0,1:T(8,128)S(1)} %get-tuple-element.559) | copy-start | bytes 98308
  25.8 116.1 %copy-start.23 = (f32[256,32]{0,1:T(8,128)}, f32[256,32]{0,1:T(8,128)S(1)}, u32[]{:S(2)}) copy-start(f32[256,32]{0,1:T(8,128)S(1)} %get-tuple-element.560) | copy-start | bytes 98308
  114.4 9.5 copy-start.10
  115.9 91.2 %all-gather.12.cloned.1.call-start = ((), (), s32[]{:S(2)}) async-start(), calls=%async_computation.7 | async-start | bytes 4718592 | tf_op jit(solution)/shard_map/all_gather | solution.py:99
  116.7 730.4 %all-gather.14.cloned.1.call-start = ((), (), s32[]{:S(2)}) async-start(), calls=%async_computation.8 | async-start | bytes 37748736 | tf_op jit(solution)/shard_map/all_gather | solution.py:173
  123.9 950.3 %all-gather.16.cloned.1.call-start = ((), (), s32[]{:S(2)}) async-start(), calls=%async_computation.9 | async-start | bytes 18874368 | tf_op jit(solution)/shard_map/all_gather | solution.py:181
  124.5 1061.8 %reduce-scatter.6.cloned.1.call-start = ((), (), s32[]{:S(2)}) async-start(), calls=%async_computation.10 | async-start | bytes 1310720 | tf_op jit(solution)/shard_map/reduce_scatter | solution.py:266
  139.1 967.2 %copy-start.45 = (f32[256]{0:T(256)}, f32[256]{0:T(256)S(1)}, u32[]{:S(2)}) copy-start(f32[256]{0:T(256)S(1)} %compare_convert_fusion) | copy-start | bytes 3076
  175.4 31.7 %copy-start.5 = (bf16[1,256,2048]{2,1,0:T(8,128)(2,1)S(1)}, bf16[1,256,2048]{2,1,0:T(8,128)(2,1)}, u32[]{:S(2)}) copy-start(bf16[1,256,2048]{2,1,0:T(8,128)(2,1)} %param.18) | copy-start | bytes 3145732
  212.0 894.3 %copy-start.31 = (f32[256]{0:T(256)}, f32[256]{0:T(256)S(1)}, u32[]{:S(2)}) copy-start(f32[256]{0:T(256)S(1)} %fusion.116) | copy-start | bytes 3076
  847.0 227.2 %copy-start.19 = (bf16[1,256,2048]{2,1,0:T(8,128)(2,1)S(1)}, bf16[1,256,2048]{2,1,0:T(8,128)(2,1)}, u32[]{:S(2)}) copy-start(bf16[1,256,2048]{2,1,0:T(8,128)(2,1)} %param.19) | copy-start | bytes 3145732
  1087.5 18.9 copy-start.1
  1144.7 117.7 %reduce-scatter.10.cloned.1.call-start = ((), (), s32[]{:S(2)}) async-start(), calls=%async_computation.12 | async-start | bytes 4718592 | tf_op jit(solution)/shard_map/reduce_scatter | solution.py:287
  1149.6 233.2 %reduce-scatter.8.cloned.1.call-start = ((), (), s32[]{:S(2)}) async-start(), calls=%async_computation.11 | async-start | bytes 7077888 | tf_op jit(solution)/shard_map/reduce_scatter | solution.py:284
  1150.6 31.6 %copy-start.22 = (f32[256,32]{0,1:T(8,128)S(1)}, f32[256,32]{0,1:T(8,128)}, u32[]{:S(2)}) copy-start(f32[256,32]{0,1:T(8,128)} %copy-done.21) | copy-start | bytes 98308
  1150.6 31.7 %copy-start.24 = (f32[256,32]{0,1:T(8,128)S(1)}, f32[256,32]{0,1:T(8,128)}, u32[]{:S(2)}) copy-start(f32[256,32]{0,1:T(8,128)} %copy-done.23) | copy-start | bytes 98308
  1193.4 474.2 %reduce-scatter.14.cloned.1.call-start = ((), (), s32[]{:S(2)}) async-start(), calls=%async_computation.14 | async-start | bytes 18874368 | tf_op jit(solution)/shard_map/reduce_scatter | solution.py:187
  1207.0 1006.3 %reduce-scatter.12.cloned.1.call-start = ((), (), s32[]{:S(2)}) async-start(), calls=%async_computation.13 | async-start | bytes 37748736 | tf_op jit(solution)/shard_map/reduce_scatter | solution.py:196
  1226.5 986.9 %copy-start.49 = (u32[32]{0:T(128)S(1)}, u32[32]{0:T(128)}, u32[]{:S(2)}) copy-start(u32[32]{0:T(128)} %constant.125) | copy-start | bytes 388
  1226.5 988.1 %copy-start.47 = (f32[256]{0:T(256)S(1)}, f32[256]{0:T(256)}, u32[]{:S(2)}) copy-start(f32[256]{0:T(256)} %copy-done.45) | copy-start | bytes 3076
  1226.5 1133.3 %all-reduce.18.cloned.1.call-start = ((), (), s32[]{:S(2)}) async-start(), calls=%async_computation.15 | async-start | bytes 15204352 | tf_op jit(solution)/shard_map/psum | solution.py:300
  2214.6 13.9 copy-start.14
  2214.7 13.9 copy-start.38
  2228.6 77.6 %copy-start.40 = (f32[256]{0:T(256)S(1)}, f32[256]{0:T(256)}, u32[]{:S(2)}) copy-start(f32[256]{0:T(256)} %copy-done.39) | copy-start | bytes 3076
  2228.6 78.3 %copy-start.8 = (f32[256,2048]{1,0:T(8,128)S(1)}, f32[256,2048]{1,0:T(8,128)}, u32[]{:S(2)}) copy-start(f32[256,2048]{1,0:T(8,128)} %copy-done.7) | copy-start | bytes 6291460
  2364.4 10.1 copy-start.15
  (31 other events, 88.0 us)
Sparse Core Ops, SparseCore 0:
  10.2 97.8 all-gather.7
  116.1 16.6 all-gather.9
  134.9 72.2 all-gather.11
  209.1 637.8 all-gather.13
  849.0 225.1 all-gather.15
  1144.8 24.4 reduce-scatter.5
  1173.3 89.0 reduce-scatter.9
  1265.9 116.7 reduce-scatter.7
  1386.5 280.9 reduce-scatter.13
  1671.7 541.6 reduce-scatter.11
  2216.1 143.6 all-reduce.17
where the time goes:
time: 2390 us; the launch traced here: 2380 us
  waiting for transfers between devices  1980 us (83%)
  matrix products  187 us (8%)
  blocking collectives  96.8 us (4%)
  other arithmetic  55.2 us (2%)
  local copies, waits for them, and re-layouts  47.4 us (2%)
    all_gather x1, waiting for transfers between devices, on_device(): lax.all_gather(gate_up, 'fsdp', axis=0, tiled=True)  635 us
    reduce_scatter x1, waiting for transfers between devices, on_device(): lax.psum_scatter(jnp.einsum('td,tgf->dgf', columns, d_proj_low, preferred...  546 us
    reduce_scatter x1, waiting for transfers between devices, on_device(): lax.psum_scatter(contract_rows(hidden, d_out_low).astype(jnp.bfloat16), '...  285 us
    all_gather x1, waiting for transfers between devices, on_device(): lax.all_gather(down_weight, 'fsdp', axis=0, tiled=True)  207 us
    reduce_scatter x1, waiting for transfers between devices, on_device(): lax.psum_scatter(qkv_term.astype(jnp.bfloat16), 'fsdp', scatter_dimension...  120 us
    all_gather x1, waiting for transfers between devices, on_device(): lax.all_gather(qkv_weight, 'fsdp', axis=0, tiled=True)  82.3 us
    psum x1, waiting for transfers between devices, on_device(): lax.psum(gate_up_shard, 'ctx').astype(jnp.float32)  49.7 us
  transfers between devices with their start and end apart: 11, of which 9 were waited for; matrix products, arithmetic and copies ran while one was open for 8% of the time, Pallas kernels for 0%

commit v1 on v0

--- a/solution.py
+++ b/solution.py
@@ -1,8 +1,12 @@
+import functools
 import math
 
 import jax
 import jax.numpy as jnp
+import numpy as np
 from jax import lax
+from jax.experimental import pallas as pl
+from jax.experimental.pallas import tpu as pltpu
 from jax.sharding import PartitionSpec as P
 
 HEADS = 16
@@ -316,9 +320,1052 @@
     )
 
 
+MESH = pl.DeviceIdType.MESH
+F32 = jnp.float32
+BF16 = jnp.bfloat16
+VMEM_BYTES = 56 << 20
+HBM = pl.BlockSpec(memory_space=pl.ANY)
+VMEM = pl.BlockSpec(memory_space=pltpu.VMEM)
+
+
+class Place:
+    def __init__(self):
+        self.f = lax.axis_index("fsdp")
+        self.c = lax.axis_index("ctx")
+        self.z, self.x = lax.div(self.f, 2), lax.rem(self.f, 2)
+        self.y, self.core = lax.div(self.c, 2), lax.rem(self.c, 2)
+        self.xo, self.yo, self.co = 1 - self.x, 1 - self.y, 1 - self.core
+        upper = lax.div(self.z, 2)
+        self.others = (self.z + 1 - 2 * lax.rem(self.z, 2), 2 - upper, 3 - 3 * upper)
+        self.x_dev = (self.z * 2 + self.xo, self.c)
+        self.c_core = self.y * 2 + self.co
+        self.c_y = self.yo * 2 + self.core
+        self.c_diag = self.yo * 2 + self.co
+        self.core_dev = (self.f, self.c_core)
+        self.y_dev = (self.f, self.c_y)
+        self.diag_dev = (self.f, self.c_diag)
+
+    def z_dev(self, z):
+        return (z * 2 + self.x, self.c)
+
+    def meet(self, partners):
+        barrier = pltpu.get_barrier_semaphore()
+        for partner in partners:
+            pl.semaphore_signal(barrier, inc=1, device_id=partner, device_id_type=MESH)
+        pl.semaphore_wait(barrier, len(partners))
+
+    def neighbours(self):
+        return [self.z_dev(o) for o in self.others] + [self.x_dev, self.core_dev, self.y_dev]
+
+
+class Links:
+    def __init__(self, place, send_sems, recv_sems, local_sems):
+        self.place = place
+        self.send_sems, self.recv_sems, self.local_sems = send_sems, recv_sems, local_sems
+        self.sends = self.recvs = self.locals = 0
+        self.open = []
+
+    def slots(self, count):
+        first = self.recvs
+        self.recvs += count
+        return first
+
+    def copy(self, src, dst, slot, device):
+        made = pltpu.make_async_remote_copy(
+            src_ref=src,
+            dst_ref=dst,
+            send_sem=self.send_sems.at[self.sends],
+            recv_sem=self.recv_sems.at[slot],
+            device_id=device,
+            device_id_type=MESH,
+        )
+        self.sends += 1
+        return made
+
+    def send(self, src, dst, slot, device):
+        made = self.copy(src, dst, slot, device)
+        made.start()
+        self.open.append(made)
+
+    def arrive(self, ref, slot):
+        pltpu.make_async_remote_copy(
+            src_ref=ref,
+            dst_ref=ref,
+            send_sem=self.send_sems.at[0],
+            recv_sem=self.recv_sems.at[slot],
+            device_id=self.place.x_dev,
+            device_id_type=MESH,
+        ).wait_recv()
+
+    def local(self, src, dst):
+        made = pltpu.make_async_copy(src, dst, self.local_sems.at[self.locals])
+        self.locals += 1
+        made.start()
+        return made
+
+    def finish(self):
+        for made in self.open:
+            made.wait_send()
+        self.open = []
+
+
+def spread_plane(links, place, chunks, ahead=2):
+    z_slot, x_slot = links.slots(4 * len(chunks)), links.slots(4 * len(chunks))
+
+    def begin(k):
+        src, dst = chunks[k]
+        for other in place.others:
+            links.send(src, dst(place.f), z_slot + 4 * k + place.z, place.z_dev(other))
+        links.send(src, dst(place.f), x_slot + 4 * k + place.z, place.x_dev)
+
+    for k in range(min(ahead, len(chunks))):
+        begin(k)
+    yield
+    for k in range(len(chunks)):
+        dst = chunks[k][1]
+        for other in place.others:
+            block = dst(other * 2 + place.x)
+            links.arrive(block, z_slot + 4 * k + other)
+            links.send(block, block, x_slot + 4 * k + other, place.x_dev)
+        if k + ahead < len(chunks):
+            begin(k + ahead)
+        yield
+    for k in range(len(chunks)):
+        for z in range(4):
+            links.arrive(chunks[k][1](z * 2 + place.xo), x_slot + 4 * k + z)
+    yield
+
+
+def reduce_plane(links, place, chunks, own, from_x, to_z, from_z, total, done, ahead=2):
+    count = len(chunks)
+    x_slot, z_slot = links.slots(count), links.slots(4 * count)
+    loads = {}
+
+    def begin(k):
+        links.send(chunks[k](place.xo), from_x.at[k], x_slot + k, place.x_dev)
+        loads[k] = links.local(chunks[k](place.x), own.at[k])
+
+    def middle(k):
+        links.arrive(from_x.at[k], x_slot + k)
+        loads[k].wait()
+        for other in place.others:
+            pair = own[k, other].astype(F32) + from_x[k, other].astype(F32)
+            to_z[k, other] = pair.astype(BF16)
+            links.send(
+                to_z.at[k, other],
+                from_z.at[k, place.z],
+                z_slot + 4 * k + place.z,
+                place.z_dev(other),
+            )
+
+    def end(k):
+        sums = own[k, place.z].astype(F32) + from_x[k, place.z].astype(F32)
+        for other in place.others:
+            links.arrive(from_z.at[k, other], z_slot + 4 * k + other)
+            sums += from_z[k, other].astype(F32)
+        total[k] = sums.astype(BF16)
+        done(k)
+
+    for k in range(min(ahead, count)):
+        begin(k)
+    yield
+    for k in range(count + 1):
+        if k < count:
+            middle(k)
+            if k + ahead < count:
+                begin(k + ahead)
+            yield
+        if k >= 1:
+            end(k - 1)
+            yield
+
+
+class SpreadCtx:
+    def __init__(self, links, place, out, parts):
+        self.links, self.place, self.out, self.parts = links, place, out, parts
+        self.slot = links.slots(3 * len(parts))
+
+    def begin(self, k, src, y_too=True):
+        place, rows = self.place, self.parts[k]
+        self.links.send(src, self.out.at[place.c, rows], self.slot + 3 * k, place.core_dev)
+        if y_too:
+            self.begin_y(k, src)
+
+    def begin_y(self, k, src):
+        place, rows = self.place, self.parts[k]
+        self.links.send(src, self.out.at[place.c, rows], self.slot + 3 * k + 1, place.y_dev)
+
+    def forward(self, k):
+        place = self.place
+        block = self.out.at[place.c_y, self.parts[k]]
+        self.links.arrive(block, self.slot + 3 * k + 1)
+        self.links.send(block, block, self.slot + 3 * k + 2, place.core_dev)
+
+    def end(self):
+        place = self.place
+        for k, rows in enumerate(self.parts):
+            self.links.arrive(self.out.at[place.c_core, rows], self.slot + 3 * k)
+            self.links.arrive(self.out.at[place.c_diag, rows], self.slot + 3 * k + 2)
+
+
+class ReduceCtx:
+    def __init__(self, links, place, part, parts, own, from_core, to_y, from_y):
+        self.links, self.place, self.part, self.parts = links, place, part, parts
+        self.own, self.from_core, self.to_y, self.from_y = own, from_core, to_y, from_y
+        self.slot = links.slots(3 * len(parts))
+        self.loads = {}
+
+    def begin(self):
+        place = self.place
+        for side, y in ((0, place.yo), (1, place.y)):
+            for k, rows in enumerate(self.parts):
+                self.links.send(
+                    self.part.at[y * 2 + place.co, rows],
+                    self.from_core.at[side, rows],
+                    self.slot + 3 * k + side,
+                    place.core_dev,
+                )
+                self.loads[side, k] = self.links.local(
+                    self.part.at[y * 2 + place.core, rows], self.own.at[side, rows]
+                )
+
+    def pair(self, side, k):
+        rows = self.parts[k]
+        self.links.arrive(self.from_core.at[side, rows], self.slot + 3 * k + side)
+        self.loads[side, k].wait()
+        return self.own[side, rows].astype(F32) + self.from_core[side, rows].astype(F32)
+
+    def cross(self, k):
+        rows = self.parts[k]
+        self.to_y[rows] = self.pair(0, k).astype(BF16)
+        self.links.send(
+            self.to_y.at[rows], self.from_y.at[rows], self.slot + 3 * k + 2, self.place.y_dev
+        )
+
+    def total(self, k):
+        rows = self.parts[k]
+        sums = self.pair(1, k)
+        self.links.arrive(self.from_y.at[rows], self.slot + 3 * k + 2)
+        return sums + self.from_y[rows].astype(F32)
+
+
+def halves(rows):
+    return [pl.ds(0, rows // 2), pl.ds(rows // 2, rows // 2)]
+
+
+def row_factor(values):
+    return lax.rsqrt(jnp.mean(values * values, axis=-1, keepdims=True) + EPSILON)
+
+
+def gather_kernel(
+    qkv_s, out_s, gain_s, x_s, qkv_w, out_w, gains, x_all, send_sems, recv_sems, local_sems
+):
+    place = Place()
+    links = Links(place, send_sems, recv_sems, local_sems)
+    fellows = [lax.rem(place.f + d, 8) for d in range(1, 8)]
+    place.meet([(f, place.c) for f in fellows] + [place.core_dev, place.y_dev])
+    plane = spread_plane(links, place, [(qkv_s, lambda f: qkv_w.at[f])])
+    next(plane)
+    kept = [
+        links.local(qkv_s, qkv_w.at[place.f]),
+        links.local(gain_s, gains.at[place.f]),
+        links.local(x_s, x_all.at[place.c]),
+    ]
+    parts = halves(x_s.shape[0])
+    spread = SpreadCtx(links, place, x_all, parts)
+    for k, rows in enumerate(parts):
+        spread.begin(k, x_s.at[rows])
+    gain_slot = links.slots(8)
+    for f in fellows:
+        links.send(gain_s, gains.at[place.f], gain_slot + place.f, (f, place.c))
+
+    root_slot, side_slot = links.slots(1), links.slots(1)
+    holds = place.z == place.c
+    down = [
+        links.copy(out_s, out_w.at[place.x], root_slot, place.z_dev(other))
+        for other in place.others
+    ]
+    side = links.copy(out_s, out_w.at[place.x], side_slot, place.x_dev)
+    onward = links.copy(out_w.at[place.x], out_w.at[place.x], side_slot, place.x_dev)
+    own = pltpu.make_async_copy(out_s, out_w.at[place.x], local_sems.at[links.locals])
+    links.locals += 1
+
+    @pl.when(holds)
+    def _():
+        for made in down:
+            made.start()
+        side.start()
+        own.start()
+
+    next(plane)
+    for k in range(len(parts)):
+        spread.forward(k)
+
+    @pl.when(jnp.logical_not(holds))
+    def _():
+        links.arrive(out_w.at[place.x], root_slot)
+        onward.start()
+
+    for f in fellows:
+        links.arrive(gains.at[f], gain_slot + f)
+    next(plane)
+    spread.end()
+    links.arrive(out_w.at[place.xo], side_slot)
+    for made in kept:
+        made.wait()
+    links.finish()
+
+    @pl.when(holds)
+    def _():
+        own.wait()
+        for made in down:
+            made.wait_send()
+        side.wait_send()
+
+    @pl.when(jnp.logical_not(holds))
+    def _():
+        onward.wait_send()
+
+
+def feed_gather_kernel(
+    gu_s, dn_s, dout_s, part, x_s, gain, gu_w, dn_w, dout_all, middle, mid_all,
+    own, from_core, to_y, from_y, mid_low, send_sems, recv_sems, local_sems,
+):
+    place = Place()
+    links = Links(place, send_sems, recv_sems, local_sems)
+    place.meet(place.neighbours())
+    step = 64
+    chunks = []
+    for src, dst in ((gu_s, gu_w), (dn_s, dn_w)):
+        for first in range(0, src.shape[0], step):
+            rows = pl.ds(first, step)
+            chunks.append((src.at[rows], lambda f, dst=dst, rows=rows: dst.at[f, rows]))
+    plane = spread_plane(links, place, chunks)
+    next(plane)
+    parts = halves(x_s.shape[0])
+    reduce = ReduceCtx(links, place, part, parts, own, from_core, to_y, from_y)
+    reduce.begin()
+    kept = [
+        links.local(gu_s, gu_w.at[place.f]),
+        links.local(dn_s, dn_w.at[place.f]),
+        links.local(dout_s, dout_all.at[place.c]),
+    ]
+    for k in range(2):
+        reduce.cross(k)
+    dout = SpreadCtx(links, place, dout_all, parts)
+    for k, rows in enumerate(parts):
+        dout.begin(k, dout_s.at[rows], y_too=False)
+    next(plane)
+    mid = SpreadCtx(links, place, mid_all, parts)
+    for k, rows in enumerate(parts):
+        value = x_s[rows].astype(F32) + reduce.total(k)
+        middle[rows] = value
+        mid_low[rows] = (value * row_factor(value) * gain[...]).astype(BF16)
+        mid.begin(k, mid_low.at[rows])
+        kept.append(links.local(mid_low.at[rows], mid_all.at[place.c, rows]))
+    next(plane)
+    for k in range(2):
+        mid.forward(k)
+    for k, rows in enumerate(parts):
+        dout.begin_y(k, dout_s.at[rows])
+    next(plane)
+    next(plane)
+    for k in range(2):
+        dout.forward(k)
+    for _ in plane:
+        pass
+    mid.end()
+    dout.end()
+    for made in kept:
+        made.wait()
+    links.finish()
+
+
+def feed_reduce_kernel(
+    gu_g, dn_g, ffn_part, dmid_part, middle, dout_s, keep, gain,
+    gu_all, dn_all, layer_out, d_middle, gain_part, branch_all,
+    own, from_x, to_z, from_z, total,
+    own1, from_core1, to_y1, from_y1, own2, from_core2, to_y2, from_y2, branch,
+    send_sems, recv_sems, local_sems,
+):
+    place = Place()
+    links = Links(place, send_sems, recv_sems, local_sems)
+    place.meet(place.neighbours())
+    step = from_x.shape[2]
+    chunks, where = [], []
+    for grad, out in ((dn_g, dn_all), (gu_g, gu_all)):
+        for first in range(0, grad.shape[2], step):
+            rows = pl.ds(first, step)
+            chunks.append(lambda x, grad=grad, rows=rows: grad.at[:, x, rows])
+            where.append((out, rows))
+    outs = [SpreadCtx(links, place, out, [rows]) for out, rows in where]
+    kept = []
+
+    def done(k):
+        out, rows = where[k]
+        outs[k].begin(0, total.at[k])
+        kept.append(links.local(total.at[k], out.at[place.c, rows]))
+
+    plane = reduce_plane(links, place, chunks, own, from_x, to_z, from_z, total, done)
+    next(plane)
+    parts = halves(middle.shape[0])
+    dmid = ReduceCtx(links, place, dmid_part, parts, own1, from_core1, to_y1, from_y1)
+    dmid.begin()
+    for k in range(2):
+        dmid.cross(k)
+    next(plane)
+    spread = SpreadCtx(links, place, branch_all, parts)
+    gain_sum = None
+    for k, rows in enumerate(parts):
+        d_norm = dmid.total(k)
+        value = middle[rows]
+        factor = row_factor(value)
+        term = jnp.sum(d_norm * value * factor, axis=0, keepdims=True)
+        gain_sum = term if gain_sum is None else gain_sum + term
+        scaled = d_norm * gain[...]
+        inner = jnp.mean(scaled * value, axis=-1, keepdims=True)
+        grad = dout_s[rows].astype(F32) + factor * scaled - value * (factor * factor * factor * inner)
+        d_middle[rows] = grad
+        branch[rows] = grad.astype(BF16)
+        spread.begin(k, branch.at[rows])
+        kept.append(links.local(branch.at[rows], branch_all.at[place.c, rows]))
+    gain_part[...] = gain_sum
+    next(plane)
+    ffn = ReduceCtx(links, place, ffn_part, parts, own2, from_core2, to_y2, from_y2)
+    ffn.begin()
+    for k in range(2):
+        spread.forward(k)
+    for k in range(2):
+        ffn.cross(k)
+    next(plane)
+    next(plane)
+    for k, rows in enumerate(parts):
+        layer_out[rows] = (keep[rows] * (middle[rows] + ffn.total(k))).astype(BF16)
+    forwarded = 0
+    for step_at, _ in enumerate(plane):
+        if step_at % 2 == 1:
+            outs[forwarded].forward(0)
+            forwarded += 1
+    for k in range(forwarded, len(outs)):
+        outs[k].forward(0)
+    spread.end()
+    for out in outs:
+        out.end()
+    for made in kept:
+        made.wait()
+    links.finish()
+
+
+def last_kernel(
+    qkv_g, out_g, dnorm_part, x_s, d_middle, gain, ffn_part, qk_part,
+    qkv_all, out_all, input_grad, stats,
+    own, from_x, to_z, from_z, total,
+    own1, from_core1, to_y1, from_y1,
+    out_own, out_x, out_low, out_z,
+    mine, plane_stats, ctx_stats, send_sems, recv_sems, local_sems,
+):
+    place = Place()
+    links = Links(place, send_sems, recv_sems, local_sems)
+    fellows = [lax.rem(place.f + d, 8) for d in range(1, 8)]
+    place.meet(
+        [(f, place.c) for f in fellows] + [place.core_dev, place.y_dev, place.diag_dev]
+    )
+    step = from_x.shape[2]
+    chunks = []
+    for first in range(0, qkv_g.shape[2], step):
+        rows = pl.ds(first, step)
+        chunks.append(lambda x, rows=rows: qkv_g.at[:, x, rows])
+    outs = [
+        SpreadCtx(links, place, qkv_all, [pl.ds(k * step, step)]) for k in range(len(chunks))
+    ]
+    kept = []
+
+    def done(k):
+        outs[k].begin(0, total.at[k])
+        kept.append(links.local(total.at[k], qkv_all.at[place.c, pl.ds(k * step, step)]))
+
+    out_slot = links.slots(1)
+    links.send(out_g.at[place.xo], out_x, out_slot, place.x_dev)
+    out_load = links.local(out_g.at[place.x], out_own)
+    plane = reduce_plane(links, place, chunks, own, from_x, to_z, from_z, total, done)
+    next(plane)
+    parts = halves(x_s.shape[0])
+    dnorm = ReduceCtx(links, place, dnorm_part, parts, own1, from_core1, to_y1, from_y1)
+    dnorm.begin()
+    for k in range(2):
+        dnorm.cross(k)
+
+    links.arrive(out_x, out_slot)
+    out_load.wait()
+    root_slot, final_slot = links.slots(4), links.slots(1)
+    holds = place.z == place.c
+    pair = out_own[...].astype(F32) + out_x[...].astype(F32)
+    out_low[...] = pair.astype(BF16)
+    to_root = links.copy(
+        out_low, out_z.at[place.z], root_slot + place.z, (place.c * 2 + place.x, place.c)
+    )
+
+    @pl.when(jnp.logical_not(holds))
+    def _():
+        to_root.start()
+
+    next(plane)
+    gain_sum = None
+    for k, rows in enumerate(parts):
+        d_norm = dnorm.total(k)
+        value = x_s[rows].astype(F32)
+        factor = row_factor(value)
+        term = jnp.sum(d_norm * value * factor, axis=0, keepdims=True)
+        gain_sum = term if gain_sum is None else gain_sum + term
+        scaled = d_norm * gain[...]
+        inner = jnp.mean(scaled * value, axis=-1, keepdims=True)
+        grad = d_middle[rows] + factor * scaled - value * (factor * factor * factor * inner)
+        input_grad[rows] = grad.astype(BF16)
+    mine[0:1] = gain_sum
+    mine[1:2] = ffn_part[...]
+    mine[2:3] = qk_part[...]
+    mine[3:8] = jnp.zeros((5, mine.shape[1]), F32)
+    plane_slot, ctx_slot = links.slots(8), links.slots(4)
+    for f in fellows:
+        links.send(mine, plane_stats.at[place.f], plane_slot + place.f, (f, place.c))
+    plane_stats[place.f] = mine[...]
+
+    final = [
+        links.copy(out_all, out_all, final_slot, device)
+        for device in (place.core_dev, place.y_dev)
+    ]
+    onward = links.copy(out_all, out_all, final_slot, place.core_dev)
+
+    @pl.when(holds)
+    def _():
+        sums = out_own[...].astype(F32) + out_x[...].astype(F32)
+        for other in place.others:
+            links.arrive(out_z.at[other], root_slot + other)
+            sums += out_z[other].astype(F32)
+        out_all[...] = sums.astype(BF16)
+        for made in final:
+            made.start()
+
+    for f in fellows:
+        links.arrive(plane_stats.at[f], plane_slot + f)
+    sums = plane_stats[0]
+    for f in range(1, 8):
+        sums += plane_stats[f]
+    ctx_stats[place.c] = sums
+    for device in (place.core_dev, place.y_dev, place.diag_dev):
+        links.send(ctx_stats.at[place.c], ctx_stats.at[place.c], ctx_slot + place.c, device)
+    for _ in plane:
+        pass
+    for out in outs:
+        out.forward(0)
+    relays = place.c_y == place.z
+
+    @pl.when(jnp.logical_not(holds))
+    def _():
+        links.arrive(out_all, final_slot)
+
+    @pl.when(relays)
+    def _():
+        onward.start()
+
+    for c in (place.c_core, place.c_y, place.c_diag):
+        links.arrive(ctx_stats.at[c], ctx_slot + c)
+    stats[...] = ((ctx_stats[0] + ctx_stats[1]) + ctx_stats[2]) + ctx_stats[3]
+    for out in outs:
+        out.end()
+    for made in kept:
+        made.wait()
+    links.finish()
+
+    @pl.when(jnp.logical_not(holds))
+    def _():
+        to_root.wait_send()
+
+    @pl.when(relays)
+    def _():
+        onward.wait_send()
+
+    @pl.when(holds)
+    def _():
+        for made in final:
+            made.wait_send()
+
+
+def low_half(shape):
+    return lax.rem(lax.broadcasted_iota(jnp.int32, shape, len(shape) - 1), 128) < 64
+
+
+def partner(values):
+    lane = lax.broadcasted_iota(jnp.int32, values.shape, len(values.shape) - 1)
+    first = lax.rem(lane, 64) < 32
+    return jnp.where(first, pltpu.roll(values, 96, 1), pltpu.roll(values, 32, 1))
+
+
+def half_sums(values):
+    low = low_half(values.shape)
+    first = jnp.sum(jnp.where(low, values, 0.0), axis=-1, keepdims=True)
+    second = jnp.sum(jnp.where(low, 0.0, values), axis=-1, keepdims=True)
+    return jnp.where(low, first, second)
+
+
+def row_loop(count, body):
+    def step(index, carry):
+        body(index)
+        return carry
+
+    lax.fori_loop(0, count, step, 0)
+
+
+BLOCK = 256
+
+
+def attention_scores(query, keys, key_bias, first, span):
+    scores = lax.dot_general(
+        query, keys, (((1,), (1,)), ((), ())), preferred_element_type=F32
+    ) * (1.0 / math.sqrt(HEAD_DIM))
+    rows = first + lax.broadcasted_iota(jnp.int32, scores.shape, 0)
+    columns = lax.broadcasted_iota(jnp.int32, scores.shape, 1)
+    return jnp.where(columns <= rows, scores, -1e30) + key_bias[:, :span]
+
+
+def attention_kernel(
+    x_all, qkv_w, out_w, gain, cos, sin, head_gain, key_bias,
+    normed, qkv_raw, qkv_low, att_low, log_sums, part, keys, values,
+):
+    seq = x_all.shape[0]
+
+    def project(index):
+        rows = pl.ds(pl.multiple_of(index * BLOCK, BLOCK), BLOCK)
+        source = x_all[rows].astype(F32)
+        normed[rows] = (source * row_factor(source) * gain[...]).astype(BF16)
+        raw = jnp.dot(normed[rows], qkv_w[...], preferred_element_type=F32)
+        for b in range(3):
+            block = raw[:, 128 * b : 128 * (b + 1)]
+            qkv_raw[b, rows] = block
+            factor = lax.rsqrt(half_sums(block * block) * (1.0 / HEAD_DIM) + EPSILON)
+            scaled = block * factor * head_gain[b : b + 1]
+            turned = scaled * cos[rows] + partner(scaled) * sin[rows]
+            if b == 2:
+                turned = jnp.where(low_half(turned.shape), turned, block)
+            qkv_low[b, rows] = turned.astype(BF16)
+            if b == 2:
+                low = low_half(turned.shape)
+                swapped = pltpu.roll(turned, 64, 1)
+                keys[rows] = jnp.where(low, turned, swapped).astype(BF16)
+                values[rows] = jnp.where(low, swapped, turned).astype(BF16)
+
+    row_loop(seq // BLOCK, project)
+
+    def heads(b):
+        for i in range(seq // BLOCK):
+            rows, span = pl.ds(i * BLOCK, BLOCK), (i + 1) * BLOCK
+            query = qkv_low[b, rows]
+            low = low_half(query.shape)
+            outs, logs = [], []
+            for half in range(2):
+                chosen = jnp.where(low if half == 0 else jnp.logical_not(low), query, 0)
+                scores = attention_scores(chosen, keys[:span], key_bias[0:1], i * BLOCK, span)
+                top = jnp.max(scores, axis=-1, keepdims=True)
+                expanded = jnp.exp(scores - top)
+                sums = jnp.sum(expanded, axis=-1, keepdims=True)
+                probs = (expanded * (1.0 / sums)).astype(BF16)
+                outs.append(jnp.dot(probs, values[:span], preferred_element_type=F32))
+                logs.append(top + jnp.log(sums))
+            att_low[b, rows] = jnp.where(low, outs[0], outs[1]).astype(BF16)
+            log_sums[b, rows] = jnp.where(low, logs[0], logs[1])
+
+    row_loop(2, heads)
+
+    def project_out(index):
+        rows = pl.ds(pl.multiple_of(index * BLOCK, BLOCK), BLOCK)
+        sums = jnp.dot(att_low[0, rows], out_w[0], preferred_element_type=F32)
+        sums += jnp.dot(att_low[1, rows], out_w[1], preferred_element_type=F32)
+        part[index] = sums.astype(BF16)
+
+    row_loop(seq // BLOCK, project_out)
+
+
+NT = (((1,), (1,)), ((), ()))
+TN = (((0,), (0,)), ((), ()))
+
+
+def attention_back_kernel(
+    branch, qkv_w, out_w, cos, sin, head_gain, key_bias,
+    normed, qkv_raw, qkv_low, att_low, log_sums,
+    part, qkv_g, out_g, gain_g, keys, values, d_att, d_low, d_keys, d_values,
+):
+    seq = branch.shape[0]
+    root = 1.0 / math.sqrt(HEAD_DIM)
+    gain_g[...] = jnp.zeros_like(gain_g)
+    d_keys[...] = jnp.zeros_like(d_keys)
+    d_values[...] = jnp.zeros_like(d_values)
+
+    def prepare(index):
+        rows = pl.ds(pl.multiple_of(index * BLOCK, BLOCK), BLOCK)
+        block = qkv_low[2, rows].astype(F32)
+        low = low_half(block.shape)
+        swapped = pltpu.roll(block, 64, 1)
+        keys[rows] = jnp.where(low, block, swapped).astype(BF16)
+        values[rows] = jnp.where(low, swapped, block).astype(BF16)
+        for b in range(2):
+            d_att[b, rows] = lax.dot_general(
+                branch[rows], out_w[b], NT, preferred_element_type=F32
+            ).astype(BF16)
+
+    row_loop(seq // BLOCK, prepare)
+
+    def unturn(row, rows, grads, block):
+        back = grads * cos[rows] + partner(grads * sin[rows])
+        factor = lax.rsqrt(half_sums(block * block) * (1.0 / HEAD_DIM) + EPSILON)
+        gain_term = jnp.sum(back * block * factor, axis=0, keepdims=True)
+        scaled = back * head_gain[row : row + 1]
+        inner = half_sums(scaled * block) * (1.0 / HEAD_DIM)
+        return factor * scaled - block * (factor * factor * factor * inner), gain_term
+
+    def heads(b):
+        out_g[b] = lax.dot_general(
+            att_low[b], branch[...], TN, preferred_element_type=F32
+        ).astype(BF16)
+        for i in range(seq // BLOCK):
+            rows, span = pl.ds(i * BLOCK, BLOCK), (i + 1) * BLOCK
+            query, d_out = qkv_low[b, rows], d_att[b, rows]
+            logs = log_sums[b, rows]
+            low = low_half(query.shape)
+            d_query = []
+            for half in range(2):
+                side = low if half == 0 else jnp.logical_not(low)
+                chosen, d_chosen = jnp.where(side, query, 0), jnp.where(side, d_out, 0)
+                scores = attention_scores(chosen, keys[:span], key_bias[0:1], i * BLOCK, span)
+                probs = jnp.exp(scores - logs[:, 64 * half : 64 * half + 1])
+                d_probs = lax.dot_general(
+                    d_chosen, values[:span], NT, preferred_element_type=F32
+                )
+                delta = jnp.sum(probs * d_probs, axis=-1, keepdims=True)
+                d_scores = (probs * (d_probs - delta)).astype(BF16)
+                d_query.append(jnp.dot(d_scores, keys[:span], preferred_element_type=F32))
+                d_keys[:span] += lax.dot_general(
+                    d_scores, chosen, TN, preferred_element_type=F32
+                )
+                d_values[:span] += lax.dot_general(
+                    probs.astype(BF16), d_chosen, TN, preferred_element_type=F32
+                )
+            grads = (jnp.where(low, d_query[0], d_query[1]) * root).astype(BF16).astype(F32)
+            d_block, gain_term = unturn(0, rows, grads, qkv_raw[b, rows])
+            d_low[b, rows] = d_block.astype(BF16)
+            gain_g[0:1] += gain_term
+
+    row_loop(2, heads)
+
+    def finish(index):
+        rows = pl.ds(pl.multiple_of(index * BLOCK, BLOCK), BLOCK)
+        k_sum, v_sum = d_keys[rows], d_values[rows]
+        low = low_half(k_sum.shape)
+        k_sum = (k_sum + pltpu.roll(k_sum, 64, 1)) * root
+        v_sum = v_sum + pltpu.roll(v_sum, 64, 1)
+        grads = jnp.where(low, k_sum, v_sum).astype(BF16).astype(F32)
+        d_block, gain_term = unturn(2, rows, grads, qkv_raw[2, rows])
+        d_low[2, rows] = jnp.where(low, d_block, grads).astype(BF16)
+        gain_g[1:2] += gain_term
+        sums = jnp.zeros((BLOCK, part.shape[2]), F32)
+        for b in range(3):
+            sums += lax.dot_general(
+                d_low[b, rows], qkv_w[:, 128 * b : 128 * (b + 1)], NT, preferred_element_type=F32
+            )
+        part[index] = sums.astype(BF16)
+
+    row_loop(seq // BLOCK, finish)
+    for b in range(3):
+        grad = lax.dot_general(d_low[b], normed[...], TN, preferred_element_type=F32).astype(BF16)
+        for f in range(8):
+            qkv_g[f, 128 * b : 128 * (b + 1)] = grad[:, 256 * f : 256 * (f + 1)]
+
+
+def shaped(shape, kind=BF16):
+    return jax.ShapeDtypeStruct(shape, kind)
+
+
+def call(kernel, ins, outs, scratch=(), sems=None, number=None, flops=0):
+    scratch = list(scratch)
+    extra = {}
+    if sems is not None:
+        scratch += [pltpu.SemaphoreType.DMA((n,)) for n in sems]
+        extra = dict(collective_id=number, has_side_effects=True)
+    return pl.pallas_call(
+        kernel,
+        out_shape=tuple(shape for shape, _ in outs),
+        in_specs=[spec for _, spec in ins],
+        out_specs=tuple(spec for _, spec in outs),
+        scratch_shapes=scratch,
+        compiler_params=pltpu.CompilerParams(vmem_limit_bytes=VMEM_BYTES, **extra),
+    )(*[array for array, _ in ins])
+
+
+def split_heads(
+    inputs,
+    cotangent,
+    lengths,
+    qkv_weight,
+    out_weight,
+    gate_up,
+    down_weight,
+    attn_gain,
+    ffn_gain,
+    qk_gain,
+):
+    tokens, width = inputs.shape[1:]
+    seq = tokens * 4
+    c = lax.axis_index("ctx")
+    length = lengths[0]
+    positions = c * tokens + jnp.arange(tokens, dtype=jnp.int32)
+    keep = (positions < length).astype(F32)[:, None]
+    all_positions = jnp.arange(seq, dtype=jnp.int32)
+    key_bias = jnp.broadcast_to(jnp.where(all_positions < length, 0.0, -1e30)[None], (8, seq))
+    source = inputs[0]
+    d_out = (keep * cotangent[0].astype(F32)).astype(BF16)
+
+    query_cols, key_cols = HEADS * HEAD_DIM, KV_HEADS * HEAD_DIM
+    qkv_s = jnp.concatenate(
+        [
+            lax.dynamic_slice_in_dim(qkv_weight, c * 256, 256, 1),
+            lax.dynamic_slice_in_dim(qkv_weight, query_cols + c * 64, 64, 1),
+            lax.dynamic_slice_in_dim(qkv_weight, query_cols + key_cols + c * 64, 64, 1),
+        ],
+        axis=1,
+    )
+    rows, parts, units = gate_up.shape
+    gu_s = lax.dynamic_index_in_dim(
+        gate_up.reshape(rows, parts, 8, 4, units // 32), c, 3, keepdims=False
+    ).reshape(rows, parts * units // 4)
+    down_rows = down_weight.shape[0] // 4
+    dn_s = lax.dynamic_slice_in_dim(down_weight, c * down_rows, down_rows, 0)
+    gain_s = jnp.concatenate(
+        [attn_gain[None], ffn_gain[None], jnp.zeros((6, rows), BF16)], axis=0
+    ).astype(F32)
+
+    half_dim = HEAD_DIM // 2
+    angles = np.arange(seq)[:, None] * 10000.0 ** (-2.0 * np.arange(half_dim) / HEAD_DIM)[None]
+    cos = jnp.tile(jnp.asarray(np.cos(angles), F32), (1, 4))
+    sine = jnp.asarray(np.sin(angles), F32)
+    sin = jnp.tile(jnp.concatenate([-sine, sine], axis=1), (1, 2))
+    q_gain = jnp.tile(qk_gain[0].astype(F32), 2)
+    k_gain = jnp.concatenate([qk_gain[1].astype(F32), jnp.ones((HEAD_DIM,), F32)])
+    head_gain = jnp.concatenate(
+        [q_gain[None], q_gain[None], k_gain[None], jnp.zeros((5, 128), F32)], axis=0
+    )
+
+    qkv_w, out_w, gains, x_all = call(
+        gather_kernel,
+        [(qkv_s, HBM), (out_weight, HBM), (gain_s, HBM), (source, HBM)],
+        [
+            (shaped((8, rows, 384)), HBM),
+            (shaped((2, out_weight.shape[0], width)), HBM),
+            (shaped((8, 8, rows), F32), HBM),
+            (shaped((4, tokens, width)), HBM),
+        ],
+        sems=(40, 40, 8),
+        number=0,
+    )
+    attn_norm = gains[:, 0].reshape(1, width)
+    ffn_norm = gains[:, 1].reshape(1, width)
+    qkv_w = qkv_w.reshape(width, 384)
+    x_all = x_all.reshape(seq, width)
+    tables = [(cos, VMEM), (sin, VMEM), (head_gain, VMEM), (key_bias, VMEM)]
+    normed, qkv_raw, qkv_low, att_low, log_sums, part = call(
+        attention_kernel,
+        [(x_all, VMEM), (qkv_w, VMEM), (out_w, VMEM), (attn_norm, VMEM)] + tables,
+        [
+            (shaped((seq, width)), VMEM),
+            (shaped((3, seq, 128), F32), VMEM),
+            (shaped((3, seq, 128)), VMEM),
+            (shaped((2, seq, 128)), VMEM),
+            (shaped((2, seq, 128), F32), VMEM),
+            (shaped((4, tokens, width)), VMEM),
+        ],
+        [pltpu.VMEM((seq, 128), BF16)] * 2,
+    )
+    ctx_scratch = [
+        pltpu.VMEM((2, tokens, width), BF16),
+        pltpu.VMEM((2, tokens, width), BF16),
+        pltpu.VMEM((tokens, width), BF16),
+        pltpu.VMEM((tokens, width), BF16),
+    ]
+    gu_w, dn_w, dout_all, middle, mid_all = call(
+        feed_gather_kernel,
+        [
+            (gu_s, HBM),
+            (dn_s, HBM),
+            (d_out, HBM),
+            (part, HBM),
+            (source, VMEM),
+            (ffn_norm, VMEM),
+        ],
+        [
+            (shaped((8, rows, width)), HBM),
+            (shaped((8, down_rows, width)), HBM),
+            (shaped((4, tokens, width)), HBM),
+            (shaped((tokens, width), F32), VMEM),
+            (shaped((4, tokens, width)), HBM),
+        ],
+        ctx_scratch + [pltpu.VMEM((tokens, width), BF16)],
+        sems=(80, 80, 16),
+        number=1,
+    )
+    hidden_units = units // 4
+    gu_full = gu_w.reshape(width, parts * hidden_units)
+    dn_full = dn_w.reshape(hidden_units, width)
+    mid_full = mid_all.reshape(seq, width)
+    dout_full = dout_all.reshape(seq, width)
+    projected = jnp.dot(mid_full, gu_full, preferred_element_type=F32)
+    gate, up = projected[:, :hidden_units], projected[:, hidden_units:]
+    sigmoid = jax.nn.sigmoid(gate)
+    hidden = (gate * sigmoid * up).astype(BF16)
+    ffn_part = jnp.dot(hidden, dn_full, preferred_element_type=F32).astype(BF16)
+    d_hidden = contract_cols(dout_full, dn_full)
+    d_projected = jnp.concatenate(
+        [
+            (d_hidden * up * (sigmoid * (1.0 + gate * (1.0 - sigmoid)))).astype(BF16),
+            (d_hidden * gate * sigmoid).astype(BF16),
+        ],
+        axis=1,
+    )
+    dn_g = contract_rows(hidden, dout_full).astype(BF16)
+    gu_g = contract_rows(mid_full, d_projected).astype(BF16)
+    dmid_part = contract_cols(d_projected, gu_full).astype(BF16)
+
+    step = 64
+    count = (rows + down_rows) // step
+    gu_all, dn_all, layer_out, d_middle, ffn_gain_part, branch_all = call(
+        feed_reduce_kernel,
+        [
+            (gu_g.reshape(4, 2, rows, width), HBM),
+            (dn_g.reshape(4, 2, down_rows, width), HBM),
+            (ffn_part.reshape(4, tokens, width), HBM),
+            (dmid_part.reshape(4, tokens, width), HBM),
+            (middle, VMEM),
+            (d_out, VMEM),
+            (keep, VMEM),
+            (ffn_norm, VMEM),
+        ],
+        [
+            (shaped((4, rows, width)), HBM),
+            (shaped((4, down_rows, width)), HBM),
+            (shaped((tokens, width)), VMEM),
+            (shaped((tokens, width), F32), VMEM),
+            (shaped((1, width), F32), VMEM),
+            (shaped((4, tokens, width)), HBM),
+        ],
+        [
+            pltpu.VMEM((count, 4, step, width), BF16),
+            pltpu.VMEM((count, 4, step, width), BF16),
+            pltpu.VMEM((count, 4, step, width), BF16),
+            pltpu.VMEM((count, 4, step, width), BF16),
+            pltpu.VMEM((count, step, width), BF16),
+        ]
+        + ctx_scratch
+        + ctx_scratch
+        + [pltpu.VMEM((tokens, width), BF16)],
+        sems=(80, 80, 40),
+        number=2,
+    )
+    dnorm_part, qkv_g, out_g, head_gain_g = call(
+        attention_back_kernel,
+        [(branch_all.reshape(seq, width), VMEM), (qkv_w, VMEM), (out_w, VMEM)]
+        + tables
+        + [(a, VMEM) for a in (normed, qkv_raw, qkv_low, att_low, log_sums)],
+        [
+            (shaped((4, tokens, width)), VMEM),
+            (shaped((8, 384, rows)), VMEM),
+            (shaped((2, 128, width)), VMEM),
+            (shaped((8, 128), F32), VMEM),
+        ],
+        [
+            pltpu.VMEM((seq, 128), BF16),
+            pltpu.VMEM((seq, 128), BF16),
+            pltpu.VMEM((2, seq, 128), BF16),
+            pltpu.VMEM((3, seq, 128), BF16),
+            pltpu.VMEM((seq, 128), F32),
+            pltpu.VMEM((seq, 128), F32),
+        ],
+    )
+    qk_part = jnp.concatenate(
+        [
+            head_gain_g[0:1, :64] + head_gain_g[0:1, 64:],
+            head_gain_g[1:2, :64],
+            jnp.zeros((1, width - 128), F32),
+        ],
+        axis=1,
+    )
+    step = 192
+    count = 384 // step
+    qkv_all, out_all, input_grad, stats = call(
+        last_kernel,
+        [
+            (qkv_g.reshape(4, 2, 384, rows), HBM),
+            (out_g, HBM),
+            (dnorm_part, HBM),
+            (source, VMEM),
+            (d_middle, VMEM),
+            (attn_norm, VMEM),
+            (ffn_gain_part, VMEM),
+            (qk_part, VMEM),
+        ],
+        [
+            (shaped((4, 384, rows)), HBM),
+            (shaped((128, width)), VMEM),
+            (shaped((tokens, width)), VMEM),
+            (shaped((8, width), F32), VMEM),
+        ],
+        [
+            pltpu.VMEM((count, 4, step, rows), BF16),
+            pltpu.VMEM((count, 4, step, rows), BF16),
+            pltpu.VMEM((count, 4, step, rows), BF16),
+            pltpu.VMEM((count, 4, step, rows), BF16),
+            pltpu.VMEM((count, step, rows), BF16),
+        ]
+        + ctx_scratch
+        + [
+            pltpu.VMEM((128, width), BF16),
+            pltpu.VMEM((128, width), BF16),
+            pltpu.VMEM((128, width), BF16),
+            pltpu.VMEM((4, 128, width), BF16),
+            pltpu.VMEM((8, width), F32),
+            pltpu.VMEM((8, 8, width), F32),
+            pltpu.VMEM((4, 8, width), F32),
+        ],
+        sems=(60, 60, 20),
+        number=3,
+    )
+    f = lax.axis_index("fsdp")
+    qkv_grad = jnp.concatenate(
+        [
+            jnp.transpose(qkv_all[:, :256], (2, 0, 1)).reshape(rows, query_cols),
+            jnp.transpose(qkv_all[:, 256:320], (2, 0, 1)).reshape(rows, key_cols),
+            jnp.transpose(qkv_all[:, 320:], (2, 0, 1)).reshape(rows, key_cols),
+        ],
+        axis=1,
+    ).astype(F32)
+    gate_up_grad = (
+        jnp.transpose(gu_all.reshape(4, rows, parts, 8, units // 32), (1, 2, 3, 0, 4))
+        .reshape(rows, parts, units)
+        .astype(F32)
+    )
+    return (
+        layer_out[None],
+        input_grad[None],
+        qkv_grad,
+        out_all.astype(F32),
+        gate_up_grad,
+        dn_all.reshape(4 * down_rows, width).astype(F32),
+        lax.dynamic_slice_in_dim(stats[0], f * rows, rows, 0),
+        lax.dynamic_slice_in_dim(stats[1], f * rows, rows, 0),
+        stats[2, :128].reshape(2, 64),
+    )
+
+
 def solution(mesh):
+    sizes = (mesh.shape["fsdp"], mesh.shape["ctx"])
     return jax.shard_map(
-        on_device,
+        split_heads if sizes == (8, 4) else on_device,
         mesh=mesh,
         in_specs=(
             P("fsdp", "ctx", None),

time: 2390 us -> 676 us (0.28)
  waiting for transfers between devices: 1980 us -> 0 us
  Pallas kernels: 0 us -> 521 us
  matrix products: 187 us -> 65.4 us
  blocking collectives: 96.8 us -> 0 us
  other arithmetic: 55.2 us -> 13.4 us
    reduce_scatter x5 -> x0, waiting for transfers between devices: 987 us -> none  [the longest x1 546 us: on_device(): lax.psum_scatter(jnp.einsum('td,tgf->dgf', columns, d_proj_low, preferred...]
    all_gather x5 -> x0, waiting for transfers between devices: 942 us -> none  [the longest x1 635 us: on_device(): lax.all_gather(gate_up, 'fsdp', axis=0, tiled=True)]
    pallas_call x0 -> x6, Pallas kernels: none -> 521 us  [call(): pl.pallas_call(kernel, out_shape=tuple((shape for shape, _ in outs)), in_...]
    dot_general x20 -> x2, matrix products: 142 us -> 23.5 us  [the longest x1 15 us: split_heads(): projected = jnp.dot(mid_full, gu_full, preferred_element_type=F32)]
    psum x2 -> x0, blocking collectives: 52.2 us -> none  [the longest x1 43.1 us: on_device(): qk_total = lax.psum(qk_part, ('fsdp', 'ctx'))]
    psum x1 -> x0, waiting for transfers between devices: 49.7 us -> none  [on_device(): lax.psum(gate_up_shard, 'ctx').astype(jnp.float32)]
    all_gather x2 -> x0, blocking collectives: 28.1 us -> none  [the longest x1 14.2 us: on_device(): lax.all_gather(attn_gain, 'fsdp', axis=0, tiled=True)]
  transfers between devices with their start and end apart: 11 -> 0, of which waited for: 9 -> 0; matrix products, arithmetic and copies ran while one was open for 8% -> 0% of each run, Pallas kernels for 0% -> 0%
where the time goes in v1:
time: 676 us; the launch traced here: 665 us
  Pallas kernels  521 us (77%)
  matrix products  65.4 us (10%)
  local copies, waits for them, and re-layouts  63.6 us (9%)
  other arithmetic  13.4 us (2%)
    pallas_call x6, Pallas kernels, call(): pl.pallas_call(kernel, out_shape=tuple((shape for shape, _ in outs)), in_...  521 us
    convert_element_type x2, local copies, waits for them, and re-layouts, split_heads(): gate_up_grad = jnp.transpose(gu_all.reshape(4, rows, parts, 8, units // 3...  23.3 us
    dot_general x2, matrix products, contract_cols(): lax.dot_general(left, right, (((1,), (1,)), ((), ())), preferred_element_...  23.1 us
    dot_general x2, matrix products, contract_rows(): lax.dot_general(left, right, (((0,), (0,)), ((), ())), preferred_element_...  18.8 us
    dot_general x1, matrix products, split_heads(): projected = jnp.dot(mid_full, gu_full, preferred_element_type=F32)  15 us

profile of v1, /device:TPU:13, one launch (start us, length us, event | category | flops | bytes accessed | tf_op | source)
XLA Modules:
  0.0 665.3 jit_solution(1167119393933302363)
XLA Ops:
  0.7 1.1 constant_dynamic-slice_fusion.3
  1.8 0.9 constant_dynamic-slice_fusion.4
  5.6 43.1 %shard_map.187 = (bf16[8,256,384]{2,1,0:T(8,128)(2,1)}, bf16[2,128,2048]{2,1,0:T(8,128)(2,1)}, f32[8,8,256]{2,1,0:T(8,128)}, bf16[4,256,2048]{2,1,0:T(8,128)(2,1)}) custom-call(bf16[256,384]{1,0:T(8,128)(2,1)} %pad_maximum_fusion.3.qkv_s, bf16[128,2048]{1,0:T(8,128)(2,1)} %out_s.1, f32[8,256]{1,0:T(8,128)} %maximum_convert_fusion.1.gain_s, ...), custom_call_target="tpu_custom_call" | custom-call | tf_op jit(solution)/shard_map/pallas_call | solution.py:1093
  48.7 1.5 fusion.7
  53.1 0.9 tile.29
  54.1 1.0 copy.40.cos
  55.2 1.0 copy.41.sin
  56.2 24.2 %shard_map.188 = (bf16[1024,2048]{1,0:T(8,128)(2,1)}, f32[3,1024,128]{2,1,0:T(8,128)}, bf16[3,1024,128]{2,1,0:T(8,128)(2,1)}, bf16[2,1024,128]{2,1,0:T(8,128)(2,...) custom-call(bf16[1024,2048]{1,0:T(8,128)(2,1)} %bitcast.80, bf16[2048,384]{1,0:T(8,128)(2,1)} %bitcast.75, ...), custom_call_target="tpu_custom_call" | custom-call | tf_op jit(solution)/shard_map/pallas_call | solution.py:1093
  81.3 8.0 %reshape.112 = bf16[256,2,8,4,128]{4,3,2,1,0:T(4,128)(2,1)} reshape(bf16[256,2,4096]{2,1,0:T(2,128)(2,1)} %param.17) | data formatting | bytes 8388608 | tf_op jit(solution)/shard_map/reshape | solution.py:1137
  89.3 8.4 %dynamic-slice_reduce_fusion = bf16[256,2,8,128]{3,2,1,0:T(8,128)(2,1)S(1)} fusion(bf16[256,2,8,4,128]{4,3,2,1,0:T(4,128)(2,1)} %reshape.112, s32[]{:T(128)S(6)} %select_n.28), kind=kLoop, calls=%fused_computation.12 | loop fusion | bytes 2097156 | tf_op jit(solution)/shard_map/jit(dynamic_index_in_dim)/dynamic_slice | solution.py:1136
  97.8 1.2 copy.59
  99.0 1.2 fusion.dout_s
  100.2 161.5 %shard_map.189 = (bf16[8,256,2048]{2,1,0:T(8,128)(2,1)}, bf16[8,128,2048]{2,1,0:T(8,128)(2,1)}, bf16[4,256,2048]{2,1,0:T(8,128)(2,1)}, f32[256,2048]{1,0:T(8,128)}, bf16[4,256,2048]{2,1,0:T(8,128)(2,1)}) custom-call(bf16[256,2048]{1,0:T(8,128)(2,1)} %bitcast.79, bf16[128,2048]{1,0:T(8,128)(2,1)} %constant_dynamic-slice_fusion.5.dn_s, ...), custom_call_target="tpu_custom_call" | custom-call | tf_op jit(solution)/shard_map/pallas_call | solution.py:1093
  261.8 15.0 %fusion.9 = f32[1024,2048]{0,1:T(8,128)} fusion(bf16[1024,2048]{1,0:T(8,128)(2,1)} %bitcast.101, bf16[2048,2048]{1,0:T(8,128)(2,1)} %bitcast.99), kind=kOutput, calls=%fused_computation.40 | convolution fusion | flops 8589934592 | bytes 20971520 | tf_op jit(solution)/shard_map/dot_general | solution.py:1218
  276.8 11.0 %multiply_convert_fusion.2 = (bf16[1024,1024]{0,1:T(8,128)(2,1)S(1)}, bf16[1024,1024]{0,1:T(8,128)(2,1)}, bf16[1024,1024]{0,1:T(8,128)(2,1)S(1)}) fusion(f32[1024,2048]{0,1:T(8,128)} %fusion.9, bf16[1024,2048]{1,0:T(8,128)(2,1)S(1)} %bitcast.103, bf16[1024,2048]{1,0:T(8,128)(2,1)} %bitcast.105), kind=kOutput, calls=%fused_computation.4 | convolution fusion | flops 4311744512 | bytes 23068672 | tf_op jit(solution)/shard_map/dot_general | solution.py:75
  287.8 12.1 %convolution_convert_fusion.1 = bf16[1024,2048]{1,0:T(8,128)(2,1)} fusion(bf16[2048,2048]{1,0:T(8,128)(2,1)S(1)} %bitcast.100, bf16[1024,1024]{0,1:T(8,128)(2,1)} %get-tuple-element.68, bf16[1024,1024]{0,1:T(8,128)(2,1)S(1)} %get-tuple-element.67), kind=kOutput, calls=%fused_computation.6 | convolution fusion | flops 8600420352 | bytes 16777216 | tf_op jit(solution)/shard_map/dot_general | solution.py:75
  299.9 8.5 %convolution_convert_fusion.2 = bf16[1024,2048]{1,0:T(8,128)(2,1)} fusion(bf16[1024,1024]{0,1:T(8,128)(2,1)S(1)} %get-tuple-element.69, bf16[1024,2048]{1,0:T(8,128)(2,1)} %bitcast.106), kind=kOutput, calls=%fused_computation.7 | convolution fusion | flops 4297064448 | bytes 10485760 | tf_op jit(solution)/shard_map/dot_general | solution.py:1222
  308.4 6.1 convolution_convert_fusion.3
  314.5 12.7 %convolution_convert_fusion = bf16[2048,2048]{1,0:T(8,128)(2,1)} fusion(bf16[1024,2048]{1,0:T(8,128)(2,1)S(1)} %bitcast.102, bf16[1024,1024]{0,1:T(8,128)(2,1)S(1)} %copy-done.11, bf16[1024,1024]{0,1:T(8,128)(2,1)S(1)} %get-tuple-element.67), kind=kOutput, calls=%fused_computation | convolution fusion | flops 8602517504 | bytes 16777216 | tf_op jit(solution)/shard_map/dot_general | solution.py:69
  327.9 179.8 %shard_map.190 = (bf16[4,256,2048]{2,1,0:T(8,128)(2,1)}, bf16[4,128,2048]{2,1,0:T(8,128)(2,1)}, bf16[256,2048]{1,0:T(8,128)(2,1)}, f32[256,2048]{1,0:T(8,128)}, ...) custom-call(bf16[4,2,256,2048]{3,2,1,0:T(8,128)(2,1)} %bitcast.74, bf16[4,2,128,2048]{3,2,1,0:T(8,128)(2,1)} %bitcast.84, ...), custom_call_target="tpu_custom_call" | custom-call | tf_op jit(solution)/shard_map/pallas_call | solution.py:1093
  507.7 29.4 %shard_map.191 = (bf16[4,256,2048]{2,1,0:T(8,128)(2,1)}, bf16[8,384,256]{2,1,0:T(8,128)(2,1)}, bf16[2,128,2048]{2,1,0:T(8,128)(2,1)}, f32[8,128]{1,0:T(8,128)}) custom-call(bf16[1024,2048]{1,0:T(8,128)(2,1)} %bitcast.78, bf16[2048,384]{1,0:T(8,128)(2,1)} %bitcast.76, bf16[2,128,2048]{2,1,0:T(8,128)(2,1)} %get-tuple-element.40.out_w, f32[1024,128]{1,0:T(8,128)} %copy.40.cos, ...), custom_call_target="tpu_custom_call" | custom-call | tf_op jit(solution)/shard_map/pallas_call | solution.py:1093
  537.1 0.9 fusion.8
  538.7 82.8 %shard_map.192 = (bf16[4,384,256]{2,1,0:T(8,128)(2,1)}, bf16[128,2048]{1,0:T(8,128)(2,1)}, bf16[256,2048]{1,0:T(8,128)(2,1)}, f32[8,2048]{1,0:T(8,128)}) custom-call(bf16[4,2,384,256]{3,2,1,0:T(8,128)(2,1)} %bitcast.88, bf16[2,128,2048]{2,1,0:T(8,128)(2,1)} %get-tuple-element.56.out_g, bf16[4,256,2048]{2,1,0:T(8,128)(2,1)} %get-tuple-element.57.dnorm_part, ...), custom_call_target="tpu_custom_call" | custom-call | tf_op jit(solution)/shard_map/pallas_call | solution.py:1093
  621.5 0.9 fusion.6
  623.0 6.9 %copy.57 = f32[128,8,16,128]{3,2,1,0:T(8,128)} copy(bf16[128,8,16,128]{3,1,2,0:T(8,128)(2,1)} %bitcast.77) | data formatting | bytes 12582912
  629.9 12.0 %copy.50 = f32[256,2,8,4,128]{4,3,2,1,0:T(4,128)} copy(f32[256,2,8,4,128]{4,2,1,0,3:T(8,128)} %bitcast.70) | data formatting | bytes 16777216 | tf_op jit(solution)/shard_map/convert_element_type | solution.py:1350
  641.9 11.3 %reshape.132 = f32[256,2,4096]{2,1,0:T(2,128)} reshape(f32[256,2,8,4,128]{4,3,2,1,0:T(4,128)} %copy.50) | data formatting | bytes 16777216 | tf_op jit(solution)/shard_map/convert_element_type | solution.py:1350
  653.7 1.3 maximum_convert_fusion
  655.0 2.2 convert_element_type.91
  658.5 4.3 bitcast_convert_fusion
  662.8 1.0 copy.63
  663.8 1.0 copy.64
  (53 shorter events, 9.7 us)
Async XLA Ops:
  0.6 79.8 %copy-start = (bf16[512,2048]{1,0:T(8,128)(2,1)S(1)}, bf16[512,2048]{1,0:T(8,128)(2,1)}, u32[]{:S(2)}) copy-start(bf16[512,2048]{1,0:T(8,128)(2,1)} %param.18) | copy-start | bytes 6291460
  0.7 54.5 %copy-start.6 = (f32[1024,64]{0,1:T(8,128)S(1)}, f32[1024,64]{0,1:T(8,128)}, u32[]{:S(2)}) copy-start(f32[1024,64]{0,1:T(8,128)} %constant.63) | copy-start | bytes 786436
  89.3 9.7 %copy-start.4 = (bf16[1,256,2048]{2,1,0:T(8,128)(2,1)S(1)}, bf16[1,256,2048]{2,1,0:T(8,128)(2,1)}, u32[]{:S(2)}) copy-start(bf16[1,256,2048]{2,1,0:T(8,128)(2,1)} %param.13) | copy-start | bytes 3145732
  261.8 15.0 %copy-start.9 = (bf16[4,256,2048]{2,1,0:T(8,128)(2,1)S(1)}, bf16[4,256,2048]{2,1,0:T(8,128)(2,1)}, u32[]{:S(2)}) copy-start(bf16[4,256,2048]{2,1,0:T(8,128)(2,1)} %get-tuple-element.44) | copy-start | bytes 12582916
  276.8 11.0 %copy-start.7 = (bf16[8,256,2048]{2,1,0:T(8,128)(2,1)S(1)}, bf16[8,256,2048]{2,1,0:T(8,128)(2,1)}, u32[]{:S(2)}) copy-start(bf16[8,256,2048]{2,1,0:T(8,128)(2,1)} %get-tuple-element.46) | copy-start | bytes 25165828
  299.9 8.5 %copy-start.10 = (bf16[4,256,2048]{2,1,0:T(8,128)(2,1)S(1)}, bf16[4,256,2048]{2,1,0:T(8,128)(2,1)}, u32[]{:S(2)}) copy-start(bf16[4,256,2048]{2,1,0:T(8,128)(2,1)} %get-tuple-element.44) | copy-start | bytes 12582916
  308.4 6.1 copy-start.8
  308.4 6.1 copy-start.11
  641.9 11.3 %copy-start.5 = (bf16[4,384,256]{2,1,0:T(8,128)(2,1)S(1)}, bf16[4,384,256]{2,1,0:T(8,128)(2,1)}, u32[]{:S(2)}) copy-start(bf16[4,384,256]{2,1,0:T(8,128)(2,1)} %get-tuple-element.62) | copy-start | bytes 2359300
  655.0 7.8 %copy-start.2 = (bf16[256,2048]{1,0:T(8,128)(2,1)S(1)}, bf16[256,2048]{1,0:T(8,128)(2,1)}, u32[]{:S(2)}) copy-start(bf16[256,2048]{1,0:T(8,128)(2,1)} %get-tuple-element.48) | copy-start | bytes 3145732
  658.5 6.2 copy-start.1
  658.5 5.3 copy-start.3

commit v2 on v1

--- a/solution.py
+++ b/solution.py
@@ -409,31 +409,35 @@
         self.open = []
 
 
-def spread_plane(links, place, chunks, ahead=2):
-    z_slot, x_slot = links.slots(4 * len(chunks)), links.slots(4 * len(chunks))
-
-    def begin(k):
-        src, dst = chunks[k]
-        for other in place.others:
-            links.send(src, dst(place.f), z_slot + 4 * k + place.z, place.z_dev(other))
-        links.send(src, dst(place.f), x_slot + 4 * k + place.z, place.x_dev)
-
-    for k in range(min(ahead, len(chunks))):
-        begin(k)
-    yield
-    for k in range(len(chunks)):
-        dst = chunks[k][1]
+class SpreadPlane:
+    def __init__(self, links, place, chunks):
+        self.links, self.place, self.chunks = links, place, chunks
+        self.z_slot, self.x_slot = links.slots(4 * len(chunks)), links.slots(4 * len(chunks))
+
+    def begin_z(self):
+        place = self.place
+        for k, (src, dst) in enumerate(self.chunks):
+            slot = self.z_slot + 4 * k + place.z
+            for other in place.others:
+                self.links.send(src, dst(place.f), slot, place.z_dev(other))
+
+    def begin_x(self, k):
+        src, dst = self.chunks[k]
+        slot = self.x_slot + 4 * k + self.place.z
+        self.links.send(src, dst(self.place.f), slot, self.place.x_dev)
+
+    def forward(self, k):
+        place, dst = self.place, self.chunks[k][1]
         for other in place.others:
             block = dst(other * 2 + place.x)
-            links.arrive(block, z_slot + 4 * k + other)
-            links.send(block, block, x_slot + 4 * k + other, place.x_dev)
-        if k + ahead < len(chunks):
-            begin(k + ahead)
-        yield
-    for k in range(len(chunks)):
-        for z in range(4):
-            links.arrive(chunks[k][1](z * 2 + place.xo), x_slot + 4 * k + z)
-    yield
+            self.links.arrive(block, self.z_slot + 4 * k + other)
+            self.links.send(block, block, self.x_slot + 4 * k + other, place.x_dev)
+
+    def end(self):
+        for k in range(len(self.chunks)):
+            for z in range(4):
+                block = self.chunks[k][1](z * 2 + self.place.xo)
+                self.links.arrive(block, self.x_slot + 4 * k + z)
 
 
 def reduce_plane(links, place, chunks, own, from_x, to_z, from_z, total, done, ahead=2):
@@ -525,15 +529,21 @@
                     self.slot + 3 * k + side,
                     place.core_dev,
                 )
-                self.loads[side, k] = self.links.local(
-                    self.part.at[y * 2 + place.core, rows], self.own.at[side, rows]
-                )
+                if self.own is not None:
+                    self.loads[side, k] = self.links.local(
+                        self.part.at[y * 2 + place.core, rows], self.own.at[side, rows]
+                    )
 
     def pair(self, side, k):
         rows = self.parts[k]
         self.links.arrive(self.from_core.at[side, rows], self.slot + 3 * k + side)
-        self.loads[side, k].wait()
-        return self.own[side, rows].astype(F32) + self.from_core[side, rows].astype(F32)
+        if self.own is None:
+            y = self.place.y if side else self.place.yo
+            own = self.part[y * 2 + self.place.core, rows]
+        else:
+            self.loads[side, k].wait()
+            own = self.own[side, rows]
+        return own.astype(F32) + self.from_core[side, rows].astype(F32)
 
     def cross(self, k):
         rows = self.parts[k]
@@ -555,130 +565,6 @@
 
 def row_factor(values):
     return lax.rsqrt(jnp.mean(values * values, axis=-1, keepdims=True) + EPSILON)
-
-
-def gather_kernel(
-    qkv_s, out_s, gain_s, x_s, qkv_w, out_w, gains, x_all, send_sems, recv_sems, local_sems
-):
-    place = Place()
-    links = Links(place, send_sems, recv_sems, local_sems)
-    fellows = [lax.rem(place.f + d, 8) for d in range(1, 8)]
-    place.meet([(f, place.c) for f in fellows] + [place.core_dev, place.y_dev])
-    plane = spread_plane(links, place, [(qkv_s, lambda f: qkv_w.at[f])])
-    next(plane)
-    kept = [
-        links.local(qkv_s, qkv_w.at[place.f]),
-        links.local(gain_s, gains.at[place.f]),
-        links.local(x_s, x_all.at[place.c]),
-    ]
-    parts = halves(x_s.shape[0])
-    spread = SpreadCtx(links, place, x_all, parts)
-    for k, rows in enumerate(parts):
-        spread.begin(k, x_s.at[rows])
-    gain_slot = links.slots(8)
-    for f in fellows:
-        links.send(gain_s, gains.at[place.f], gain_slot + place.f, (f, place.c))
-
-    root_slot, side_slot = links.slots(1), links.slots(1)
-    holds = place.z == place.c
-    down = [
-        links.copy(out_s, out_w.at[place.x], root_slot, place.z_dev(other))
-        for other in place.others
-    ]
-    side = links.copy(out_s, out_w.at[place.x], side_slot, place.x_dev)
-    onward = links.copy(out_w.at[place.x], out_w.at[place.x], side_slot, place.x_dev)
-    own = pltpu.make_async_copy(out_s, out_w.at[place.x], local_sems.at[links.locals])
-    links.locals += 1
-
-    @pl.when(holds)
-    def _():
-        for made in down:
-            made.start()
-        side.start()
-        own.start()
-
-    next(plane)
-    for k in range(len(parts)):
-        spread.forward(k)
-
-    @pl.when(jnp.logical_not(holds))
-    def _():
-        links.arrive(out_w.at[place.x], root_slot)
-        onward.start()
-
-    for f in fellows:
-        links.arrive(gains.at[f], gain_slot + f)
-    next(plane)
-    spread.end()
-    links.arrive(out_w.at[place.xo], side_slot)
-    for made in kept:
-        made.wait()
-    links.finish()
-
-    @pl.when(holds)
-    def _():
-        own.wait()
-        for made in down:
-            made.wait_send()
-        side.wait_send()
-
-    @pl.when(jnp.logical_not(holds))
-    def _():
-        onward.wait_send()
-
-
-def feed_gather_kernel(
-    gu_s, dn_s, dout_s, part, x_s, gain, gu_w, dn_w, dout_all, middle, mid_all,
-    own, from_core, to_y, from_y, mid_low, send_sems, recv_sems, local_sems,
-):
-    place = Place()
-    links = Links(place, send_sems, recv_sems, local_sems)
-    place.meet(place.neighbours())
-    step = 64
-    chunks = []
-    for src, dst in ((gu_s, gu_w), (dn_s, dn_w)):
-        for first in range(0, src.shape[0], step):
-            rows = pl.ds(first, step)
-            chunks.append((src.at[rows], lambda f, dst=dst, rows=rows: dst.at[f, rows]))
-    plane = spread_plane(links, place, chunks)
-    next(plane)
-    parts = halves(x_s.shape[0])
-    reduce = ReduceCtx(links, place, part, parts, own, from_core, to_y, from_y)
-    reduce.begin()
-    kept = [
-        links.local(gu_s, gu_w.at[place.f]),
-        links.local(dn_s, dn_w.at[place.f]),
-        links.local(dout_s, dout_all.at[place.c]),
-    ]
-    for k in range(2):
-        reduce.cross(k)
-    dout = SpreadCtx(links, place, dout_all, parts)
-    for k, rows in enumerate(parts):
-        dout.begin(k, dout_s.at[rows], y_too=False)
-    next(plane)
-    mid = SpreadCtx(links, place, mid_all, parts)
-    for k, rows in enumerate(parts):
-        value = x_s[rows].astype(F32) + reduce.total(k)
-        middle[rows] = value
-        mid_low[rows] = (value * row_factor(value) * gain[...]).astype(BF16)
-        mid.begin(k, mid_low.at[rows])
-        kept.append(links.local(mid_low.at[rows], mid_all.at[place.c, rows]))
-    next(plane)
-    for k in range(2):
-        mid.forward(k)
-    for k, rows in enumerate(parts):
-        dout.begin_y(k, dout_s.at[rows])
-    next(plane)
-    next(plane)
-    for k in range(2):
-        dout.forward(k)
-    for _ in plane:
-        pass
-    mid.end()
-    dout.end()
-    for made in kept:
-        made.wait()
-    links.finish()
 
 
 def feed_reduce_kernel(
@@ -928,17 +814,93 @@
     return jnp.where(columns <= rows, scores, -1e30) + key_bias[:, :span]
 
 
-def attention_kernel(
-    x_all, qkv_w, out_w, gain, cos, sin, head_gain, key_bias,
-    normed, qkv_raw, qkv_low, att_low, log_sums, part, keys, values,
+def forward_kernel(
+    qkv_s, out_s, gain_s, x_s, gu_s, dn_s, dout_s, cos_h, sin_h, head_gain, key_bias,
+    qkv_wh, out_wh, gains, normed_h, qkv_raw_h, qkv_low_h, att_low_h, log_sums_h,
+    gu_w, dn_w, dout_all, middle, mid_all,
+    cos, sin, gain_blocks, qkv_w, out_w, x_all, normed, qkv_raw, qkv_low, att_low, log_sums,
+    part, keys, values, from_core, to_y, from_y, mid_low, send_sems, recv_sems, local_sems,
 ):
-    seq = x_all.shape[0]
+    place = Place()
+    links = Links(place, send_sems, recv_sems, local_sems)
+    fellows = [lax.rem(place.f + d, 8) for d in range(1, 8)]
+    place.meet([(f, place.c) for f in fellows] + [place.core_dev, place.y_dev])
+
+    qkv_plane = SpreadPlane(links, place, [(qkv_s, lambda f: qkv_w.at[f])])
+    qkv_plane.begin_z()
+    qkv_plane.begin_x(0)
+    tokens = x_s.shape[0]
+    parts = halves(tokens)
+    x_spread = SpreadCtx(links, place, x_all, parts)
+    for k, rows in enumerate(parts):
+        x_spread.begin(k, x_s.at[rows])
+    gain_slot = links.slots(8)
+    for f in fellows:
+        links.send(gain_s, gain_blocks.at[place.f], gain_slot + place.f, (f, place.c))
+    kept = [
+        links.local(qkv_s, qkv_w.at[place.f]),
+        links.local(gain_s, gain_blocks.at[place.f]),
+        links.local(x_s, x_all.at[place.c]),
+        links.local(cos_h, cos),
+        links.local(sin_h, sin),
+    ]
+
+    root_slot, side_slot = links.slots(1), links.slots(1)
+    holds = place.z == place.c
+    down = [
+        links.copy(out_s, out_w.at[place.x], root_slot, place.z_dev(other))
+        for other in place.others
+    ]
+    side = links.copy(out_s, out_w.at[place.x], side_slot, place.x_dev)
+    onward = links.copy(out_w.at[place.x], out_w.at[place.x], side_slot, place.x_dev)
+    own = pltpu.make_async_copy(out_s, out_w.at[place.x], local_sems.at[links.locals])
+    links.locals += 1
+
+    @pl.when(holds)
+    def _():
+        for made in down:
+            made.start()
+        side.start()
+        own.start()
+
+    step = 64
+    chunks = []
+    for src, dst in ((dn_s, dn_w), (gu_s, gu_w)):
+        for first in range(0, src.shape[0], step):
+            rows = pl.ds(first, step)
+            chunks.append((src.at[rows], lambda f, dst=dst, rows=rows: dst.at[f, rows]))
+    plane = SpreadPlane(links, place, chunks)
+    plane.begin_z()
+    plane.begin_x(0)
+    plane.begin_x(1)
+    qkv_plane.forward(0)
+    for k in range(2, len(chunks)):
+        plane.begin_x(k)
+    last = [
+        links.local(gu_s, gu_w.at[place.f]),
+        links.local(dn_s, dn_w.at[place.f]),
+        links.local(dout_s, dout_all.at[place.c]),
+    ]
+    for f in fellows:
+        links.arrive(gain_blocks.at[f], gain_slot + f)
+    for made in kept:
+        made.wait()
+    gains[...] = jnp.zeros_like(gains)
+    for f in range(8):
+        gains[0:2, 256 * f : 256 * (f + 1)] = gain_blocks[f, 0:2]
+    dout = SpreadCtx(links, place, dout_all, parts)
+    for k, rows in enumerate(parts):
+        x_spread.forward(k)
+        dout.begin(k, dout_s.at[rows])
+    x_spread.end()
+    qkv_plane.end()
 
     def project(index):
         rows = pl.ds(pl.multiple_of(index * BLOCK, BLOCK), BLOCK)
-        source = x_all[rows].astype(F32)
-        normed[rows] = (source * row_factor(source) * gain[...]).astype(BF16)
-        raw = jnp.dot(normed[rows], qkv_w[...], preferred_element_type=F32)
+        source = x_all[index].astype(F32)
+        normed[rows] = (source * row_factor(source) * gains[0:1]).astype(BF16)
+        weight = qkv_w[...].reshape(normed.shape[1], qkv_w.shape[2])
+        raw = jnp.dot(normed[rows], weight, preferred_element_type=F32)
         for b in range(3):
             block = raw[:, 128 * b : 128 * (b + 1)]
             qkv_raw[b, rows] = block
@@ -954,7 +916,14 @@
                 keys[rows] = jnp.where(low, turned, swapped).astype(BF16)
                 values[rows] = jnp.where(low, swapped, turned).astype(BF16)
 
+    seq = normed.shape[0]
     row_loop(seq // BLOCK, project)
+    last += [
+        links.local(normed, normed_h),
+        links.local(qkv_raw, qkv_raw_h),
+        links.local(qkv_low, qkv_low_h),
+        links.local(qkv_w, qkv_wh),
+    ]
 
     def heads(b):
         for i in range(seq // BLOCK):
@@ -976,6 +945,19 @@
 
     row_loop(2, heads)
 
+    @pl.when(jnp.logical_not(holds))
+    def _():
+        links.arrive(out_w.at[place.x], root_slot)
+        onward.start()
+
+    @pl.when(holds)
+    def _():
+        own.wait()
+
+    for k in range(len(parts)):
+        dout.forward(k)
+    links.arrive(out_w.at[place.xo], side_slot)
+
     def project_out(index):
         rows = pl.ds(pl.multiple_of(index * BLOCK, BLOCK), BLOCK)
         sums = jnp.dot(att_low[0, rows], out_w[0], preferred_element_type=F32)
@@ -983,6 +965,45 @@
         part[index] = sums.astype(BF16)
 
     row_loop(seq // BLOCK, project_out)
+    reduce = ReduceCtx(links, place, part, parts, None, from_core, to_y, from_y)
+    reduce.begin()
+    last += [
+        links.local(att_low, att_low_h),
+        links.local(log_sums, log_sums_h),
+        links.local(out_w, out_wh),
+    ]
+    for k in range(2):
+        reduce.cross(k)
+    plane.forward(0)
+    plane.forward(1)
+    mid = SpreadCtx(links, place, mid_all, parts)
+    for k, rows in enumerate(parts):
+        value = x_all[place.c, rows].astype(F32) + reduce.total(k)
+        middle[rows] = value
+        mid_low[rows] = (value * row_factor(value) * gains[1:2]).astype(BF16)
+        mid.begin(k, mid_low.at[rows])
+        last.append(links.local(mid_low.at[rows], mid_all.at[place.c, rows]))
+    plane.forward(2)
+    for k in range(2):
+        mid.forward(k)
+    for k in range(3, len(chunks)):
+        plane.forward(k)
+    plane.end()
+    mid.end()
+    dout.end()
+    for made in last:
+        made.wait()
+    links.finish()
+
+    @pl.when(holds)
+    def _():
+        for made in down:
+            made.wait_send()
+        side.wait_send()
+
+    @pl.when(jnp.logical_not(holds))
+    def _():
+        onward.wait_send()
 
 
 NT = (((1,), (1,)), ((), ()))
@@ -1153,63 +1174,61 @@
         [q_gain[None], q_gain[None], k_gain[None], jnp.zeros((5, 128), F32)], axis=0
     )
 
-    qkv_w, out_w, gains, x_all = call(
-        gather_kernel,
-        [(qkv_s, HBM), (out_weight, HBM), (gain_s, HBM), (source, HBM)],
-        [
-            (shaped((8, rows, 384)), HBM),
-            (shaped((2, out_weight.shape[0], width)), HBM),
-            (shaped((8, 8, rows), F32), HBM),
-            (shaped((4, tokens, width)), HBM),
-        ],
-        sems=(40, 40, 8),
-        number=0,
-    )
-    attn_norm = gains[:, 0].reshape(1, width)
-    ffn_norm = gains[:, 1].reshape(1, width)
-    qkv_w = qkv_w.reshape(width, 384)
-    x_all = x_all.reshape(seq, width)
-    tables = [(cos, VMEM), (sin, VMEM), (head_gain, VMEM), (key_bias, VMEM)]
-    normed, qkv_raw, qkv_low, att_low, log_sums, part = call(
-        attention_kernel,
-        [(x_all, VMEM), (qkv_w, VMEM), (out_w, VMEM), (attn_norm, VMEM)] + tables,
-        [
-            (shaped((seq, width)), VMEM),
-            (shaped((3, seq, 128), F32), VMEM),
-            (shaped((3, seq, 128)), VMEM),
-            (shaped((2, seq, 128)), VMEM),
-            (shaped((2, seq, 128), F32), VMEM),
-            (shaped((4, tokens, width)), VMEM),
-        ],
-        [pltpu.VMEM((seq, 128), BF16)] * 2,
-    )
     ctx_scratch = [
         pltpu.VMEM((2, tokens, width), BF16),
         pltpu.VMEM((2, tokens, width), BF16),
         pltpu.VMEM((tokens, width), BF16),
         pltpu.VMEM((tokens, width), BF16),
     ]
-    gu_w, dn_w, dout_all, middle, mid_all = call(
-        feed_gather_kernel,
+    table = pltpu.VMEM((seq, 128), F32)
+    (
+        qkv_w, out_w, gains, normed, qkv_raw, qkv_low, att_low, log_sums,
+        gu_w, dn_w, dout_all, middle, mid_all,
+    ) = call(
+        forward_kernel,
+        [(a, HBM) for a in (qkv_s, out_weight, gain_s, source, gu_s, dn_s, d_out, cos, sin)]
+        + [(head_gain, VMEM), (key_bias, VMEM)],
         [
-            (gu_s, HBM),
-            (dn_s, HBM),
-            (d_out, HBM),
-            (part, HBM),
-            (source, VMEM),
-            (ffn_norm, VMEM),
-        ],
-        [
+            (shaped((8, rows, 384)), HBM),
+            (shaped((2, out_weight.shape[0], width)), HBM),
+            (shaped((8, width), F32), VMEM),
+            (shaped((seq, width)), HBM),
+            (shaped((3, seq, 128), F32), HBM),
+            (shaped((3, seq, 128)), HBM),
+            (shaped((2, seq, 128)), HBM),
+            (shaped((2, seq, 128), F32), HBM),
             (shaped((8, rows, width)), HBM),
             (shaped((8, down_rows, width)), HBM),
             (shaped((4, tokens, width)), HBM),
             (shaped((tokens, width), F32), VMEM),
             (shaped((4, tokens, width)), HBM),
         ],
-        ctx_scratch + [pltpu.VMEM((tokens, width), BF16)],
-        sems=(80, 80, 16),
-        number=1,
-    )
+        [
+            table,
+            table,
+            pltpu.VMEM((8, 8, rows), F32),
+            pltpu.VMEM((8, rows, 384), BF16),
+            pltpu.VMEM((2, out_weight.shape[0], width), BF16),
+            pltpu.VMEM((4, tokens, width), BF16),
+            pltpu.VMEM((seq, width), BF16),
+            pltpu.VMEM((3, seq, 128), F32),
+            pltpu.VMEM((3, seq, 128), BF16),
+            pltpu.VMEM((2, seq, 128), BF16),
+            pltpu.VMEM((2, seq, 128), F32),
+            pltpu.VMEM((4, tokens, width), BF16),
+            pltpu.VMEM((seq, 128), BF16),
+            pltpu.VMEM((seq, 128), BF16),
+            pltpu.VMEM((2, tokens, width), BF16),
+            pltpu.VMEM((tokens, width), BF16),
+            pltpu.VMEM((tokens, width), BF16),
+            pltpu.VMEM((tokens, width), BF16),
+        ],
+        sems=(90, 100, 24),
+        number=0,
+    )
+    attn_norm, ffn_norm = gains[0:1], gains[1:2]
+    qkv_w = qkv_w.reshape(width, 384)
+    tables = [(cos, VMEM), (sin, VMEM), (head_gain, VMEM), (key_bias, VMEM)]
     hidden_units = units // 4
     gu_full = gu_w.reshape(width, parts * hidden_units)
     dn_full = dn_w.reshape(hidden_units, width)

time: 676 us -> 648 us (0.959)
  the two profiles are of different devices: /device:TPU:13 before, /device:TPU:3 now
where the time goes in v2:
time: 648 us; the launch traced here: 640 us
  Pallas kernels  499 us (77%)
  matrix products  65 us (10%)
  local copies, waits for them, and re-layouts  61.1 us (9%)
  other arithmetic  12.7 us (2%)
    pallas_call x4, Pallas kernels, call(): pl.pallas_call(kernel, out_shape=tuple((shape for shape, _ in outs)), in_...  499 us
    convert_element_type x2, local copies, waits for them, and re-layouts, split_heads(): gate_up_grad = jnp.transpose(gu_all.reshape(4, rows, parts, 8, units // 3...  23.3 us
    dot_general x2, matrix products, contract_cols(): lax.dot_general(left, right, (((1,), (1,)), ((), ())), preferred_element_...  23.1 us
    dot_general x2, matrix products, contract_rows(): lax.dot_general(left, right, (((0,), (0,)), ((), ())), preferred_element_...  18.6 us
    dot_general x1, matrix products, split_heads(): projected = jnp.dot(mid_full, gu_full, preferred_element_type=F32)  14.8 us

profile of v2, /device:TPU:3, one launch (start us, length us, event | category | flops | bytes accessed | tf_op | source)
XLA Modules:
  0.0 640.0 jit_solution(15763542059235806687)
XLA Ops:
  0.7 1.1 constant_dynamic-slice_fusion.4
  1.8 0.9 constant_dynamic-slice_fusion.5
  2.7 0.8 pad_maximum_fusion.3.qkv_s
  3.5 0.8 constant_dynamic-slice_fusion.2.dn_s
  4.3 7.8 %reshape.109 = bf16[256,2,8,4,128]{4,3,2,1,0:T(4,128)(2,1)} reshape(bf16[256,2,4096]{2,1,0:T(2,128)(2,1)} %param.17) | data formatting | bytes 8388608 | tf_op jit(solution)/shard_map/reshape | solution.py:1158
  12.2 8.4 %dynamic-slice_reduce_fusion = bf16[256,2,8,128]{3,2,1,0:T(8,128)(2,1)S(1)} fusion(bf16[256,2,8,4,128]{4,3,2,1,0:T(4,128)(2,1)} %reshape.109, s32[]{:T(128)S(6)} %select_n.31), kind=kLoop, calls=%fused_computation.12 | loop fusion | bytes 2097156 | tf_op jit(solution)/shard_map/jit(dynamic_index_in_dim)/dynamic_slice | solution.py:1157
  20.7 1.2 copy.59
  22.6 1.2 fusion.dout_s
  25.3 1.0 copy.40.cos_h.cos
  26.4 1.0 copy.41.sin_h.sin
  28.2 184.9 %shard_map.187 = (bf16[8,256,384]{2,1,0:T(8,128)(2,1)}, bf16[2,128,2048]{2,1,0:T(8,128)(2,1)}, f32[8,2048]{1,0:T(8,128)}, bf16[1024,2048]{1,0:T(8,128)(2,1)}, f3...) custom-call(bf16[256,384]{1,0:T(8,128)(2,1)} %pad_maximum_fusion.3.q, ...), custom_call_target="tpu_custom_call" | custom-call | tf_op jit(solution)/shard_map/pallas_call | solution.py:1114
  213.0 14.8 %fusion.9 = f32[1024,2048]{0,1:T(8,128)} fusion(bf16[1024,2048]{1,0:T(8,128)(2,1)} %bitcast.91, bf16[2048,2048]{1,0:T(8,128)(2,1)} %bitcast.89), kind=kOutput, calls=%fused_computation.40 | convolution fusion | flops 8589934592 | bytes 20971520 | tf_op jit(solution)/shard_map/dot_general | solution.py:1237
  227.8 11.4 %multiply_convert_fusion.2 = (bf16[1024,1024]{0,1:T(8,128)(2,1)S(1)}, bf16[1024,1024]{0,1:T(8,128)(2,1)}, bf16[1024,1024]{0,1:T(8,128)(2,1)S(1)}) fusion(f32[1024,2048]{0,1:T(8,128)} %fusion.9, bf16[1024,2048]{1,0:T(8,128)(2,1)S(1)} %bitcast.93, bf16[1024,2048]{1,0:T(8,128)(2,1)} %bitcast.95), kind=kOutput, calls=%fused_computation.4 | convolution fusion | flops 4311744512 | bytes 23068672 | tf_op jit(solution)/shard_map/dot_general | solution.py:75
  239.2 11.7 %convolution_convert_fusion.1 = bf16[1024,2048]{1,0:T(8,128)(2,1)} fusion(bf16[2048,2048]{1,0:T(8,128)(2,1)S(1)} %bitcast.90, bf16[1024,1024]{0,1:T(8,128)(2,1)} %get-tuple-element.64, bf16[1024,1024]{0,1:T(8,128)(2,1)S(1)} %get-tuple-element.63), kind=kOutput, calls=%fused_computation.6 | convolution fusion | flops 8600420352 | bytes 16777216 | tf_op jit(solution)/shard_map/dot_general | solution.py:75
  250.9 8.5 %convolution_convert_fusion.2 = bf16[1024,2048]{1,0:T(8,128)(2,1)} fusion(bf16[1024,1024]{0,1:T(8,128)(2,1)S(1)} %get-tuple-element.65, bf16[1024,2048]{1,0:T(8,128)(2,1)} %bitcast.96), kind=kOutput, calls=%fused_computation.7 | convolution fusion | flops 4297064448 | bytes 10485760 | tf_op jit(solution)/shard_map/dot_general | solution.py:1241
  259.4 6.1 convolution_convert_fusion.3
  265.5 12.5 %convolution_convert_fusion = bf16[2048,2048]{1,0:T(8,128)(2,1)} fusion(bf16[1024,2048]{1,0:T(8,128)(2,1)S(1)} %bitcast.92, bf16[1024,1024]{0,1:T(8,128)(2,1)S(1)} %copy-done.15, bf16[1024,1024]{0,1:T(8,128)(2,1)S(1)} %get-tuple-element.63), kind=kOutput, calls=%fused_computation | convolution fusion | flops 8602517504 | bytes 16777216 | tf_op jit(solution)/shard_map/dot_general | solution.py:69
  278.0 1.5 fusion.7
  280.2 200.8 %shard_map.188 = (bf16[4,256,2048]{2,1,0:T(8,128)(2,1)}, bf16[4,128,2048]{2,1,0:T(8,128)(2,1)}, bf16[256,2048]{1,0:T(8,128)(2,1)}, f32[256,2048]{1,0:T(8,128)}, ...) custom-call(bf16[4,2,256,2048]{3,2,1,0:T(8,128)(2,1)} %bitcast.68, bf16[4,2,128,2048]{3,2,1,0:T(8,128)(2,1)} %bitcast.75, ...), custom_call_target="tpu_custom_call" | custom-call | tf_op jit(solution)/shard_map/pallas_call | solution.py:1114
  481.0 29.3 %shard_map.189 = (bf16[4,256,2048]{2,1,0:T(8,128)(2,1)}, bf16[8,384,256]{2,1,0:T(8,128)(2,1)}, bf16[2,128,2048]{2,1,0:T(8,128)(2,1)}, f32[8,128]{1,0:T(8,128)}) custom-call(bf16[1024,2048]{1,0:T(8,128)(2,1)} %bitcast.70, bf16[2048,384]{1,0:T(8,128)(2,1)} %bitcast.81, bf16[2,128,2048]{2,1,0:T(8,128)(2,1)} %get-tuple-element.45.out_w, ...), custom_call_target="tpu_custom_call" | custom-call | tf_op jit(solution)/shard_map/pallas_call | solution.py:1114
  510.4 0.9 fusion.8
  511.9 84.4 %shard_map.190 = (bf16[4,384,256]{2,1,0:T(8,128)(2,1)}, bf16[128,2048]{1,0:T(8,128)(2,1)}, bf16[256,2048]{1,0:T(8,128)(2,1)}, f32[8,2048]{1,0:T(8,128)}) custom-call(bf16[4,2,384,256]{3,2,1,0:T(8,128)(2,1)} %bitcast.82, bf16[2,128,2048]{2,1,0:T(8,128)(2,1)} %get-tuple-element.52.out_g, bf16[4,256,2048]{2,1,0:T(8,128)(2,1)} %get-tuple-element.53.dnorm_part, ...), custom_call_target="tpu_custom_call" | custom-call | tf_op jit(solution)/shard_map/pallas_call | solution.py:1114
  596.3 0.9 fusion.6
  597.8 6.9 %copy.57 = f32[128,8,16,128]{3,2,1,0:T(8,128)} copy(bf16[128,8,16,128]{3,1,2,0:T(8,128)(2,1)} %bitcast.69) | data formatting | bytes 12582912
  604.7 12.0 %copy.50 = f32[256,2,8,4,128]{4,3,2,1,0:T(4,128)} copy(f32[256,2,8,4,128]{4,2,1,0,3:T(8,128)} %bitcast.67) | data formatting | bytes 16777216 | tf_op jit(solution)/shard_map/convert_element_type | solution.py:1369
  616.7 11.3 %reshape.128 = f32[256,2,4096]{2,1,0:T(2,128)} reshape(f32[256,2,8,4,128]{4,3,2,1,0:T(4,128)} %copy.50) | data formatting | bytes 16777216 | tf_op jit(solution)/shard_map/convert_element_type | solution.py:1369
  628.5 1.3 maximum_convert_fusion
  629.8 2.2 convert_element_type.91
  632.0 0.7 slice_reduce_fusion
  633.4 4.3 bitcast_convert_fusion
  637.7 1.0 copy.63
  638.6 1.0 copy.64
  (59 shorter events, 5.4 us)
Async XLA Ops:
  0.6 2.9 copy-start
  12.2 10.4 %copy-start.4 = (bf16[1,256,2048]{2,1,0:T(8,128)(2,1)S(1)}, bf16[1,256,2048]{2,1,0:T(8,128)(2,1)}, u32[]{:S(2)}) copy-start(bf16[1,256,2048]{2,1,0:T(8,128)(2,1)} %param.13) | copy-start | bytes 3145732
  12.2 12.2 %copy-start.8 = (bf16[2,64]{1,0:T(2,128)(2,1)S(1)}, bf16[2,64]{1,0:T(2,128)(2,1)}, u32[]{:S(2)}) copy-start(bf16[2,64]{1,0:T(2,128)(2,1)} %param.21) | copy-start | bytes 772
  12.2 13.1 %copy-start.7 = (f32[1024,32]{0,1:T(8,128)S(1)}, f32[1024,32]{0,1:T(8,128)}, u32[]{:S(2)}) copy-start(f32[1024,32]{0,1:T(8,128)} %constant.55.clone) | copy-start | bytes 393220
  12.2 14.1 %copy-start.6 = (f32[1024,64]{0,1:T(8,128)S(1)}, f32[1024,64]{0,1:T(8,128)}, u32[]{:S(2)}) copy-start(f32[1024,64]{0,1:T(8,128)} %constant.63) | copy-start | bytes 786436
  20.6 6.7 %copy-start.13 = (bf16[256]{0:T(256)(128)(2,1)S(1)}, bf16[256]{0:T(256)(128)(2,1)}, u32[]{:S(2)}) copy-start(bf16[256]{0:T(256)(128)(2,1)} %param.19) | copy-start | bytes 1540
  20.6 6.7 %copy-start.14 = (bf16[256]{0:T(256)(128)(2,1)S(1)}, bf16[256]{0:T(256)(128)(2,1)}, u32[]{:S(2)}) copy-start(bf16[256]{0:T(256)(128)(2,1)} %param.20) | copy-start | bytes 1540
  213.0 14.8 %copy-start.11 = (bf16[4,256,2048]{2,1,0:T(8,128)(2,1)S(1)}, bf16[4,256,2048]{2,1,0:T(8,128)(2,1)}, u32[]{:S(2)}) copy-start(bf16[4,256,2048]{2,1,0:T(8,128)(2,1)} %get-tuple-element.37) | copy-start | bytes 12582916
  227.8 11.4 %copy-start.9 = (bf16[8,256,2048]{2,1,0:T(8,128)(2,1)S(1)}, bf16[8,256,2048]{2,1,0:T(8,128)(2,1)}, u32[]{:S(2)}) copy-start(bf16[8,256,2048]{2,1,0:T(8,128)(2,1)} %get-tuple-element.39) | copy-start | bytes 25165828
  250.9 8.5 %copy-start.12 = (bf16[4,256,2048]{2,1,0:T(8,128)(2,1)S(1)}, bf16[4,256,2048]{2,1,0:T(8,128)(2,1)}, u32[]{:S(2)}) copy-start(bf16[4,256,2048]{2,1,0:T(8,128)(2,1)} %get-tuple-element.37) | copy-start | bytes 12582916
  259.4 6.1 copy-start.10
  259.4 6.1 copy-start.15
  616.7 11.3 %copy-start.5 = (bf16[4,384,256]{2,1,0:T(8,128)(2,1)S(1)}, bf16[4,384,256]{2,1,0:T(8,128)(2,1)}, u32[]{:S(2)}) copy-start(bf16[4,384,256]{2,1,0:T(8,128)(2,1)} %get-tuple-element.58) | copy-start | bytes 2359300
  629.8 7.8 %copy-start.2 = (bf16[256,2048]{1,0:T(8,128)(2,1)S(1)}, bf16[256,2048]{1,0:T(8,128)(2,1)}, u32[]{:S(2)}) copy-start(bf16[256,2048]{1,0:T(8,128)(2,1)} %get-tuple-element.42) | copy-start | bytes 3145732
  633.4 6.2 copy-start.1
  633.4 5.3 copy-start.3

commit v3 on v2

--- a/solution.py
+++ b/solution.py
@@ -323,7 +323,7 @@
 MESH = pl.DeviceIdType.MESH
 F32 = jnp.float32
 BF16 = jnp.bfloat16
-VMEM_BYTES = 56 << 20
+VMEM_BYTES = 60 << 20
 HBM = pl.BlockSpec(memory_space=pl.ANY)
 VMEM = pl.BlockSpec(memory_space=pltpu.VMEM)
 
@@ -345,6 +345,9 @@
         self.y_dev = (self.f, self.c_y)
         self.diag_dev = (self.f, self.c_diag)
 
+    def rank(self, source, target):
+        return jnp.where(source > target, source - 1, source)
+
     def z_dev(self, z):
         return (z * 2 + self.x, self.c)
 
@@ -386,6 +389,12 @@
         made = self.copy(src, dst, slot, device)
         made.start()
         self.open.append(made)
+        return made
+
+    def settle(self, sends):
+        for made in sends:
+            made.wait_send()
+            self.open = [one for one in self.open if one is not made]
 
     def arrive(self, ref, slot):
         pltpu.make_async_remote_copy(
@@ -440,70 +449,81 @@
                 self.links.arrive(block, self.x_slot + 4 * k + z)
 
 
-def reduce_plane(links, place, chunks, own, from_x, to_z, from_z, total, done, ahead=2):
-    count = len(chunks)
-    x_slot, z_slot = links.slots(count), links.slots(4 * count)
-    loads = {}
-
-    def begin(k):
-        links.send(chunks[k](place.xo), from_x.at[k], x_slot + k, place.x_dev)
-        loads[k] = links.local(chunks[k](place.x), own.at[k])
-
-    def middle(k):
-        links.arrive(from_x.at[k], x_slot + k)
-        loads[k].wait()
+class ReducePlane:
+    def __init__(self, links, place, chunks, from_x, from_z, own=None):
+        self.links, self.place, self.chunks = links, place, chunks
+        self.from_x, self.from_z, self.own = from_x, from_z, own
+        self.x_slot, self.z_slot = links.slots(len(chunks)), links.slots(3 * len(chunks))
+        self.loads, self.z_sends = {}, {}
+
+    def send_x(self, k):
+        place = self.place
+        self.links.send(self.chunks[k](place.xo), self.from_x.at[k], self.x_slot + k, place.x_dev)
+
+    def load(self, k):
+        slots = self.own.shape[0]
+        for made in self.z_sends.pop(k - slots, []):
+            made.wait_send()
+        self.loads[k] = self.links.local(self.chunks[k](self.place.x), self.own.at[k % slots])
+
+    def mine(self, k):
+        if self.own is None:
+            return self.chunks[k](self.place.x)
+        return self.own.at[k % self.own.shape[0]]
+
+    def middle(self, k):
+        place = self.place
+        self.links.arrive(self.from_x.at[k], self.x_slot + k)
+        if k in self.loads:
+            self.loads[k].wait()
+        mine = self.mine(k)
+        self.z_sends[k] = []
         for other in place.others:
-            pair = own[k, other].astype(F32) + from_x[k, other].astype(F32)
-            to_z[k, other] = pair.astype(BF16)
-            links.send(
-                to_z.at[k, other],
-                from_z.at[k, place.z],
-                z_slot + 4 * k + place.z,
+            mine[other] = (mine[other].astype(F32) + self.from_x[k, other].astype(F32)).astype(BF16)
+            rank = place.rank(place.z, other)
+            made = self.links.copy(
+                mine.at[other],
+                self.from_z.at[k, rank],
+                self.z_slot + 3 * k + rank,
                 place.z_dev(other),
             )
-
-    def end(k):
-        sums = own[k, place.z].astype(F32) + from_x[k, place.z].astype(F32)
-        for other in place.others:
-            links.arrive(from_z.at[k, other], z_slot + 4 * k + other)
-            sums += from_z[k, other].astype(F32)
-        total[k] = sums.astype(BF16)
-        done(k)
-
-    for k in range(min(ahead, count)):
-        begin(k)
-    yield
-    for k in range(count + 1):
-        if k < count:
-            middle(k)
-            if k + ahead < count:
-                begin(k + ahead)
-            yield
-        if k >= 1:
-            end(k - 1)
-            yield
+            made.start()
+            self.z_sends[k].append(made)
+
+    def end(self, k):
+        place = self.place
+        mine = self.mine(k)
+        sums = mine[place.z].astype(F32) + self.from_x[k, place.z].astype(F32)
+        for rank in range(3):
+            self.links.arrive(self.from_z.at[k, rank], self.z_slot + 3 * k + rank)
+            sums += self.from_z[k, rank].astype(F32)
+        total = self.from_x.at[k, place.z]
+        total[...] = sums.astype(BF16)
+        return total
+
+    def finish(self):
+        for sends in self.z_sends.values():
+            for made in sends:
+                made.wait_send()
 
 
 class SpreadCtx:
     def __init__(self, links, place, out, parts):
         self.links, self.place, self.out, self.parts = links, place, out, parts
         self.slot = links.slots(3 * len(parts))
-
-    def begin(self, k, src, y_too=True):
+        self.sends = []
+
+    def begin(self, k, src):
         place, rows = self.place, self.parts[k]
-        self.links.send(src, self.out.at[place.c, rows], self.slot + 3 * k, place.core_dev)
-        if y_too:
-            self.begin_y(k, src)
-
-    def begin_y(self, k, src):
-        place, rows = self.place, self.parts[k]
-        self.links.send(src, self.out.at[place.c, rows], self.slot + 3 * k + 1, place.y_dev)
+        out = self.out.at[place.c, rows]
+        self.sends.append(self.links.send(src, out, self.slot + 3 * k + 1, place.y_dev))
+        self.sends.append(self.links.send(src, out, self.slot + 3 * k, place.core_dev))
 
     def forward(self, k):
         place = self.place
         block = self.out.at[place.c_y, self.parts[k]]
         self.links.arrive(block, self.slot + 3 * k + 1)
-        self.links.send(block, block, self.slot + 3 * k + 2, place.core_dev)
+        self.sends.append(self.links.send(block, block, self.slot + 3 * k + 2, place.core_dev))
 
     def end(self):
         place = self.place
@@ -517,7 +537,7 @@
         self.links, self.place, self.part, self.parts = links, place, part, parts
         self.own, self.from_core, self.to_y, self.from_y = own, from_core, to_y, from_y
         self.slot = links.slots(3 * len(parts))
-        self.loads = {}
+        self.loads, self.sends = {}, []
 
     def begin(self):
         place = self.place
@@ -548,9 +568,10 @@
     def cross(self, k):
         rows = self.parts[k]
         self.to_y[rows] = self.pair(0, k).astype(BF16)
-        self.links.send(
+        made = self.links.send(
             self.to_y.at[rows], self.from_y.at[rows], self.slot + 3 * k + 2, self.place.y_dev
         )
+        self.sends.append(made)
 
     def total(self, k):
         rows = self.parts[k]
@@ -567,216 +588,6 @@
     return lax.rsqrt(jnp.mean(values * values, axis=-1, keepdims=True) + EPSILON)
 
 
-def feed_reduce_kernel(
-    gu_g, dn_g, ffn_part, dmid_part, middle, dout_s, keep, gain,
-    gu_all, dn_all, layer_out, d_middle, gain_part, branch_all,
-    own, from_x, to_z, from_z, total,
-    own1, from_core1, to_y1, from_y1, own2, from_core2, to_y2, from_y2, branch,
-    send_sems, recv_sems, local_sems,
-):
-    place = Place()
-    links = Links(place, send_sems, recv_sems, local_sems)
-    place.meet(place.neighbours())
-    step = from_x.shape[2]
-    chunks, where = [], []
-    for grad, out in ((dn_g, dn_all), (gu_g, gu_all)):
-        for first in range(0, grad.shape[2], step):
-            rows = pl.ds(first, step)
-            chunks.append(lambda x, grad=grad, rows=rows: grad.at[:, x, rows])
-            where.append((out, rows))
-    outs = [SpreadCtx(links, place, out, [rows]) for out, rows in where]
-    kept = []
-
-    def done(k):
-        out, rows = where[k]
-        outs[k].begin(0, total.at[k])
-        kept.append(links.local(total.at[k], out.at[place.c, rows]))
-
-    plane = reduce_plane(links, place, chunks, own, from_x, to_z, from_z, total, done)
-    next(plane)
-    parts = halves(middle.shape[0])
-    dmid = ReduceCtx(links, place, dmid_part, parts, own1, from_core1, to_y1, from_y1)
-    dmid.begin()
-    for k in range(2):
-        dmid.cross(k)
-    next(plane)
-    spread = SpreadCtx(links, place, branch_all, parts)
-    gain_sum = None
-    for k, rows in enumerate(parts):
-        d_norm = dmid.total(k)
-        value = middle[rows]
-        factor = row_factor(value)
-        term = jnp.sum(d_norm * value * factor, axis=0, keepdims=True)
-        gain_sum = term if gain_sum is None else gain_sum + term
-        scaled = d_norm * gain[...]
-        inner = jnp.mean(scaled * value, axis=-1, keepdims=True)
-        grad = dout_s[rows].astype(F32) + factor * scaled - value * (factor * factor * factor * inner)
-        d_middle[rows] = grad
-        branch[rows] = grad.astype(BF16)
-        spread.begin(k, branch.at[rows])
-        kept.append(links.local(branch.at[rows], branch_all.at[place.c, rows]))
-    gain_part[...] = gain_sum
-    next(plane)
-    ffn = ReduceCtx(links, place, ffn_part, parts, own2, from_core2, to_y2, from_y2)
-    ffn.begin()
-    for k in range(2):
-        spread.forward(k)
-    for k in range(2):
-        ffn.cross(k)
-    next(plane)
-    next(plane)
-    for k, rows in enumerate(parts):
-        layer_out[rows] = (keep[rows] * (middle[rows] + ffn.total(k))).astype(BF16)
-    forwarded = 0
-    for step_at, _ in enumerate(plane):
-        if step_at % 2 == 1:
-            outs[forwarded].forward(0)
-            forwarded += 1
-    for k in range(forwarded, len(outs)):
-        outs[k].forward(0)
-    spread.end()
-    for out in outs:
-        out.end()
-    for made in kept:
-        made.wait()
-    links.finish()
-
-
-def last_kernel(
-    qkv_g, out_g, dnorm_part, x_s, d_middle, gain, ffn_part, qk_part,
-    qkv_all, out_all, input_grad, stats,
-    own, from_x, to_z, from_z, total,
-    own1, from_core1, to_y1, from_y1,
-    out_own, out_x, out_low, out_z,
-    mine, plane_stats, ctx_stats, send_sems, recv_sems, local_sems,
-):
-    place = Place()
-    links = Links(place, send_sems, recv_sems, local_sems)
-    fellows = [lax.rem(place.f + d, 8) for d in range(1, 8)]
-    place.meet(
-        [(f, place.c) for f in fellows] + [place.core_dev, place.y_dev, place.diag_dev]
-    )
-    step = from_x.shape[2]
-    chunks = []
-    for first in range(0, qkv_g.shape[2], step):
-        rows = pl.ds(first, step)
-        chunks.append(lambda x, rows=rows: qkv_g.at[:, x, rows])
-    outs = [
-        SpreadCtx(links, place, qkv_all, [pl.ds(k * step, step)]) for k in range(len(chunks))
-    ]
-    kept = []
-
-    def done(k):
-        outs[k].begin(0, total.at[k])
-        kept.append(links.local(total.at[k], qkv_all.at[place.c, pl.ds(k * step, step)]))
-
-    out_slot = links.slots(1)
-    links.send(out_g.at[place.xo], out_x, out_slot, place.x_dev)
-    out_load = links.local(out_g.at[place.x], out_own)
-    plane = reduce_plane(links, place, chunks, own, from_x, to_z, from_z, total, done)
-    next(plane)
-    parts = halves(x_s.shape[0])
-    dnorm = ReduceCtx(links, place, dnorm_part, parts, own1, from_core1, to_y1, from_y1)
-    dnorm.begin()
-    for k in range(2):
-        dnorm.cross(k)
-
-    links.arrive(out_x, out_slot)
-    out_load.wait()
-    root_slot, final_slot = links.slots(4), links.slots(1)
-    holds = place.z == place.c
-    pair = out_own[...].astype(F32) + out_x[...].astype(F32)
-    out_low[...] = pair.astype(BF16)
-    to_root = links.copy(
-        out_low, out_z.at[place.z], root_slot + place.z, (place.c * 2 + place.x, place.c)
-    )
-
-    @pl.when(jnp.logical_not(holds))
-    def _():
-        to_root.start()
-
-    next(plane)
-    gain_sum = None
-    for k, rows in enumerate(parts):
-        d_norm = dnorm.total(k)
-        value = x_s[rows].astype(F32)
-        factor = row_factor(value)
-        term = jnp.sum(d_norm * value * factor, axis=0, keepdims=True)
-        gain_sum = term if gain_sum is None else gain_sum + term
-        scaled = d_norm * gain[...]
-        inner = jnp.mean(scaled * value, axis=-1, keepdims=True)
-        grad = d_middle[rows] + factor * scaled - value * (factor * factor * factor * inner)
-        input_grad[rows] = grad.astype(BF16)
-    mine[0:1] = gain_sum
-    mine[1:2] = ffn_part[...]
-    mine[2:3] = qk_part[...]
-    mine[3:8] = jnp.zeros((5, mine.shape[1]), F32)
-    plane_slot, ctx_slot = links.slots(8), links.slots(4)
-    for f in fellows:
-        links.send(mine, plane_stats.at[place.f], plane_slot + place.f, (f, place.c))
-    plane_stats[place.f] = mine[...]
-
-    final = [
-        links.copy(out_all, out_all, final_slot, device)
-        for device in (place.core_dev, place.y_dev)
-    ]
-    onward = links.copy(out_all, out_all, final_slot, place.core_dev)
-
-    @pl.when(holds)
-    def _():
-        sums = out_own[...].astype(F32) + out_x[...].astype(F32)
-        for other in place.others:
-            links.arrive(out_z.at[other], root_slot + other)
-            sums += out_z[other].astype(F32)
-        out_all[...] = sums.astype(BF16)
-        for made in final:
-            made.start()
-
-    for f in fellows:
-        links.arrive(plane_stats.at[f], plane_slot + f)
-    sums = plane_stats[0]
-    for f in range(1, 8):
-        sums += plane_stats[f]
-    ctx_stats[place.c] = sums
-    for device in (place.core_dev, place.y_dev, place.diag_dev):
-        links.send(ctx_stats.at[place.c], ctx_stats.at[place.c], ctx_slot + place.c, device)
-    for _ in plane:
-        pass
-    for out in outs:
-        out.forward(0)
-    relays = place.c_y == place.z
-
-    @pl.when(jnp.logical_not(holds))
-    def _():
-        links.arrive(out_all, final_slot)
-
-    @pl.when(relays)
-    def _():
-        onward.start()
-
-    for c in (place.c_core, place.c_y, place.c_diag):
-        links.arrive(ctx_stats.at[c], ctx_slot + c)
-    stats[...] = ((ctx_stats[0] + ctx_stats[1]) + ctx_stats[2]) + ctx_stats[3]
-    for out in outs:
-        out.end()
-    for made in kept:
-        made.wait()
-    links.finish()
-
-    @pl.when(jnp.logical_not(holds))
-    def _():
-        to_root.wait_send()
-
-    @pl.when(relays)
-    def _():
-        onward.wait_send()
-
-    @pl.when(holds)
-    def _():
-        for made in final:
-            made.wait_send()
-
-
 def low_half(shape):
     return lax.rem(lax.broadcasted_iota(jnp.int32, shape, len(shape) - 1), 128) < 64
 
@@ -803,6 +614,7 @@
 
 
 BLOCK = 256
+SHORT = 128
 
 
 def attention_scores(query, keys, key_bias, first, span):
@@ -815,11 +627,11 @@
 
 
 def forward_kernel(
-    qkv_s, out_s, gain_s, x_s, gu_s, dn_s, dout_s, cos_h, sin_h, head_gain, key_bias,
+    qkv_s, out_s, gain_s, x_s, gate_up, dn_s, dout_s, cos_h, sin_h, head_gain, key_bias,
     qkv_wh, out_wh, gains, normed_h, qkv_raw_h, qkv_low_h, att_low_h, log_sums_h,
     gu_w, dn_w, dout_all, middle, mid_all,
     cos, sin, gain_blocks, qkv_w, out_w, x_all, normed, qkv_raw, qkv_low, att_low, log_sums,
-    part, keys, values, from_core, to_y, from_y, mid_low, send_sems, recv_sems, local_sems,
+    part, keys, values, from_core, to_y, from_y, mid_low, gu_pairs, gu_rows, gu_s, send_sems, recv_sems, local_sems,
 ):
     place = Place()
     links = Links(place, send_sems, recv_sems, local_sems)
@@ -829,6 +641,10 @@
     qkv_plane = SpreadPlane(links, place, [(qkv_s, lambda f: qkv_w.at[f])])
     qkv_plane.begin_z()
     qkv_plane.begin_x(0)
+    picks = []
+    for f in range(8):
+        start = pl.multiple_of(512 * f + 128 * place.c, 128)
+        picks.append(links.local(gate_up.at[:, :, pl.ds(start, 128)], gu_pairs.at[f]))
     tokens = x_s.shape[0]
     parts = halves(tokens)
     x_spread = SpreadCtx(links, place, x_all, parts)
@@ -851,7 +667,7 @@
         links.copy(out_s, out_w.at[place.x], root_slot, place.z_dev(other))
         for other in place.others
     ]
-    side = links.copy(out_s, out_w.at[place.x], side_slot, place.x_dev)
+    sideways = links.copy(out_s, out_w.at[place.x], side_slot, place.x_dev)
     onward = links.copy(out_w.at[place.x], out_w.at[place.x], side_slot, place.x_dev)
     own = pltpu.make_async_copy(out_s, out_w.at[place.x], local_sems.at[links.locals])
     links.locals += 1
@@ -860,9 +676,17 @@
     def _():
         for made in down:
             made.start()
-        side.start()
+        sideways.start()
         own.start()
 
+    rows = gu_s.shape[0]
+    for f in range(8):
+        picks[f].wait()
+        gu_rows[...] = gu_pairs.at[f].reshape(2 * rows, 128)[...].astype(F32)
+        for side in range(2):
+            first = 1024 * side + 128 * f
+            picked = gu_rows[pl.ds(side, rows, stride=2), :]
+            gu_s[:, first : first + 128] = picked.astype(BF16)
     step = 64
     chunks = []
     for src, dst in ((dn_s, dn_w), (gu_s, gu_w)):
@@ -999,7 +823,7 @@
     def _():
         for made in down:
             made.wait_send()
-        side.wait_send()
+        sideways.wait_send()
 
     @pl.when(jnp.logical_not(holds))
     def _():
@@ -1010,16 +834,100 @@
 TN = (((0,), (0,)), ((), ()))
 
 
-def attention_back_kernel(
-    branch, qkv_w, out_w, cos, sin, head_gain, key_bias,
-    normed, qkv_raw, qkv_low, att_low, log_sums,
-    part, qkv_g, out_g, gain_g, keys, values, d_att, d_low, d_keys, d_values,
+def norm_back(d_norm, value, gain):
+    factor = row_factor(value)
+    gain_sum = jnp.sum(d_norm * value * factor, axis=0, keepdims=True)
+    scaled = d_norm * gain
+    inner = jnp.mean(scaled * value, axis=-1, keepdims=True)
+    return factor * scaled - value * (factor * factor * factor * inner), gain_sum
+
+
+def backward_kernel(
+    gu_g, dn_g, ffn_part, dmid_part, middle_h, dout_h, x_h, keep, gains,
+    cos_h, sin_h, head_gain, key_bias,
+    normed_h, qkv_raw_h, qkv_low_h, att_low_h, log_sums_h, qkv_wh, out_wh,
+    gu_all, dn_all, layer_out, qkv_all, out_all, input_grad, stats,
+    own, from_x, from_z,
+    ctx_own, from_core1, to_y1, from_y1, from_core2, to_y2, from_y2,
+    middle, dout_s, d_middle, branch_all, part,
+    cos, sin, qkv_raw, qkv_low, att_low, log_sums, qkv_w, out_w,
+    keys, values, d_att, d_low, d_keys, d_values, gain_g,
+    qkv_g, qkv_x, qkv_z, out_g, out_x, out_z,
+    mine, plane_stats, ctx_stats, free, send_sems, recv_sems, local_sems,
 ):
-    seq = branch.shape[0]
-    root = 1.0 / math.sqrt(HEAD_DIM)
+    place = Place()
+    links = Links(place, send_sems, recv_sems, local_sems)
+    fellows = [lax.rem(place.f + d, 8) for d in range(1, 8)]
+    place.meet(
+        [(f, place.c) for f in fellows] + [place.core_dev, place.y_dev, place.diag_dev]
+    )
+    step = from_x.shape[2]
+    chunks, where = [], []
+    for grad, out in ((dn_g, dn_all), (gu_g, gu_all)):
+        for first in range(0, grad.shape[2], step):
+            rows = pl.ds(first, step)
+            chunks.append(lambda x, grad=grad, rows=rows: grad.at[:, x, rows])
+            where.append((out, rows))
+    count = len(chunks)
+    plane = ReducePlane(links, place, chunks, from_x, from_z, own)
+    outs = [SpreadCtx(links, place, out, [rows]) for out, rows in where]
+    kept = []
+
+    def end(k):
+        total = plane.end(k)
+        if k + own.shape[0] < count:
+            plane.load(k + own.shape[0])
+        out, rows = where[k]
+        outs[k].begin(0, total)
+        kept.append(links.local(total, out.at[place.c, rows]))
+
+    tokens, width = middle.shape
+    parts = halves(tokens)
+    dmid = ReduceCtx(links, place, dmid_part, parts, ctx_own, from_core1, to_y1, from_y1)
+    dmid.begin()
+    for k in range(count):
+        plane.send_x(k)
+    early = [links.local(middle_h, middle), links.local(dout_h, dout_s)]
+    for k in range(own.shape[0]):
+        plane.load(k)
+    late = [
+        links.local(a, b)
+        for a, b in (
+            (out_wh, out_w), (qkv_low_h, qkv_low), (att_low_h, att_low), (log_sums_h, log_sums),
+            (cos_h, cos), (sin_h, sin), (qkv_raw_h, qkv_raw), (qkv_wh, qkv_w),
+        )
+    ]
+    for k in range(2):
+        dmid.cross(k)
+    for made in early:
+        made.wait()
     gain_g[...] = jnp.zeros_like(gain_g)
     d_keys[...] = jnp.zeros_like(d_keys)
     d_values[...] = jnp.zeros_like(d_values)
+    plane.middle(0)
+    branch = SpreadCtx(links, place, branch_all, parts)
+    ffn_gain = None
+    for k, rows in enumerate(parts):
+        grad, term = norm_back(dmid.total(k), middle[rows], gains[1:2])
+        ffn_gain = term if ffn_gain is None else ffn_gain + term
+        grad += dout_s[rows].astype(F32)
+        d_middle[rows] = grad
+        branch_all[place.c, rows] = grad.astype(BF16)
+        branch.begin(k, branch_all.at[place.c, rows])
+    ffn = ReduceCtx(links, place, ffn_part, parts, ctx_own, from_core2, to_y2, from_y2)
+    ffn.begin()
+    plane.middle(1)
+    for k in range(2):
+        branch.forward(k)
+    for k in range(2):
+        ffn.cross(k)
+    end(0)
+    branch.end()
+    for made in late:
+        made.wait()
+
+    root = 1.0 / math.sqrt(HEAD_DIM)
+    seq = 4 * tokens
 
     def prepare(index):
         rows = pl.ds(pl.multiple_of(index * BLOCK, BLOCK), BLOCK)
@@ -1030,10 +938,22 @@
         values[rows] = jnp.where(low, swapped, block).astype(BF16)
         for b in range(2):
             d_att[b, rows] = lax.dot_general(
-                branch[rows], out_w[b], NT, preferred_element_type=F32
+                branch_all[index], out_w[b], NT, preferred_element_type=F32
             ).astype(BF16)
 
+    x_load = links.local(x_h, dout_s)
     row_loop(seq // BLOCK, prepare)
+    for b in range(2):
+        left = att_low[b].T
+        for j in range(8):
+            columns = slice(256 * j, 256 * (j + 1))
+            right = branch_all[:, :, columns].reshape(seq, 256)
+            out_g[b, :, columns] = jnp.dot(left, right, preferred_element_type=F32).astype(BF16)
+    out_slot = links.slots(1)
+    links.send(out_g.at[place.xo], out_x, out_slot, place.x_dev)
+    links.settle(branch.sends)
+    normed_load = links.local(normed_h, branch_all)
+    plane.middle(2)
 
     def unturn(row, rows, grads, block):
         back = grads * cos[rows] + partner(grads * sin[rows])
@@ -1044,11 +964,8 @@
         return factor * scaled - block * (factor * factor * factor * inner), gain_term
 
     def heads(b):
-        out_g[b] = lax.dot_general(
-            att_low[b], branch[...], TN, preferred_element_type=F32
-        ).astype(BF16)
-        for i in range(seq // BLOCK):
-            rows, span = pl.ds(i * BLOCK, BLOCK), (i + 1) * BLOCK
+        for i in range(seq // SHORT):
+            rows, span = pl.ds(i * SHORT, SHORT), (i + 1) * SHORT
             query, d_out = qkv_low[b, rows], d_att[b, rows]
             logs = log_sums[b, rows]
             low = low_half(query.shape)
@@ -1056,7 +973,7 @@
             for half in range(2):
                 side = low if half == 0 else jnp.logical_not(low)
                 chosen, d_chosen = jnp.where(side, query, 0), jnp.where(side, d_out, 0)
-                scores = attention_scores(chosen, keys[:span], key_bias[0:1], i * BLOCK, span)
+                scores = attention_scores(chosen, keys[:span], key_bias[0:1], i * SHORT, span)
                 probs = jnp.exp(scores - logs[:, 64 * half : 64 * half + 1])
                 d_probs = lax.dot_general(
                     d_chosen, values[:span], NT, preferred_element_type=F32
@@ -1076,6 +993,8 @@
             gain_g[0:1] += gain_term
 
     row_loop(2, heads)
+    end(1)
+    plane.middle(3)
 
     def finish(index):
         rows = pl.ds(pl.multiple_of(index * BLOCK, BLOCK), BLOCK)
@@ -1087,18 +1006,175 @@
         d_block, gain_term = unturn(2, rows, grads, qkv_raw[2, rows])
         d_low[2, rows] = jnp.where(low, d_block, grads).astype(BF16)
         gain_g[1:2] += gain_term
-        sums = jnp.zeros((BLOCK, part.shape[2]), F32)
-        for b in range(3):
-            sums += lax.dot_general(
-                d_low[b, rows], qkv_w[:, 128 * b : 128 * (b + 1)], NT, preferred_element_type=F32
+        for j in range(4):
+            columns = slice(512 * j, 512 * (j + 1))
+            sums = jnp.zeros((BLOCK, 512), F32)
+            for b in range(3):
+                weight = qkv_w[columns, 128 * b : 128 * (b + 1)]
+                sums += lax.dot_general(d_low[b, rows], weight, NT, preferred_element_type=F32)
+            part[index, :, columns] = sums.astype(BF16)
+
+    row_loop(seq // BLOCK, finish)
+
+    for k, rows in enumerate(parts):
+        layer_out[rows] = (keep[rows] * (middle[rows] + ffn.total(k))).astype(BF16)
+    links.settle(ffn.sends)
+    for device in (place.core_dev, place.y_dev):
+        pl.semaphore_signal(free, inc=1, device_id=device, device_id_type=MESH)
+    pl.semaphore_wait(free, 2)
+    dnorm = ReduceCtx(links, place, part, parts, None, from_core2, to_y2, from_y2)
+    dnorm.begin()
+    normed_load.wait()
+    for b in range(3):
+        left = d_low[b].T
+        for f in range(8):
+            right = branch_all[:, :, 256 * f : 256 * (f + 1)].reshape(seq, 256)
+            qkv_g[f // 2, f % 2, 128 * b : 128 * (b + 1)] = jnp.dot(
+                left, right, preferred_element_type=F32
+            ).astype(BF16)
+    qkv_step = qkv_x.shape[2]
+    qkv_rows = [pl.ds(k * qkv_step, qkv_step) for k in range(qkv_x.shape[0])]
+    qkv_chunks = [lambda x, rows=rows: qkv_g.at[:, x, rows] for rows in qkv_rows]
+    qkv_plane = ReducePlane(links, place, qkv_chunks, qkv_x, qkv_z)
+    qkv_outs = [SpreadCtx(links, place, qkv_all, [rows]) for rows in qkv_rows]
+    for k in range(len(qkv_chunks)):
+        qkv_plane.send_x(k)
+    for k in range(2):
+        dnorm.cross(k)
+    end(2)
+    plane.middle(4)
+    outs[0].forward(0)
+    end(3)
+    plane.middle(5)
+    outs[1].forward(0)
+
+    attn_gain = None
+    x_load.wait()
+    for k, rows in enumerate(parts):
+        grad, term = norm_back(dnorm.total(k), dout_s[rows].astype(F32), gains[0:1])
+        attn_gain = term if attn_gain is None else attn_gain + term
+        input_grad[rows] = (d_middle[rows] + grad).astype(BF16)
+    mine[0:1] = attn_gain
+    mine[1:2] = ffn_gain
+    mine[2:8] = jnp.zeros((6, width), F32)
+    mine[2:3, 0:128] = gain_g[0:1]
+    mine[2:3, 128:256] = gain_g[1:2]
+    plane_slot, ctx_slot = links.slots(8), links.slots(4)
+    for f in fellows:
+        links.send(mine, plane_stats.at[place.f], plane_slot + place.f, (f, place.c))
+    plane_stats[place.f] = mine[...]
+
+    links.arrive(out_x, out_slot)
+    root_slot, final_slot = links.slots(3), links.slots(1)
+    holds = place.z == place.c
+    out_mine = out_g.at[place.x]
+    out_mine[...] = (out_mine[...].astype(F32) + out_x[...].astype(F32)).astype(BF16)
+    rank = place.rank(place.z, place.c)
+    to_root = links.copy(
+        out_mine,
+        out_z.at[lax.rem(rank, 3)],
+        root_slot + lax.rem(rank, 3),
+        (place.c * 2 + place.x, place.c),
+    )
+
+    @pl.when(jnp.logical_not(holds))
+    def _():
+        to_root.start()
+
+    for k in range(len(qkv_chunks)):
+        qkv_plane.middle(k)
+    for k in range(4, count):
+        end(k)
+    for k in range(2, 4):
+        outs[k].forward(0)
+    for f in fellows:
+        links.arrive(plane_stats.at[f], plane_slot + f)
+    sums = plane_stats[0]
+    for f in range(1, 8):
+        sums += plane_stats[f]
+    ctx_stats[place.c] = sums
+    for device in (place.core_dev, place.y_dev, place.diag_dev):
+        links.send(ctx_stats.at[place.c], ctx_stats.at[place.c], ctx_slot + place.c, device)
+
+    final = [
+        links.copy(out_all, out_all, final_slot, device)
+        for device in (place.core_dev, place.y_dev)
+    ]
+    onward = links.copy(out_all, out_all, final_slot, place.core_dev)
+
+    @pl.when(holds)
+    def _():
+        sums = out_mine[...].astype(F32)
+        for other in range(3):
+            links.arrive(out_z.at[other], root_slot + other)
+            sums += out_z[other].astype(F32)
+        out_all[...] = sums.astype(BF16)
+        for made in final:
+            made.start()
+
+    for k in range(len(qkv_chunks)):
+        total = qkv_plane.end(k)
+        qkv_outs[k].begin(0, total)
+        kept.append(links.local(total, qkv_all.at[place.c, qkv_rows[k]]))
+    for k in range(4, count):
+        outs[k].forward(0)
+    relays = place.c_y == place.z
+
+    @pl.when(jnp.logical_not(holds))
+    def _():
+        links.arrive(out_all, final_slot)
+
+    @pl.when(relays)
+    def _():
+        onward.start()
+
+    for c in (place.c_core, place.c_y, place.c_diag):
+        links.arrive(ctx_stats.at[c], ctx_slot + c)
+    stats[...] = ((ctx_stats[0] + ctx_stats[1]) + ctx_stats[2]) + ctx_stats[3]
+    for out in qkv_outs:
+        out.forward(0)
+    for out in outs + qkv_outs:
+        out.end()
+    for made in kept:
+        made.wait()
+    links.finish()
+    plane.finish()
+    qkv_plane.finish()
+
+    @pl.when(jnp.logical_not(holds))
+    def _():
+        to_root.wait_send()
+
+    @pl.when(relays)
+    def _():
+        onward.wait_send()
+
+    @pl.when(holds)
+    def _():
+        for made in final:
+            made.wait_send()
+
+
+def interleave_kernel(parts, out, pairs, sems):
+    rows = parts.shape[1]
+    first = pl.multiple_of(pl.program_id(0) * rows, rows)
+    sent = []
+    for c in range(4):
+        for f in range(8):
+            b = 4 * f + c
+            for side in range(2):
+                column = 1024 * side + 128 * f
+                block = parts[c, :, column : column + 128]
+                pairs[b, pl.ds(side, rows, stride=2), :] = block.astype(F32)
+            made = pltpu.make_async_copy(
+                pairs.at[b].reshape(rows, 2, 128),
+                out.at[pl.ds(first, rows), :, pl.ds(128 * b, 128)],
+                sems.at[b],
             )
-        part[index] = sums.astype(BF16)
-
-    row_loop(seq // BLOCK, finish)
-    for b in range(3):
-        grad = lax.dot_general(d_low[b], normed[...], TN, preferred_element_type=F32).astype(BF16)
-        for f in range(8):
-            qkv_g[f, 128 * b : 128 * (b + 1)] = grad[:, 256 * f : 256 * (f + 1)]
+            made.start()
+            sent.append(made)
+    for made in sent:
+        made.wait()
 
 
 def shaped(shape, kind=BF16):
@@ -1154,9 +1230,6 @@
         axis=1,
     )
     rows, parts, units = gate_up.shape
-    gu_s = lax.dynamic_index_in_dim(
-        gate_up.reshape(rows, parts, 8, 4, units // 32), c, 3, keepdims=False
-    ).reshape(rows, parts * units // 4)
     down_rows = down_weight.shape[0] // 4
     dn_s = lax.dynamic_slice_in_dim(down_weight, c * down_rows, down_rows, 0)
     gain_s = jnp.concatenate(
@@ -1174,19 +1247,13 @@
         [q_gain[None], q_gain[None], k_gain[None], jnp.zeros((5, 128), F32)], axis=0
     )
 
-    ctx_scratch = [
-        pltpu.VMEM((2, tokens, width), BF16),
-        pltpu.VMEM((2, tokens, width), BF16),
-        pltpu.VMEM((tokens, width), BF16),
-        pltpu.VMEM((tokens, width), BF16),
-    ]
     table = pltpu.VMEM((seq, 128), F32)
     (
         qkv_w, out_w, gains, normed, qkv_raw, qkv_low, att_low, log_sums,
         gu_w, dn_w, dout_all, middle, mid_all,
     ) = call(
         forward_kernel,
-        [(a, HBM) for a in (qkv_s, out_weight, gain_s, source, gu_s, dn_s, d_out, cos, sin)]
+        [(a, HBM) for a in (qkv_s, out_weight, gain_s, source, gate_up, dn_s, d_out, cos, sin)]
         + [(head_gain, VMEM), (key_bias, VMEM)],
         [
             (shaped((8, rows, 384)), HBM),
@@ -1222,13 +1289,14 @@
             pltpu.VMEM((tokens, width), BF16),
             pltpu.VMEM((tokens, width), BF16),
             pltpu.VMEM((tokens, width), BF16),
+            pltpu.VMEM((8, rows, 2, 128), BF16),
+            pltpu.VMEM((2 * rows, 128), F32),
+            pltpu.VMEM((rows, width), BF16),
         ],
-        sems=(90, 100, 24),
+        sems=(90, 100, 32),
         number=0,
     )
-    attn_norm, ffn_norm = gains[0:1], gains[1:2]
     qkv_w = qkv_w.reshape(width, 384)
-    tables = [(cos, VMEM), (sin, VMEM), (head_gain, VMEM), (key_bias, VMEM)]
     hidden_units = units // 4
     gu_full = gu_w.reshape(width, parts * hidden_units)
     dn_full = dn_w.reshape(hidden_units, width)
@@ -1253,106 +1321,75 @@
 
     step = 64
     count = (rows + down_rows) // step
-    gu_all, dn_all, layer_out, d_middle, ffn_gain_part, branch_all = call(
-        feed_reduce_kernel,
+    block = pltpu.VMEM((tokens, width), BF16)
+    pair = pltpu.VMEM((2, tokens, width), BF16)
+    heads = pltpu.VMEM((seq, 128), BF16)
+    gu_all, dn_all, layer_out, qkv_all, out_all, input_grad, stats = call(
+        backward_kernel,
         [
             (gu_g.reshape(4, 2, rows, width), HBM),
             (dn_g.reshape(4, 2, down_rows, width), HBM),
             (ffn_part.reshape(4, tokens, width), HBM),
             (dmid_part.reshape(4, tokens, width), HBM),
-            (middle, VMEM),
-            (d_out, VMEM),
+            (middle, HBM),
+            (d_out, HBM),
+            (source, HBM),
             (keep, VMEM),
-            (ffn_norm, VMEM),
-        ],
+            (gains, VMEM),
+            (cos, HBM),
+            (sin, HBM),
+            (head_gain, VMEM),
+            (key_bias, VMEM),
+            (normed.reshape(4, tokens, width), HBM),
+        ]
+        + [(a, HBM) for a in (qkv_raw, qkv_low, att_low, log_sums, qkv_w, out_w)],
         [
             (shaped((4, rows, width)), HBM),
             (shaped((4, down_rows, width)), HBM),
             (shaped((tokens, width)), VMEM),
-            (shaped((tokens, width), F32), VMEM),
-            (shaped((1, width), F32), VMEM),
-            (shaped((4, tokens, width)), HBM),
-        ],
-        [
-            pltpu.VMEM((count, 4, step, width), BF16),
-            pltpu.VMEM((count, 4, step, width), BF16),
-            pltpu.VMEM((count, 4, step, width), BF16),
-            pltpu.VMEM((count, 4, step, width), BF16),
-            pltpu.VMEM((count, step, width), BF16),
-        ]
-        + ctx_scratch
-        + ctx_scratch
-        + [pltpu.VMEM((tokens, width), BF16)],
-        sems=(80, 80, 40),
-        number=2,
-    )
-    dnorm_part, qkv_g, out_g, head_gain_g = call(
-        attention_back_kernel,
-        [(branch_all.reshape(seq, width), VMEM), (qkv_w, VMEM), (out_w, VMEM)]
-        + tables
-        + [(a, VMEM) for a in (normed, qkv_raw, qkv_low, att_low, log_sums)],
-        [
-            (shaped((4, tokens, width)), VMEM),
-            (shaped((8, 384, rows)), VMEM),
-            (shaped((2, 128, width)), VMEM),
-            (shaped((8, 128), F32), VMEM),
-        ],
-        [
-            pltpu.VMEM((seq, 128), BF16),
-            pltpu.VMEM((seq, 128), BF16),
-            pltpu.VMEM((2, seq, 128), BF16),
-            pltpu.VMEM((3, seq, 128), BF16),
-            pltpu.VMEM((seq, 128), F32),
-            pltpu.VMEM((seq, 128), F32),
-        ],
-    )
-    qk_part = jnp.concatenate(
-        [
-            head_gain_g[0:1, :64] + head_gain_g[0:1, 64:],
-            head_gain_g[1:2, :64],
-            jnp.zeros((1, width - 128), F32),
-        ],
-        axis=1,
-    )
-    step = 192
-    count = 384 // step
-    qkv_all, out_all, input_grad, stats = call(
-        last_kernel,
-        [
-            (qkv_g.reshape(4, 2, 384, rows), HBM),
-            (out_g, HBM),
-            (dnorm_part, HBM),
-            (source, VMEM),
-            (d_middle, VMEM),
-            (attn_norm, VMEM),
-            (ffn_gain_part, VMEM),
-            (qk_part, VMEM),
-        ],
-        [
             (shaped((4, 384, rows)), HBM),
             (shaped((128, width)), VMEM),
             (shaped((tokens, width)), VMEM),
             (shaped((8, width), F32), VMEM),
         ],
         [
-            pltpu.VMEM((count, 4, step, rows), BF16),
-            pltpu.VMEM((count, 4, step, rows), BF16),
-            pltpu.VMEM((count, 4, step, rows), BF16),
-            pltpu.VMEM((count, 4, step, rows), BF16),
-            pltpu.VMEM((count, step, rows), BF16),
-        ]
-        + ctx_scratch
-        + [
+            pltpu.VMEM((2, 4, step, width), BF16),
+            pltpu.VMEM((count, 4, step, width), BF16),
+            pltpu.VMEM((count, 3, step, width), BF16),
+            pair, pair, block, block, pair, block, block,
+            pltpu.VMEM((tokens, width), F32),
+            block,
+            pltpu.VMEM((tokens, width), F32),
+            pltpu.VMEM((4, tokens, width), BF16),
+            pltpu.VMEM((4, tokens, width), BF16),
+            table,
+            table,
+            pltpu.VMEM((3, seq, 128), F32),
+            pltpu.VMEM((3, seq, 128), BF16),
+            pltpu.VMEM((2, seq, 128), BF16),
+            pltpu.VMEM((2, seq, 128), F32),
+            pltpu.VMEM((width, 384), BF16),
+            pltpu.VMEM((2, 128, width), BF16),
+            heads,
+            heads,
+            pltpu.VMEM((2, seq, 128), BF16),
+            pltpu.VMEM((3, seq, 128), BF16),
+            table,
+            table,
+            pltpu.VMEM((8, 128), F32),
+            pltpu.VMEM((4, 2, 384, rows), BF16),
+            pltpu.VMEM((2, 4, 192, rows), BF16),
+            pltpu.VMEM((2, 3, 192, rows), BF16),
+            pltpu.VMEM((2, 128, width), BF16),
             pltpu.VMEM((128, width), BF16),
-            pltpu.VMEM((128, width), BF16),
-            pltpu.VMEM((128, width), BF16),
-            pltpu.VMEM((4, 128, width), BF16),
+            pltpu.VMEM((3, 128, width), BF16),
             pltpu.VMEM((8, width), F32),
             pltpu.VMEM((8, 8, width), F32),
             pltpu.VMEM((4, 8, width), F32),
+            pltpu.SemaphoreType.REGULAR,
         ],
-        sems=(60, 60, 20),
-        number=3,
+        sems=(120, 120, 50),
+        number=1,
     )
     f = lax.axis_index("fsdp")
     qkv_grad = jnp.concatenate(
@@ -1363,11 +1400,19 @@
         ],
         axis=1,
     ).astype(F32)
-    gate_up_grad = (
-        jnp.transpose(gu_all.reshape(4, rows, parts, 8, units // 32), (1, 2, 3, 0, 4))
-        .reshape(rows, parts, units)
-        .astype(F32)
-    )
+    some = 64
+    gate_up_grad = pl.pallas_call(
+        interleave_kernel,
+        grid=(rows // some,),
+        in_specs=[pl.BlockSpec((4, some, width), lambda i: (0, i, 0))],
+        out_specs=HBM,
+        out_shape=shaped((rows, parts, units), F32),
+        scratch_shapes=[
+            pltpu.VMEM((32, 2 * some, 128), F32),
+            pltpu.SemaphoreType.DMA((32,)),
+        ],
+        compiler_params=pltpu.CompilerParams(vmem_limit_bytes=VMEM_BYTES),
+    )(gu_all)
     return (
         layer_out[None],
         input_grad[None],
@@ -1377,7 +1422,7 @@
         dn_all.reshape(4 * down_rows, width).astype(F32),
         lax.dynamic_slice_in_dim(stats[0], f * rows, rows, 0),
         lax.dynamic_slice_in_dim(stats[1], f * rows, rows, 0),
-        stats[2, :128].reshape(2, 64),
+        jnp.stack([stats[2, :64] + stats[2, 64:128], stats[2, 128:192]]),
     )
 
 

time: 648 us -> 542 us (0.84)
  the two profiles are of different devices: /device:TPU:3 before, /device:TPU:13 now
where the time goes in v3:
time: 542 us; the launch traced here: 531 us
  Pallas kernels  441 us (81%)
  matrix products  65.1 us (12%)
  other arithmetic  13.3 us (2%)
  local copies, waits for them, and re-layouts  9.82 us (2%)
    pallas_call x2, Pallas kernels, call(): pl.pallas_call(kernel, out_shape=tuple((shape for shape, _ in outs)), in_...  434 us
    dot_general x2, matrix products, contract_cols(): lax.dot_general(left, right, (((1,), (1,)), ((), ())), preferred_element_...  23.1 us
    dot_general x2, matrix products, contract_rows(): lax.dot_general(left, right, (((0,), (0,)), ((), ())), preferred_element_...  18.6 us
    dot_general x1, matrix products, split_heads(): projected = jnp.dot(mid_full, gu_full, preferred_element_type=F32)  15 us

profile of v3, /device:TPU:13, one launch (start us, length us, event | category | flops | bytes accessed | tf_op | source)
XLA Modules:
  0.0 531.4 jit_solution(8392842806095427387)
XLA Ops:
  0.7 1.1 constant_dynamic-slice_fusion.4
  1.9 0.9 constant_dynamic-slice_fusion.5
  2.8 0.8 pad_maximum_fusion.3.qkv_s
  3.6 0.8 constant_dynamic-slice_fusion.2.dn_s
  5.1 2.4 fusion.dout_s.dout_h
  7.5 0.6 broadcast_in_dim.48.key_bias
  8.3 0.7 maximum_maximum_fusion.head_gain
  9.0 1.0 copy.35.cos_h
  10.1 1.0 copy.36.sin_h
  11.2 0.7 maximum_convert_fusion.1.gain_s
  11.9 188.5 %shard_map.187 = (bf16[8,256,384]{2,1,0:T(8,128)(2,1)}, bf16[2,128,2048]{2,1,0:T(8,128)(2,1)}, f32[8,2048]{1,0:T(8,128)}, bf16[1024,2048]{1,0:T(8,128)(2,1)}, f3...) custom-call(bf16[256,384]{1,0:T(8,128)(2,1)} %pad_maximum_fusion.3.q, ...), custom_call_target="tpu_custom_call" | custom-call | tf_op jit(solution)/shard_map/pallas_call | solution.py:1190
  200.3 15.0 %fusion.7 = f32[1024,2048]{0,1:T(8,128)} fusion(bf16[1024,2048]{1,0:T(8,128)(2,1)} %bitcast.73, bf16[2048,2048]{1,0:T(8,128)(2,1)} %bitcast.71), kind=kOutput, calls=%fused_computation.36 | convolution fusion | flops 8589934592 | bytes 20971520 | tf_op jit(solution)/shard_map/dot_general | solution.py:1305
  215.3 10.9 %multiply_convert_fusion.2 = (bf16[1024,1024]{0,1:T(8,128)(2,1)S(1)}, bf16[1024,1024]{0,1:T(8,128)(2,1)}, bf16[1024,1024]{0,1:T(8,128)(2,1)S(1)}) fusion(f32[1024,2048]{0,1:T(8,128)} %fusion.7, bf16[1024,2048]{1,0:T(8,128)(2,1)S(1)} %bitcast.75, bf16[1024,2048]{1,0:T(8,128)(2,1)} %bitcast.77), kind=kOutput, calls=%fused_computation.4 | convolution fusion | flops 4311744512 | bytes 23068672 | tf_op jit(solution)/shard_map/dot_general | solution.py:75
  226.3 12.2 %convolution_convert_fusion.1 = bf16[1024,2048]{1,0:T(8,128)(2,1)} fusion(bf16[2048,2048]{1,0:T(8,128)(2,1)S(1)} %bitcast.72, bf16[1024,1024]{0,1:T(8,128)(2,1)} %get-tuple-element.50, bf16[1024,1024]{0,1:T(8,128)(2,1)S(1)} %get-tuple-element.49), kind=kOutput, calls=%fused_computation.6 | convolution fusion | flops 8600420352 | bytes 16777216 | tf_op jit(solution)/shard_map/dot_general | solution.py:75
  238.4 8.4 %convolution_convert_fusion.2 = bf16[1024,2048]{1,0:T(8,128)(2,1)} fusion(bf16[1024,1024]{0,1:T(8,128)(2,1)S(1)} %get-tuple-element.51, bf16[1024,2048]{1,0:T(8,128)(2,1)} %bitcast.78), kind=kOutput, calls=%fused_computation.7 | convolution fusion | flops 4297064448 | bytes 10485760 | tf_op jit(solution)/shard_map/dot_general | solution.py:1309
  246.9 6.1 %convolution_convert_fusion.3 = bf16[1024,2048]{1,0:T(8,128)(2,1)} fusion(bf16[1024,1024]{0,1:T(8,128)(2,1)S(1)} %get-tuple-element.51, bf16[1024,2048]{1,0:T(8,128)(2,1)S(1)} %bitcast.76), kind=kOutput, calls=%fused_computation.8 | convolution fusion | flops 4297064448 | bytes 10485760 | tf_op jit(solution)/shard_map/dot_general | solution.py:69
  253.0 12.5 %convolution_convert_fusion = bf16[2048,2048]{1,0:T(8,128)(2,1)} fusion(bf16[1024,2048]{1,0:T(8,128)(2,1)S(1)} %bitcast.74, bf16[1024,1024]{0,1:T(8,128)(2,1)S(1)} %copy-done.15, bf16[1024,1024]{0,1:T(8,128)(2,1)S(1)} %get-tuple-element.49), kind=kOutput, calls=%fused_computation | convolution fusion | flops 8602517504 | bytes 16777216 | tf_op jit(solution)/shard_map/dot_general | solution.py:69
  265.5 0.7 fusion.1.keep
  266.2 245.3 %shard_map.188 = (bf16[4,256,2048]{2,1,0:T(8,128)(2,1)}, bf16[4,128,2048]{2,1,0:T(8,128)(2,1)}, bf16[256,2048]{1,0:T(8,128)(2,1)}, bf16[4,384,256]{2,1,0:T(8,128...) custom-call(bf16[4,2,256,2048]{3,2,1,0:T(8,128)(2,1)} %bitcast.54, ...), custom_call_target="tpu_custom_call" | custom-call | tf_op jit(solution)/shard_map/pallas_call | solution.py:1190
  511.5 0.8 slice_add_fusion
  512.3 0.6 pad_maximum_fusion.4
  512.9 0.9 fusion.6
  513.8 0.6 constant_dynamic-slice_fusion
  514.4 7.4 %shard_map.189 = f32[256,2,4096]{2,1,0:T(2,128)} custom-call(bf16[4,256,2048]{2,1,0:T(8,128)(2,1)} %get-tuple-element.46.parts), custom_call_target="tpu_custom_call" | custom-call | tf_op jit(solution)/shard_map/pallas_call | solution.py:1404
  521.8 0.2 copy.42
  522.1 0.1 copy.43
  522.2 0.1 copy.44
  522.3 1.3 maximum_convert_fusion
  523.6 4.3 bitcast_convert_fusion
  527.9 1.1 convert_element_type.79
  529.0 1.0 copy.52
  530.0 1.0 copy.53
  (48 shorter events, 0.5 us)
Async XLA Ops:
  0.6 2.9 copy-start
  0.7 8.3 %copy-start.7 = (f32[1024,32]{0,1:T(8,128)S(1)}, f32[1024,32]{0,1:T(8,128)}, u32[]{:S(2)}) copy-start(f32[1024,32]{0,1:T(8,128)} %constant.49.clone) | copy-start | bytes 393220
  0.7 9.4 %copy-start.6 = (f32[1024,64]{0,1:T(8,128)S(1)}, f32[1024,64]{0,1:T(8,128)}, u32[]{:S(2)}) copy-start(f32[1024,64]{0,1:T(8,128)} %constant.57) | copy-start | bytes 786436
  0.7 7.4 %copy-start.8 = (bf16[2,64]{1,0:T(2,128)(2,1)S(1)}, bf16[2,64]{1,0:T(2,128)(2,1)}, u32[]{:S(2)}) copy-start(bf16[2,64]{1,0:T(2,128)(2,1)} %param.21) | copy-start | bytes 772
  0.7 10.4 %copy-start.13 = (bf16[256]{0:T(256)(128)(2,1)S(1)}, bf16[256]{0:T(256)(128)(2,1)}, u32[]{:S(2)}) copy-start(bf16[256]{0:T(256)(128)(2,1)} %param.19) | copy-start | bytes 1540
  0.7 10.4 %copy-start.14 = (bf16[256]{0:T(256)(128)(2,1)S(1)}, bf16[256]{0:T(256)(128)(2,1)}, u32[]{:S(2)}) copy-start(bf16[256]{0:T(256)(128)(2,1)} %param.20) | copy-start | bytes 1540
  200.3 15.0 %copy-start.11 = (bf16[4,256,2048]{2,1,0:T(8,128)(2,1)S(1)}, bf16[4,256,2048]{2,1,0:T(8,128)(2,1)}, u32[]{:S(2)}) copy-start(bf16[4,256,2048]{2,1,0:T(8,128)(2,1)} %get-tuple-element.30) | copy-start | bytes 12582916
  215.3 11.0 %copy-start.9 = (bf16[8,256,2048]{2,1,0:T(8,128)(2,1)S(1)}, bf16[8,256,2048]{2,1,0:T(8,128)(2,1)}, u32[]{:S(2)}) copy-start(bf16[8,256,2048]{2,1,0:T(8,128)(2,1)} %get-tuple-element.32) | copy-start | bytes 25165828
  238.4 8.4 %copy-start.12 = (bf16[4,256,2048]{2,1,0:T(8,128)(2,1)S(1)}, bf16[4,256,2048]{2,1,0:T(8,128)(2,1)}, u32[]{:S(2)}) copy-start(bf16[4,256,2048]{2,1,0:T(8,128)(2,1)} %get-tuple-element.30) | copy-start | bytes 12582916
  246.9 6.1 %copy-start.10 = (bf16[4,256,2048]{2,1,0:T(8,128)(2,1)S(1)}, bf16[4,256,2048]{2,1,0:T(8,128)(2,1)}, u32[]{:S(2)}) copy-start(bf16[4,256,2048]{2,1,0:T(8,128)(2,1)} %get-tuple-element.29) | copy-start | bytes 12582916
  246.9 6.1 %copy-start.15 = (bf16[1024,1024]{0,1:T(8,128)(2,1)S(1)}, bf16[1024,1024]{0,1:T(8,128)(2,1)}, u32[]{:S(2)}) copy-start(bf16[1024,1024]{0,1:T(8,128)(2,1)} %get-tuple-element.50) | copy-start | bytes 6291460
  514.4 7.4 %copy-start.4 = (bf16[4,384,256]{2,1,0:T(8,128)(2,1)S(1)}, bf16[4,384,256]{2,1,0:T(8,128)(2,1)}, u32[]{:S(2)}) copy-start(bf16[4,384,256]{2,1,0:T(8,128)(2,1)} %get-tuple-element.44) | copy-start | bytes 2359300
  522.3 5.6 %copy-start.5 = (bf16[128,2048]{1,0:T(8,128)(2,1)S(1)}, bf16[128,2048]{1,0:T(8,128)(2,1)}, u32[]{:S(2)}) copy-start(bf16[128,2048]{1,0:T(8,128)(2,1)} %get-tuple-element.45) | copy-start | bytes 1572868
  523.6 5.4 %copy-start.3 = (bf16[256,2048]{1,0:T(8,128)(2,1)S(1)}, bf16[256,2048]{1,0:T(8,128)(2,1)}, u32[]{:S(2)}) copy-start(bf16[256,2048]{1,0:T(8,128)(2,1)} %get-tuple-element.42) | copy-start | bytes 3145732
  523.6 6.3 %copy-start.2 = (bf16[256,2048]{1,0:T(8,128)(2,1)S(1)}, bf16[256,2048]{1,0:T(8,128)(2,1)}, u32[]{:S(2)}) copy-start(bf16[256,2048]{1,0:T(8,128)(2,1)} %get-tuple-element.43) | copy-start | bytes 3145732
  523.6 7.3 %copy-start.1 = (bf16[512,2048]{1,0:T(8,128)(2,1)S(1)}, bf16[512,2048]{1,0:T(8,128)(2,1)}, u32[]{:S(2)}) copy-start(bf16[512,2048]{1,0:T(8,128)(2,1)} %param.18) | copy-start | bytes 6291460

commit v4 on v3

--- a/solution.py
+++ b/solution.py
@@ -337,6 +337,8 @@
         self.xo, self.yo, self.co = 1 - self.x, 1 - self.y, 1 - self.core
         upper = lax.div(self.z, 2)
         self.others = (self.z + 1 - 2 * lax.rem(self.z, 2), 2 - upper, 3 - 3 * upper)
+        self.inner = lax.rem(self.z, 2) + upper == 1
+        self.far = 2 - 2 * upper
         self.x_dev = (self.z * 2 + self.xo, self.c)
         self.c_core = self.y * 2 + self.co
         self.c_y = self.yo * 2 + self.core
@@ -449,16 +451,64 @@
                 self.links.arrive(block, self.x_slot + 4 * k + z)
 
 
+class SpreadTree(SpreadPlane):
+    def begin_z(self):
+        place = self.place
+        self.passed = []
+        for k, (src, dst) in enumerate(self.chunks):
+            slot = self.z_slot + 4 * k + place.z
+            for other in place.others[:2]:
+                self.links.send(src, dst(place.f), slot, place.z_dev(other))
+
+    def onward(self, k):
+        place, dst = self.place, self.chunks[k][1]
+        blocks = [(dst(o * 2 + place.x), self.z_slot + 4 * k + o) for o in place.others[1:]]
+        made = [
+            self.links.copy(block, block, slot, place.z_dev(place.others[0]))
+            for block, slot in blocks
+        ]
+        self.passed += made
+
+        @pl.when(place.inner)
+        def _():
+            for (block, slot), one in zip(blocks, made):
+                self.links.arrive(block, slot)
+                one.start()
+
+    def forward(self, k):
+        place, dst = self.place, self.chunks[k][1]
+        blocks = [(dst(o * 2 + place.x), self.z_slot + 4 * k + o) for o in place.others]
+        self.links.arrive(*blocks[0])
+        near = self.x_slot + 4 * k + place.others[0]
+        self.links.send(blocks[0][0], blocks[0][0], near, place.x_dev)
+
+        @pl.when(jnp.logical_not(place.inner))
+        def _():
+            for block, slot in blocks[1:]:
+                self.links.arrive(block, slot)
+
+        for other, (block, _) in zip(place.others[1:], blocks[1:]):
+            self.links.send(block, block, self.x_slot + 4 * k + other, place.x_dev)
+
+    def finish(self):
+        @pl.when(self.place.inner)
+        def _():
+            for made in self.passed:
+                made.wait_send()
+
+
 class ReducePlane:
     def __init__(self, links, place, chunks, from_x, from_z, own=None):
         self.links, self.place, self.chunks = links, place, chunks
         self.from_x, self.from_z, self.own = from_x, from_z, own
+        self.summed = 0
         self.x_slot, self.z_slot = links.slots(len(chunks)), links.slots(3 * len(chunks))
         self.loads, self.z_sends = {}, {}
 
     def send_x(self, k):
         place = self.place
-        self.links.send(self.chunks[k](place.xo), self.from_x.at[k], self.x_slot + k, place.x_dev)
+        from_x = self.from_x.at[k - self.summed]
+        self.links.send(self.chunks[k](place.xo), from_x, self.x_slot + k, place.x_dev)
 
     def load(self, k):
         slots = self.own.shape[0]
@@ -507,6 +557,86 @@
                 made.wait_send()
 
 
+class ReduceTree(ReducePlane):
+    def __init__(self, links, place, chunks, from_x, from_z, via, own, summed):
+        super().__init__(links, place, chunks, from_x, from_z, own)
+        self.summed = summed
+        self.via, self.via_slot = via, links.slots(len(chunks))
+        self.outer = jnp.logical_not(place.inner)
+
+    def load(self, k):
+        slots = self.own.shape[0]
+        self.settle(self.z_sends.pop(k - slots, []))
+        self.loads[k] = self.links.local(self.chunks[k](self.place.x), self.own.at[k % slots])
+
+    def settle(self, sends):
+        for made, when in sends:
+            if when is None:
+                made.wait_send()
+            else:
+                pl.when(when)(made.wait_send)
+
+    def middle(self, k):
+        place = self.place
+        self.loads[k].wait()
+        mine = self.mine(k)
+        if k >= self.summed:
+            from_x = self.from_x.at[k - self.summed]
+            self.links.arrive(from_x, self.x_slot + k)
+            for other in place.others:
+                pair = mine[other].astype(F32) + from_x[other].astype(F32)
+                mine[other] = pair.astype(BF16)
+        near = place.others[0]
+        device = place.z_dev(near)
+        direct = self.links.copy(mine.at[near], self.from_z.at[k, 0], self.z_slot + 3 * k, device)
+        direct.start()
+        far = self.links.copy(
+            mine.at[pl.ds(place.far, 2)], self.via.at[k], self.via_slot + k, device
+        )
+        pl.when(self.outer)(far.start)
+        self.z_sends[k] = [(direct, None), (far, self.outer)]
+
+    def combine(self, k):
+        place = self.place
+        mine = self.mine(k)
+
+        sent = [
+            self.links.copy(
+                mine.at[place.far + j],
+                self.from_z.at[k, 1],
+                self.z_slot + 3 * k + 1,
+                place.z_dev(place.far + j),
+            )
+            for j in range(2)
+        ]
+
+        @pl.when(place.inner)
+        def _():
+            self.links.arrive(self.via.at[k], self.via_slot + k)
+            for j in range(2):
+                here = mine[place.far + j].astype(F32) + self.via[k, j].astype(F32)
+                mine[place.far + j] = here.astype(BF16)
+                sent[j].start()
+
+        self.z_sends[k] += [(made, place.inner) for made in sent]
+
+    def end(self, k):
+        place = self.place
+        sums = self.mine(k)[place.z].astype(F32)
+        if k >= self.summed:
+            sums += self.from_x[k - self.summed, place.z].astype(F32)
+        for side in range(2):
+            self.links.arrive(self.from_z.at[k, side], self.z_slot + 3 * k + side)
+            sums += self.from_z[k, side].astype(F32)
+        total = self.from_z.at[k, 0]
+        total[...] = sums.astype(BF16)
+        return total
+
+    def finish(self):
+        for sends in self.z_sends.values():
+            self.settle(sends)
+
+
 class SpreadCtx:
     def __init__(self, links, place, out, parts):
         self.links, self.place, self.out, self.parts = links, place, out, parts
@@ -549,10 +679,15 @@
                     self.slot + 3 * k + side,
                     place.core_dev,
                 )
-                if self.own is not None:
-                    self.loads[side, k] = self.links.local(
-                        self.part.at[y * 2 + place.core, rows], self.own.at[side, rows]
-                    )
+                if self.own is not None and side == 0:
+                    self.load(0, k)
+
+    def load(self, side, k):
+        rows = self.parts[k]
+        y = self.place.y if side else self.place.yo
+        self.loads[side, k] = self.links.local(
+            self.part.at[y * 2 + self.place.core, rows], self.own.at[rows]
+        )
 
     def pair(self, side, k):
         rows = self.parts[k]
@@ -562,12 +697,14 @@
             own = self.part[y * 2 + self.place.core, rows]
         else:
             self.loads[side, k].wait()
-            own = self.own[side, rows]
+            own = self.own[rows]
         return own.astype(F32) + self.from_core[side, rows].astype(F32)
 
     def cross(self, k):
         rows = self.parts[k]
         self.to_y[rows] = self.pair(0, k).astype(BF16)
+        if self.own is not None:
+            self.load(1, k)
         made = self.links.send(
             self.to_y.at[rows], self.from_y.at[rows], self.slot + 3 * k + 2, self.place.y_dev
         )
@@ -605,12 +742,12 @@
     return jnp.where(low, first, second)
 
 
-def row_loop(count, body):
+def row_loop(count, body, first=0):
     def step(index, carry):
         body(index)
         return carry
 
-    lax.fori_loop(0, count, step, 0)
+    lax.fori_loop(first, first + count, step, 0)
 
 
 BLOCK = 256
@@ -665,8 +802,11 @@
     holds = place.z == place.c
     down = [
         links.copy(out_s, out_w.at[place.x], root_slot, place.z_dev(other))
-        for other in place.others
+        for other in place.others[:2]
     ]
+    relay = links.copy(out_w.at[place.x], out_w.at[place.x], root_slot, place.z_dev(place.others[0]))
+    across = lax.div(place.c, 2) != lax.div(place.z, 2)
+    relays = jnp.logical_and(place.inner, across)
     sideways = links.copy(out_s, out_w.at[place.x], side_slot, place.x_dev)
     onward = links.copy(out_w.at[place.x], out_w.at[place.x], side_slot, place.x_dev)
     own = pltpu.make_async_copy(out_s, out_w.at[place.x], local_sems.at[links.locals])
@@ -687,18 +827,18 @@
             first = 1024 * side + 128 * f
             picked = gu_rows[pl.ds(side, rows, stride=2), :]
             gu_s[:, first : first + 128] = picked.astype(BF16)
-    step = 64
+    step = 32
     chunks = []
     for src, dst in ((dn_s, dn_w), (gu_s, gu_w)):
         for first in range(0, src.shape[0], step):
             rows = pl.ds(first, step)
             chunks.append((src.at[rows], lambda f, dst=dst, rows=rows: dst.at[f, rows]))
-    plane = SpreadPlane(links, place, chunks)
+    plane = SpreadTree(links, place, chunks)
     plane.begin_z()
-    plane.begin_x(0)
-    plane.begin_x(1)
+    for k in range(4):
+        plane.begin_x(k)
     qkv_plane.forward(0)
-    for k in range(2, len(chunks)):
+    for k in range(4, len(chunks)):
         plane.begin_x(k)
     last = [
         links.local(gu_s, gu_w.at[place.f]),
@@ -741,6 +881,8 @@
                 values[rows] = jnp.where(low, swapped, turned).astype(BF16)
 
     seq = normed.shape[0]
+    att_low[...] = jnp.zeros_like(att_low)
+    log_sums[...] = jnp.zeros_like(log_sums)
     row_loop(seq // BLOCK, project)
     last += [
         links.local(normed, normed_h),
@@ -749,27 +891,38 @@
         links.local(qkv_w, qkv_wh),
     ]
 
-    def heads(b):
+    def heads(index):
+        b, half = lax.div(index, 2), lax.rem(index, 2)
         for i in range(seq // BLOCK):
             rows, span = pl.ds(i * BLOCK, BLOCK), (i + 1) * BLOCK
             query = qkv_low[b, rows]
-            low = low_half(query.shape)
-            outs, logs = [], []
-            for half in range(2):
-                chosen = jnp.where(low if half == 0 else jnp.logical_not(low), query, 0)
-                scores = attention_scores(chosen, keys[:span], key_bias[0:1], i * BLOCK, span)
-                top = jnp.max(scores, axis=-1, keepdims=True)
-                expanded = jnp.exp(scores - top)
-                sums = jnp.sum(expanded, axis=-1, keepdims=True)
-                probs = (expanded * (1.0 / sums)).astype(BF16)
-                outs.append(jnp.dot(probs, values[:span], preferred_element_type=F32))
-                logs.append(top + jnp.log(sums))
-            att_low[b, rows] = jnp.where(low, outs[0], outs[1]).astype(BF16)
-            log_sums[b, rows] = jnp.where(low, logs[0], logs[1])
-
+            side = lax.div(lax.broadcasted_iota(jnp.int32, query.shape, 1), 64) == half
+            chosen = jnp.where(side, query, 0)
+            scores = attention_scores(chosen, keys[:span], key_bias[0:1], i * BLOCK, span)
+            top = jnp.max(scores, axis=-1, keepdims=True)
+            expanded = jnp.exp(scores - top)
+            sums = jnp.sum(expanded, axis=-1, keepdims=True)
+            probs = (expanded * (1.0 / sums)).astype(BF16)
+            out = jnp.dot(probs, values[:span], preferred_element_type=F32)
+            att_low[b, rows] = jnp.where(side, out.astype(BF16), att_low[b, rows])
+            log_sums[b, rows] = jnp.where(side, top + jnp.log(sums), log_sums[b, rows])
+
+    @pl.when(relays)
+    def _():
+        links.arrive(out_w.at[place.x], root_slot)
+        relay.start()
+        onward.start()
+
+    plane.onward(0)
     row_loop(2, heads)
-
-    @pl.when(jnp.logical_not(holds))
+    plane.onward(1)
+    plane.onward(2)
+    row_loop(2, heads, 2)
+    plane.onward(3)
+    for k in range(3):
+        plane.forward(k)
+
+    @pl.when(jnp.logical_not(jnp.logical_or(holds, relays)))
     def _():
         links.arrive(out_w.at[place.x], root_slot)
         onward.start()
@@ -796,10 +949,17 @@
         links.local(log_sums, log_sums_h),
         links.local(out_w, out_wh),
     ]
+    plane.onward(4)
     for k in range(2):
         reduce.cross(k)
-    plane.forward(0)
-    plane.forward(1)
+    plane.forward(3)
+    plane.onward(5)
+    plane.onward(6)
+    plane.forward(4)
+    plane.onward(7)
+    plane.forward(5)
+    plane.onward(8)
+    plane.forward(6)
     mid = SpreadCtx(links, place, mid_all, parts)
     for k, rows in enumerate(parts):
         value = x_all[place.c, rows].astype(F32) + reduce.total(k)
@@ -807,10 +967,13 @@
         mid_low[rows] = (value * row_factor(value) * gains[1:2]).astype(BF16)
         mid.begin(k, mid_low.at[rows])
         last.append(links.local(mid_low.at[rows], mid_all.at[place.c, rows]))
-    plane.forward(2)
+    for k in range(9, len(chunks)):
+        plane.onward(k)
+    plane.forward(7)
+    plane.forward(8)
     for k in range(2):
         mid.forward(k)
-    for k in range(3, len(chunks)):
+    for k in range(9, len(chunks)):
         plane.forward(k)
     plane.end()
     mid.end()
@@ -818,12 +981,17 @@
     for made in last:
         made.wait()
     links.finish()
+    plane.finish()
 
     @pl.when(holds)
     def _():
         for made in down:
             made.wait_send()
         sideways.wait_send()
+
+    @pl.when(relays)
+    def _():
+        relay.wait_send()
 
     @pl.when(jnp.logical_not(holds))
     def _():
@@ -842,18 +1010,141 @@
     return factor * scaled - value * (factor * factor * factor * inner), gain_sum
 
 
+def feed_kernel(
+    gu_h, dn_h, dout_h, mid_h, middle_h, gains,
+    gu_g, dn_pair, ffn_h, d_middle_h, branch_s, ffn_gain,
+    gu_w, dn_w, dout, mid, hidden, d_proj, dn_g, from_x, stage,
+    part, from_core, to_y, from_y, middle, branch, send_sems, recv_sems, local_sems,
+):
+    place = Place()
+    links = Links(place, send_sems, recv_sems, local_sems)
+    shards, rows, width = gu_w.shape
+    units, seq = hidden.shape[1], hidden.shape[0]
+    tokens = mid.shape[1]
+    first = [links.local(mid_h, mid)]
+    later, loads = [], []
+    for n in range(units // 256):
+        gate, up = pl.ds(256 * n, 256), pl.ds(units + 256 * n, 256)
+        loads.append([
+            links.local(gu_h.at[:, :, gate], gu_w.at[:, :, gate]),
+            links.local(gu_h.at[:, :, up], gu_w.at[:, :, up]),
+        ])
+        if n == 0:
+            first += [links.local(dout_h, dout), links.local(dn_h, dn_w)]
+    later.append(links.local(middle_h, middle))
+    place.meet([place.x_dev, place.core_dev, place.y_dev])
+    for made in first:
+        made.wait()
+
+    x_slot = links.slots(4)
+    for n in range(units // 256):
+        for made in loads[n]:
+            made.wait()
+        gate_columns, up_columns = slice(256 * n, 256 * (n + 1)), slice(units + 256 * n, units + 256 * (n + 1))
+
+        def activation(index, gate_columns=gate_columns, up_columns=up_columns, n=n):
+            low = mid[index]
+            gate = jnp.dot(
+                low, gu_w[:, :, gate_columns].reshape(width, 256), preferred_element_type=F32
+            )
+            up = jnp.dot(
+                low, gu_w[:, :, up_columns].reshape(width, 256), preferred_element_type=F32
+            )
+            d_hidden = lax.dot_general(
+                dout[index], dn_w[2 * n : 2 * n + 2].reshape(256, width), NT,
+                preferred_element_type=F32,
+            )
+            at = pl.ds(pl.multiple_of(index * tokens, tokens), tokens)
+            sigmoid = 1.0 / (1.0 + jnp.exp(-gate))
+            silu = gate * sigmoid
+            hidden[at, gate_columns] = (silu * up).astype(BF16)
+            d_gate = d_hidden * up * (sigmoid * (1.0 + gate * (1.0 - sigmoid)))
+            d_proj[at, gate_columns] = d_gate.astype(BF16)
+            d_proj[at, up_columns] = (d_hidden * silu).astype(BF16)
+
+        row_loop(4, activation)
+        left = hidden[:, gate_columns].T
+
+        def down_grad(j, left=left, n=n):
+            wide = pl.ds(pl.multiple_of(512 * j, 512), 512)
+            right = dout[:, :, wide].reshape(seq, 512)
+            grad = jnp.dot(left, right, preferred_element_type=F32).astype(BF16)
+            dn_g[n, 0, :, wide] = grad[:128]
+            dn_g[n, 1, :, wide] = grad[128:]
+
+        row_loop(4, down_grad)
+        links.send(dn_g.at[n, place.xo], from_x.at[n], x_slot + n, place.x_dev)
+
+    def mid_grad(f):
+        grad = lax.dot_general(d_proj[...], gu_w[f], NT, preferred_element_type=F32)
+        columns = pl.ds(pl.multiple_of(rows * f, rows), rows)
+        part[:, :, columns] = grad.astype(BF16).reshape(4, tokens, rows)
+
+    row_loop(shards, mid_grad)
+    parts = halves(tokens)
+    dmid = ReduceCtx(links, place, part, parts, None, from_core, to_y, from_y)
+    dmid.begin()
+
+    def gate_up_grad(z):
+        for x in range(2):
+            columns = pl.ds(pl.multiple_of(2 * rows * z + rows * x, rows), rows)
+            left = mid[:, :, columns].reshape(seq, rows).T
+            for j in range(4):
+                wide = slice(512 * j, 512 * (j + 1))
+                grad = jnp.dot(left, d_proj[:, wide], preferred_element_type=F32)
+                stage[x, :, wide] = grad.astype(BF16)
+        made = pltpu.make_async_copy(stage, gu_g.at[z], local_sems.at[links.locals])
+        made.start()
+        made.wait()
+
+    row_loop(1, gate_up_grad)
+    for k in range(2):
+        dmid.cross(k)
+    lax.fori_loop(1, 4, lambda z, carry: (gate_up_grad(z), carry)[1], 0)
+    links.locals += 1
+
+    def feed_out(index):
+        at = pl.ds(pl.multiple_of(index * tokens, tokens), tokens)
+        for j in range(4):
+            wide = slice(512 * j, 512 * (j + 1))
+            right = dn_w[:, :, wide].reshape(units, 512)
+            sums = jnp.dot(hidden[at], right, preferred_element_type=F32)
+            mid[index, :, wide] = sums.astype(BF16)
+
+    row_loop(4, feed_out)
+    later.append(links.local(mid, ffn_h))
+    later[0].wait()
+    gain_sum = None
+    for k, at in enumerate(parts):
+        grad, term = norm_back(dmid.total(k), middle[at], gains[1:2])
+        gain_sum = term if gain_sum is None else gain_sum + term
+        middle[at] = grad + dout[place.c, at].astype(F32)
+        branch[at] = middle[at].astype(BF16)
+        later.append(links.local(middle.at[at], d_middle_h.at[at]))
+        later.append(links.local(branch.at[at], branch_s.at[at]))
+    ffn_gain[...] = gain_sum
+    for n in range(4):
+        links.arrive(from_x.at[n], x_slot + n)
+        pair = dn_g[n, place.x].astype(F32) + from_x[n].astype(F32)
+        from_x[n] = pair.astype(BF16)
+        later.append(links.local(from_x.at[n], dn_pair.at[n]))
+    for made in later[1:]:
+        made.wait()
+    links.finish()
+
+
 def backward_kernel(
-    gu_g, dn_g, ffn_part, dmid_part, middle_h, dout_h, x_h, keep, gains,
+    gu_g, dn_pair, ffn_part, middle_h, d_middle_h, branch_s, x_h, keep, gains, ffn_gain,
     cos_h, sin_h, head_gain, key_bias,
     normed_h, qkv_raw_h, qkv_low_h, att_low_h, log_sums_h, qkv_wh, out_wh,
     gu_all, dn_all, layer_out, qkv_all, out_all, input_grad, stats,
-    own, from_x, from_z,
+    own, from_x, from_z, via,
     ctx_own, from_core1, to_y1, from_y1, from_core2, to_y2, from_y2,
-    middle, dout_s, d_middle, branch_all, part,
+    middle, x_s, d_middle, branch_all, part,
     cos, sin, qkv_raw, qkv_low, att_low, log_sums, qkv_w, out_w,
     keys, values, d_att, d_low, d_keys, d_values, gain_g,
     qkv_g, qkv_x, qkv_z, out_g, out_x, out_z,
-    mine, plane_stats, ctx_stats, free, send_sems, recv_sems, local_sems,
+    mine, plane_stats, ctx_stats, send_sems, recv_sems, local_sems,
 ):
     place = Place()
     links = Links(place, send_sems, recv_sems, local_sems)
@@ -863,13 +1154,17 @@
     )
     step = from_x.shape[2]
     chunks, where = [], []
-    for grad, out in ((dn_g, dn_all), (gu_g, gu_all)):
-        for first in range(0, grad.shape[2], step):
-            rows = pl.ds(first, step)
-            chunks.append(lambda x, grad=grad, rows=rows: grad.at[:, x, rows])
-            where.append((out, rows))
+    for first in range(0, dn_pair.shape[1], step):
+        rows = pl.ds(first, step)
+        chunks.append(lambda x, rows=rows: dn_pair.at[:, rows])
+        where.append((dn_all, rows))
+    summed = len(chunks)
+    for first in range(0, gu_g.shape[2], step):
+        rows = pl.ds(first, step)
+        chunks.append(lambda x, rows=rows: gu_g.at[:, x, rows])
+        where.append((gu_all, rows))
     count = len(chunks)
-    plane = ReducePlane(links, place, chunks, from_x, from_z, own)
+    plane = ReduceTree(links, place, chunks, from_x, from_z, via, own, summed)
     outs = [SpreadCtx(links, place, out, [rows]) for out, rows in where]
     kept = []
 
@@ -883,45 +1178,37 @@
 
     tokens, width = middle.shape
     parts = halves(tokens)
-    dmid = ReduceCtx(links, place, dmid_part, parts, ctx_own, from_core1, to_y1, from_y1)
-    dmid.begin()
-    for k in range(count):
+    branch = SpreadCtx(links, place, branch_all, parts)
+    for k, rows in enumerate(parts):
+        branch.begin(k, branch_s.at[rows])
+    for k in (2, 3):
         plane.send_x(k)
-    early = [links.local(middle_h, middle), links.local(dout_h, dout_s)]
+    ffn = ReduceCtx(links, place, ffn_part, parts, ctx_own, from_core1, to_y1, from_y1)
+    ffn.begin()
     for k in range(own.shape[0]):
         plane.load(k)
     late = [
         links.local(a, b)
         for a, b in (
+            (branch_s, branch_all.at[place.c]),
             (out_wh, out_w), (qkv_low_h, qkv_low), (att_low_h, att_low), (log_sums_h, log_sums),
             (cos_h, cos), (sin_h, sin), (qkv_raw_h, qkv_raw), (qkv_wh, qkv_w),
+            (middle_h, middle), (d_middle_h, d_middle), (x_h, x_s),
         )
     ]
-    for k in range(2):
-        dmid.cross(k)
-    for made in early:
-        made.wait()
     gain_g[...] = jnp.zeros_like(gain_g)
     d_keys[...] = jnp.zeros_like(d_keys)
+    d_low[...] = jnp.zeros_like(d_low)
     d_values[...] = jnp.zeros_like(d_values)
     plane.middle(0)
-    branch = SpreadCtx(links, place, branch_all, parts)
-    ffn_gain = None
-    for k, rows in enumerate(parts):
-        grad, term = norm_back(dmid.total(k), middle[rows], gains[1:2])
-        ffn_gain = term if ffn_gain is None else ffn_gain + term
-        grad += dout_s[rows].astype(F32)
-        d_middle[rows] = grad
-        branch_all[place.c, rows] = grad.astype(BF16)
-        branch.begin(k, branch_all.at[place.c, rows])
-    ffn = ReduceCtx(links, place, ffn_part, parts, ctx_own, from_core2, to_y2, from_y2)
-    ffn.begin()
     plane.middle(1)
     for k in range(2):
-        branch.forward(k)
-    for k in range(2):
         ffn.cross(k)
-    end(0)
+    branch.forward(0)
+    plane.combine(0)
+    branch.forward(1)
+    plane.middle(2)
+    plane.combine(1)
     branch.end()
     for made in late:
         made.wait()
@@ -941,7 +1228,6 @@
                 branch_all[index], out_w[b], NT, preferred_element_type=F32
             ).astype(BF16)
 
-    x_load = links.local(x_h, dout_s)
     row_loop(seq // BLOCK, prepare)
     for b in range(2):
         left = att_low[b].T
@@ -951,9 +1237,11 @@
             out_g[b, :, columns] = jnp.dot(left, right, preferred_element_type=F32).astype(BF16)
     out_slot = links.slots(1)
     links.send(out_g.at[place.xo], out_x, out_slot, place.x_dev)
+    for k in range(4, count):
+        plane.send_x(k)
     links.settle(branch.sends)
     normed_load = links.local(normed_h, branch_all)
-    plane.middle(2)
+    plane.middle(3)
 
     def unturn(row, rows, grads, block):
         back = grads * cos[rows] + partner(grads * sin[rows])
@@ -963,38 +1251,43 @@
         inner = half_sums(scaled * block) * (1.0 / HEAD_DIM)
         return factor * scaled - block * (factor * factor * factor * inner), gain_term
 
-    def heads(b):
+    def heads(index):
+        b, half = lax.div(index, 2), lax.rem(index, 2)
         for i in range(seq // SHORT):
             rows, span = pl.ds(i * SHORT, SHORT), (i + 1) * SHORT
-            query, d_out = qkv_low[b, rows], d_att[b, rows]
-            logs = log_sums[b, rows]
-            low = low_half(query.shape)
-            d_query = []
-            for half in range(2):
-                side = low if half == 0 else jnp.logical_not(low)
-                chosen, d_chosen = jnp.where(side, query, 0), jnp.where(side, d_out, 0)
-                scores = attention_scores(chosen, keys[:span], key_bias[0:1], i * SHORT, span)
-                probs = jnp.exp(scores - logs[:, 64 * half : 64 * half + 1])
-                d_probs = lax.dot_general(
-                    d_chosen, values[:span], NT, preferred_element_type=F32
-                )
-                delta = jnp.sum(probs * d_probs, axis=-1, keepdims=True)
-                d_scores = (probs * (d_probs - delta)).astype(BF16)
-                d_query.append(jnp.dot(d_scores, keys[:span], preferred_element_type=F32))
-                d_keys[:span] += lax.dot_general(
-                    d_scores, chosen, TN, preferred_element_type=F32
-                )
-                d_values[:span] += lax.dot_general(
-                    probs.astype(BF16), d_chosen, TN, preferred_element_type=F32
-                )
-            grads = (jnp.where(low, d_query[0], d_query[1]) * root).astype(BF16).astype(F32)
+            query = qkv_low[b, rows]
+            lane = lax.broadcasted_iota(jnp.int32, query.shape, 1)
+            side = lax.div(lane, 64) == half
+            chosen = jnp.where(side, query, 0)
+            d_chosen = jnp.where(side, d_att[b, rows], 0)
+            logs = jnp.max(jnp.where(side, log_sums[b, rows], -1e30), axis=-1, keepdims=True)
+            scores = attention_scores(chosen, keys[:span], key_bias[0:1], i * SHORT, span)
+            probs = jnp.exp(scores - logs)
+            d_probs = lax.dot_general(d_chosen, values[:span], NT, preferred_element_type=F32)
+            delta = jnp.sum(probs * d_probs, axis=-1, keepdims=True)
+            d_scores = (probs * (d_probs - delta)).astype(BF16)
+            d_query = jnp.dot(d_scores, keys[:span], preferred_element_type=F32) * root
+            d_keys[:span] += lax.dot_general(d_scores, chosen, TN, preferred_element_type=F32)
+            d_values[:span] += lax.dot_general(
+                probs.astype(BF16), d_chosen, TN, preferred_element_type=F32
+            )
+            d_low[b, rows] = jnp.where(side, d_query.astype(BF16), d_low[b, rows])
+
+    def unturn_queries(index):
+        rows = pl.ds(pl.multiple_of(index * BLOCK, BLOCK), BLOCK)
+        for b in range(2):
+            grads = d_low[b, rows].astype(F32)
             d_block, gain_term = unturn(0, rows, grads, qkv_raw[b, rows])
             d_low[b, rows] = d_block.astype(BF16)
             gain_g[0:1] += gain_term
 
     row_loop(2, heads)
+    plane.combine(2)
+    end(0)
+    row_loop(2, heads, 2)
+    plane.combine(3)
     end(1)
-    plane.middle(3)
+    row_loop(seq // BLOCK, unturn_queries)
 
     def finish(index):
         rows = pl.ds(pl.multiple_of(index * BLOCK, BLOCK), BLOCK)
@@ -1016,12 +1309,6 @@
 
     row_loop(seq // BLOCK, finish)
 
-    for k, rows in enumerate(parts):
-        layer_out[rows] = (keep[rows] * (middle[rows] + ffn.total(k))).astype(BF16)
-    links.settle(ffn.sends)
-    for device in (place.core_dev, place.y_dev):
-        pl.semaphore_signal(free, inc=1, device_id=device, device_id_type=MESH)
-    pl.semaphore_wait(free, 2)
     dnorm = ReduceCtx(links, place, part, parts, None, from_core2, to_y2, from_y2)
     dnorm.begin()
     normed_load.wait()
@@ -1039,31 +1326,18 @@
     qkv_outs = [SpreadCtx(links, place, qkv_all, [rows]) for rows in qkv_rows]
     for k in range(len(qkv_chunks)):
         qkv_plane.send_x(k)
+    plane.middle(4)
     for k in range(2):
         dnorm.cross(k)
     end(2)
-    plane.middle(4)
     outs[0].forward(0)
+    outs[1].forward(0)
     end(3)
+    for k, rows in enumerate(parts):
+        layer_out[rows] = (keep[rows] * (middle[rows] + ffn.total(k))).astype(BF16)
     plane.middle(5)
-    outs[1].forward(0)
-
-    attn_gain = None
-    x_load.wait()
-    for k, rows in enumerate(parts):
-        grad, term = norm_back(dnorm.total(k), dout_s[rows].astype(F32), gains[0:1])
-        attn_gain = term if attn_gain is None else attn_gain + term
-        input_grad[rows] = (d_middle[rows] + grad).astype(BF16)
-    mine[0:1] = attn_gain
-    mine[1:2] = ffn_gain
-    mine[2:8] = jnp.zeros((6, width), F32)
-    mine[2:3, 0:128] = gain_g[0:1]
-    mine[2:3, 128:256] = gain_g[1:2]
-    plane_slot, ctx_slot = links.slots(8), links.slots(4)
-    for f in fellows:
-        links.send(mine, plane_stats.at[place.f], plane_slot + place.f, (f, place.c))
-    plane_stats[place.f] = mine[...]
-
+    plane.combine(4)
+    outs[2].forward(0)
     links.arrive(out_x, out_slot)
     root_slot, final_slot = links.slots(3), links.slots(1)
     holds = place.z == place.c
@@ -1081,12 +1355,28 @@
     def _():
         to_root.start()
 
+    attn_gain = None
+    for k, rows in enumerate(parts):
+        grad, term = norm_back(dnorm.total(k), x_s[rows].astype(F32), gains[0:1])
+        attn_gain = term if attn_gain is None else attn_gain + term
+        input_grad[rows] = (d_middle[rows] + grad).astype(BF16)
+    mine[...] = jnp.zeros_like(mine)
+    for f in range(8):
+        mine[f, 0:1] = attn_gain[:, 256 * f : 256 * (f + 1)]
+        mine[f, 1:2] = ffn_gain[:, 256 * f : 256 * (f + 1)]
+        mine[f, 2:3, 0:128] = gain_g[0:1]
+        mine[f, 2:3, 128:256] = gain_g[1:2]
+    plane_slot, ctx_slot = links.slots(8), links.slots(4)
+    for f in fellows:
+        links.send(mine.at[f], plane_stats.at[place.f], plane_slot + place.f, (f, place.c))
+    plane_stats[place.f] = mine[place.f]
+
+    end(4)
+    outs[3].forward(0)
     for k in range(len(qkv_chunks)):
         qkv_plane.middle(k)
-    for k in range(4, count):
-        end(k)
-    for k in range(2, 4):
-        outs[k].forward(0)
+    plane.combine(5)
+    end(5)
     for f in fellows:
         links.arrive(plane_stats.at[f], plane_slot + f)
     sums = plane_stats[0]
@@ -1293,49 +1583,61 @@
             pltpu.VMEM((2 * rows, 128), F32),
             pltpu.VMEM((rows, width), BF16),
         ],
-        sems=(90, 100, 32),
+        sems=(170, 170, 32),
         number=0,
     )
     qkv_w = qkv_w.reshape(width, 384)
+    block = pltpu.VMEM((tokens, width), BF16)
+    pair = pltpu.VMEM((2, tokens, width), BF16)
+    whole = pltpu.VMEM((4, tokens, width), BF16)
     hidden_units = units // 4
-    gu_full = gu_w.reshape(width, parts * hidden_units)
-    dn_full = dn_w.reshape(hidden_units, width)
-    mid_full = mid_all.reshape(seq, width)
-    dout_full = dout_all.reshape(seq, width)
-    projected = jnp.dot(mid_full, gu_full, preferred_element_type=F32)
-    gate, up = projected[:, :hidden_units], projected[:, hidden_units:]
-    sigmoid = jax.nn.sigmoid(gate)
-    hidden = (gate * sigmoid * up).astype(BF16)
-    ffn_part = jnp.dot(hidden, dn_full, preferred_element_type=F32).astype(BF16)
-    d_hidden = contract_cols(dout_full, dn_full)
-    d_projected = jnp.concatenate(
+    gu_g, dn_pair, ffn_part, d_middle, branch_s, ffn_gain_part = call(
+        feed_kernel,
+        [(a, HBM) for a in (gu_w, dn_w, dout_all, mid_all, middle)] + [(gains, VMEM)],
         [
-            (d_hidden * up * (sigmoid * (1.0 + gate * (1.0 - sigmoid)))).astype(BF16),
-            (d_hidden * gate * sigmoid).astype(BF16),
+            (shaped((4, 2, rows, width)), HBM),
+            (shaped((4, down_rows, width)), HBM),
+            (shaped((4, tokens, width)), HBM),
+            (shaped((tokens, width), F32), HBM),
+            (shaped((tokens, width)), HBM),
+            (shaped((1, width), F32), VMEM),
         ],
-        axis=1,
-    )
-    dn_g = contract_rows(hidden, dout_full).astype(BF16)
-    gu_g = contract_rows(mid_full, d_projected).astype(BF16)
-    dmid_part = contract_cols(d_projected, gu_full).astype(BF16)
-
+        [
+            pltpu.VMEM((8, rows, width), BF16),
+            pltpu.VMEM((8, down_rows, width), BF16),
+            whole,
+            whole,
+            pltpu.VMEM((seq, hidden_units), BF16),
+            pltpu.VMEM((seq, parts * hidden_units), BF16),
+            pltpu.VMEM((4, 2, down_rows, width), BF16),
+            pltpu.VMEM((4, down_rows, width), BF16),
+            pltpu.VMEM((2, rows, width), BF16),
+            whole,
+            pair,
+            block,
+            block,
+            pltpu.VMEM((tokens, width), F32),
+            block,
+        ],
+        sems=(16, 16, 24),
+        number=2,
+    )
     step = 64
     count = (rows + down_rows) // step
-    block = pltpu.VMEM((tokens, width), BF16)
-    pair = pltpu.VMEM((2, tokens, width), BF16)
     heads = pltpu.VMEM((seq, 128), BF16)
     gu_all, dn_all, layer_out, qkv_all, out_all, input_grad, stats = call(
         backward_kernel,
         [
-            (gu_g.reshape(4, 2, rows, width), HBM),
-            (dn_g.reshape(4, 2, down_rows, width), HBM),
-            (ffn_part.reshape(4, tokens, width), HBM),
-            (dmid_part.reshape(4, tokens, width), HBM),
+            (gu_g, HBM),
+            (dn_pair, HBM),
+            (ffn_part, HBM),
             (middle, HBM),
-            (d_out, HBM),
+            (d_middle, HBM),
+            (branch_s, HBM),
             (source, HBM),
             (keep, VMEM),
             (gains, VMEM),
+            (ffn_gain_part, VMEM),
             (cos, HBM),
             (sin, HBM),
             (head_gain, VMEM),
@@ -1350,13 +1652,14 @@
             (shaped((4, 384, rows)), HBM),
             (shaped((128, width)), VMEM),
             (shaped((tokens, width)), VMEM),
-            (shaped((8, width), F32), VMEM),
+            (shaped((8, rows), F32), VMEM),
         ],
         [
-            pltpu.VMEM((2, 4, step, width), BF16),
-            pltpu.VMEM((count, 4, step, width), BF16),
-            pltpu.VMEM((count, 3, step, width), BF16),
-            pair, pair, block, block, pair, block, block,
+            pltpu.VMEM((4, 4, step, width), BF16),
+            pltpu.VMEM((rows // step, 4, step, width), BF16),
+            pltpu.VMEM((count, 2, step, width), BF16),
+            pltpu.VMEM((count, 2, step, width), BF16),
+            block, pair, block, block, pair, block, block,
             pltpu.VMEM((tokens, width), F32),
             block,
             pltpu.VMEM((tokens, width), F32),
@@ -1383,15 +1686,13 @@
             pltpu.VMEM((2, 128, width), BF16),
             pltpu.VMEM((128, width), BF16),
             pltpu.VMEM((3, 128, width), BF16),
-            pltpu.VMEM((8, width), F32),
-            pltpu.VMEM((8, 8, width), F32),
-            pltpu.VMEM((4, 8, width), F32),
-            pltpu.SemaphoreType.REGULAR,
+            pltpu.VMEM((8, 8, rows), F32),
+            pltpu.VMEM((8, 8, rows), F32),
+            pltpu.VMEM((4, 8, rows), F32),
         ],
         sems=(120, 120, 50),
         number=1,
     )
-    f = lax.axis_index("fsdp")
     qkv_grad = jnp.concatenate(
         [
             jnp.transpose(qkv_all[:, :256], (2, 0, 1)).reshape(rows, query_cols),
@@ -1420,8 +1721,8 @@
         out_all.astype(F32),
         gate_up_grad,
         dn_all.reshape(4 * down_rows, width).astype(F32),
-        lax.dynamic_slice_in_dim(stats[0], f * rows, rows, 0),
-        lax.dynamic_slice_in_dim(stats[1], f * rows, rows, 0),
+        stats[0],
+        stats[1],
         jnp.stack([stats[2, :64] + stats[2, 64:128], stats[2, 128:192]]),
     )
 

time: 542 us -> 490 us (0.904); the launches traced: 531 us -> 487 us
  matrix products: 65.1 us -> 0 us
  Pallas kernels: 441 us -> 464 us
    dot_general x6 -> x0, matrix products: 65.1 us -> none  [the longest x2 23.1 us: contract_cols(): lax.dot_general(left, right, (((1,), (1,)), ((), ())), preferred_element_...]
    pallas_call x2 -> x3, Pallas kernels: 434 us -> 457 us  [call(): pl.pallas_call(kernel, out_shape=tuple((shape for shape, _ in outs)), in_...]
where the time goes in v4:
time: 490 us; the launch traced here: 487 us
  Pallas kernels  464 us (95%)
  local copies, waits for them, and re-layouts  10.8 us (2%)
  other arithmetic  10.5 us (2%)
    pallas_call x3, Pallas kernels, call(): pl.pallas_call(kernel, out_shape=tuple((shape for shape, _ in outs)), in_...  457 us

profile of v4, /device:TPU:13, one launch (start us, length us, event | category | flops | bytes accessed | tf_op | source)
XLA Modules:
  0.0 486.9 jit_solution(1526982184991338991)
XLA Ops:
  0.6 0.0 copy-start
  0.7 1.1 constant_dynamic-slice_fusion.2
  1.8 0.9 constant_dynamic-slice_fusion.3
  2.8 0.8 pad_maximum_fusion.qkv_s
  3.5 0.8 constant_dynamic-slice_fusion.dn_s
  5.1 1.2 fusion.dout_s
  6.3 0.6 broadcast_in_dim.48.key_bias
  6.9 0.1 broadcast_in_dim_tile.4
  7.0 0.1 pad.10.clone
  7.1 0.7 maximum_maximum_fusion.head_gain
  7.8 1.0 copy.31.cos_h
  8.9 1.0 copy.32.sin_h
  9.9 0.1 pad.13.clone
  10.0 0.7 maximum_convert_fusion.1.gain_s
  10.6 175.6 %shard_map.187 = (bf16[8,256,384]{2,1,0:T(8,128)(2,1)}, bf16[2,128,2048]{2,1,0:T(8,128)(2,1)}, f32[8,2048]{1,0:T(8,128)}, bf16[1024,2048]{1,0:T(8,128)(2,1)}, f3...) custom-call(bf16[256,384]{1,0:T(8,128)(2,1)} %pad_maximum_fusion.qkv, ...), custom_call_target="tpu_custom_call" | custom-call | tf_op jit(solution)/shard_map/pallas_call | solution.py:1480
  186.3 75.7 %shard_map.188 = (bf16[4,2,256,2048]{3,2,1,0:T(8,128)(2,1)}, bf16[4,128,2048]{2,1,0:T(8,128)(2,1)}, bf16[4,256,2048]{2,1,0:T(8,128)(2,1)}, f32[256,2048]{1,0:T(8...) custom-call(bf16[8,256,2048]{2,1,0:T(8,128)(2,1)} %get-tuple-element.35.gu_h, ...), custom_call_target="tpu_custom_call" | custom-call | tf_op jit(solution)/shard_map/pallas_call | solution.py:1480
  262.0 0.7 fusion.1.keep
  262.7 205.2 %shard_map.189 = (bf16[4,256,2048]{2,1,0:T(8,128)(2,1)}, bf16[4,128,2048]{2,1,0:T(8,128)(2,1)}, bf16[256,2048]{1,0:T(8,128)(2,1)}, bf16[4,384,256]{2,1,0:T(8,128...) custom-call(bf16[4,2,256,2048]{3,2,1,0:T(8,128)(2,1)} %get-tuple-element.41.gu_g, ...), custom_call_target="tpu_custom_call" | custom-call | tf_op jit(solution)/shard_map/pallas_call | solution.py:1480
  467.9 0.8 slice_add_fusion
  468.7 0.6 pad_maximum_fusion.1
  469.3 7.4 %shard_map.190 = f32[256,2,4096]{2,1,0:T(2,128)} custom-call(bf16[4,256,2048]{2,1,0:T(8,128)(2,1)} %get-tuple-element.58.parts), custom_call_target="tpu_custom_call" | custom-call | tf_op jit(solution)/shard_map/pallas_call | solution.py:1705
  476.7 0.2 copy.36
  476.9 1.1 fusion.3
  478.0 0.1 copy.37
  478.2 0.1 copy.38
  478.3 1.3 maximum_convert_fusion
  479.6 2.7 bitcast_convert_fusion
  482.3 1.1 convert_element_type.51
  483.3 1.3 fusion.4
  484.7 1.0 copy.45
  485.7 1.0 copy.46
  486.6 0.0 copy-done.1
  (36 shorter events, 0.2 us)
Async XLA Ops:
  0.6 2.9 copy-start
  0.7 4.4 copy-start.5
  0.7 6.3 %copy-start.10 = (bf16[2,64]{1,0:T(2,128)(2,1)S(1)}, bf16[2,64]{1,0:T(2,128)(2,1)}, u32[]{:S(2)}) copy-start(bf16[2,64]{1,0:T(2,128)(2,1)} %param.21) | copy-start | bytes 772
  0.7 7.1 %copy-start.9 = (f32[1024,32]{0,1:T(8,128)S(1)}, f32[1024,32]{0,1:T(8,128)}, u32[]{:S(2)}) copy-start(f32[1024,32]{0,1:T(8,128)} %constant.38.clone) | copy-start | bytes 393220
  4.4 4.4 copy-start.8
  6.3 3.6 copy-start.11
  6.3 3.6 copy-start.12
  469.3 7.4 %copy-start.6 = (bf16[4,384,256]{2,1,0:T(8,128)(2,1)S(1)}, bf16[4,384,256]{2,1,0:T(8,128)(2,1)}, u32[]{:S(2)}) copy-start(bf16[4,384,256]{2,1,0:T(8,128)(2,1)} %get-tuple-element.56) | copy-start | bytes 2359300
  476.7 2.9 copy-start.2
  479.6 2.7 copy-start.7
  479.6 5.1 %copy-start.4 = (bf16[256,2048]{1,0:T(8,128)(2,1)S(1)}, bf16[256,2048]{1,0:T(8,128)(2,1)}, u32[]{:S(2)}) copy-start(bf16[256,2048]{1,0:T(8,128)(2,1)} %get-tuple-element.54) | copy-start | bytes 3145732
  482.3 3.4 copy-start.3
  484.7 2.0 copy-start.1

commit v5 on v4

--- a/solution.py
+++ b/solution.py
@@ -664,18 +664,21 @@
 
 class ReduceCtx:
     def __init__(self, links, place, part, parts, own, from_core, to_y, from_y):
-        self.links, self.place, self.part, self.parts = links, place, part, parts
+        self.links, self.place, self.part = links, place, part
+        self.parts = [rows if isinstance(rows, tuple) else (rows,) for rows in parts]
         self.own, self.from_core, self.to_y, self.from_y = own, from_core, to_y, from_y
         self.slot = links.slots(3 * len(parts))
         self.loads, self.sends = {}, []
 
-    def begin(self):
+    def begin(self, only=None):
         place = self.place
         for side, y in ((0, place.yo), (1, place.y)):
             for k, rows in enumerate(self.parts):
+                if only not in (None, k):
+                    continue
                 self.links.send(
-                    self.part.at[y * 2 + place.co, rows],
-                    self.from_core.at[side, rows],
+                    self.part.at[y * 2 + place.co, *rows],
+                    self.from_core.at[side, *rows],
                     self.slot + 3 * k + side,
                     place.core_dev,
                 )
@@ -686,19 +689,19 @@
         rows = self.parts[k]
         y = self.place.y if side else self.place.yo
         self.loads[side, k] = self.links.local(
-            self.part.at[y * 2 + self.place.core, rows], self.own.at[rows]
+            self.part.at[y * 2 + self.place.core, *rows], self.own.at[rows]
         )
 
     def pair(self, side, k):
         rows = self.parts[k]
-        self.links.arrive(self.from_core.at[side, rows], self.slot + 3 * k + side)
+        self.links.arrive(self.from_core.at[side, *rows], self.slot + 3 * k + side)
         if self.own is None:
             y = self.place.y if side else self.place.yo
-            own = self.part[y * 2 + self.place.core, rows]
+            own = self.part[y * 2 + self.place.core, *rows]
         else:
             self.loads[side, k].wait()
             own = self.own[rows]
-        return own.astype(F32) + self.from_core[side, rows].astype(F32)
+        return own.astype(F32) + self.from_core[side, *rows].astype(F32)
 
     def cross(self, k):
         rows = self.parts[k]
@@ -763,11 +766,20 @@
     return jnp.where(columns <= rows, scores, -1e30) + key_bias[:, :span]
 
 
+def turn_tables(angles, cos, sin):
+    for i in range(16):
+        rows = slice(64 * i, 64 * (i + 1))
+        cos_high, sin_high = angles[i : i + 1], angles[16 + i : 17 + i]
+        cos_low, sin_low = angles[32:96], angles[96:160]
+        cos[rows] = cos_high * cos_low - sin_high * sin_low
+        sin[rows] = sin_high * cos_low + cos_high * sin_low
+
+
 def forward_kernel(
-    qkv_s, out_s, gain_s, x_s, gate_up, dn_s, dout_s, cos_h, sin_h, head_gain, key_bias,
+    lengths, qkv_weight, out_s, gain_s, x_s, gate_up, down_weight, cotangent, angles, qk_gain,
     qkv_wh, out_wh, gains, normed_h, qkv_raw_h, qkv_low_h, att_low_h, log_sums_h,
-    gu_w, dn_w, dout_all, middle, mid_all,
-    cos, sin, gain_blocks, qkv_w, out_w, x_all, normed, qkv_raw, qkv_low, att_low, log_sums,
+    gu_w, dn_w, dout_all, middle, mid_all, head_gain, key_bias,
+    kv_pairs, kv_s, dout_s, cos, sin, gain_blocks, qkv_w, out_w, x_all, normed, qkv_raw, qkv_low, att_low, log_sums,
     part, keys, values, from_core, to_y, from_y, mid_low, gu_pairs, gu_rows, gu_s, send_sems, recv_sems, local_sems,
 ):
     place = Place()
@@ -775,9 +787,30 @@
     fellows = [lax.rem(place.f + d, 8) for d in range(1, 8)]
     place.meet([(f, place.c) for f in fellows] + [place.core_dev, place.y_dev])
 
-    qkv_plane = SpreadPlane(links, place, [(qkv_s, lambda f: qkv_w.at[f])])
+    q_columns = pl.ds(pl.multiple_of(256 * place.c, 256), 256)
+    for j in range(2):
+        pair = pl.ds(pl.multiple_of(1024 + 256 * j + 128 * place.y, 128), 128)
+        links.local(qkv_weight.at[:, pair], kv_pairs.at[j]).wait()
+    cot_load = links.local(cotangent, dout_s)
+    low = low_half(kv_pairs.shape[1:])
+    first, second = [], []
+    for j in range(2):
+        value = kv_pairs[j].astype(F32)
+        swapped = pltpu.roll(value, 64, 1)
+        first.append(jnp.where(place.core == 0, value, swapped))
+        second.append(jnp.where(place.core == 0, swapped, value))
+    kv_s[...] = jnp.where(low, first[0], second[1]).astype(BF16)
+    qkv_plane = SpreadPlane(
+        links,
+        place,
+        [
+            (qkv_weight.at[:, q_columns], lambda f: qkv_w.at[f, :, 0:256]),
+            (kv_s, lambda f: qkv_w.at[f, :, 256:384]),
+        ],
+    )
     qkv_plane.begin_z()
     qkv_plane.begin_x(0)
+    qkv_plane.begin_x(1)
     picks = []
     for f in range(8):
         start = pl.multiple_of(512 * f + 128 * place.c, 128)
@@ -791,11 +824,10 @@
     for f in fellows:
         links.send(gain_s, gain_blocks.at[place.f], gain_slot + place.f, (f, place.c))
     kept = [
-        links.local(qkv_s, qkv_w.at[place.f]),
+        links.local(qkv_weight.at[:, q_columns], qkv_w.at[place.f, :, 0:256]),
+        links.local(kv_s, qkv_w.at[place.f, :, 256:384]),
         links.local(gain_s, gain_blocks.at[place.f]),
         links.local(x_s, x_all.at[place.c]),
-        links.local(cos_h, cos),
-        links.local(sin_h, sin),
     ]
 
     root_slot, side_slot = links.slots(1), links.slots(1)
@@ -829,15 +861,21 @@
             gu_s[:, first : first + 128] = picked.astype(BF16)
     step = 32
     chunks = []
+    dn_s = down_weight.at[pl.ds(pl.multiple_of(128 * place.c, 128), dn_w.shape[1])]
     for src, dst in ((dn_s, dn_w), (gu_s, gu_w)):
         for first in range(0, src.shape[0], step):
             rows = pl.ds(first, step)
             chunks.append((src.at[rows], lambda f, dst=dst, rows=rows: dst.at[f, rows]))
     plane = SpreadTree(links, place, chunks)
     plane.begin_z()
+    cot_load.wait()
+    length = lengths[0]
+    positions = tokens * place.c + lax.broadcasted_iota(jnp.int32, (tokens, 1), 0)
+    dout_s[...] = jnp.where(positions < length, dout_s[...].astype(F32), 0.0).astype(BF16)
     for k in range(4):
         plane.begin_x(k)
     qkv_plane.forward(0)
+    qkv_plane.forward(1)
     for k in range(4, len(chunks)):
         plane.begin_x(k)
     last = [
@@ -845,6 +883,15 @@
         links.local(dn_s, dn_w.at[place.f]),
         links.local(dout_s, dout_all.at[place.c]),
     ]
+    turn_tables(angles, cos, sin)
+    columns = lax.broadcasted_iota(jnp.int32, key_bias.shape, 1)
+    key_bias[...] = jnp.where(columns < length, 0.0, -1e30)
+    ones = jnp.ones((1, HEAD_DIM), F32)
+    q_gain, k_gain = qk_gain[0:1].astype(F32), qk_gain[1:2].astype(F32)
+    head_gain[...] = jnp.zeros_like(head_gain)
+    for b in range(2):
+        head_gain[b : b + 1] = jnp.concatenate([q_gain, q_gain], axis=1)
+    head_gain[2:3] = jnp.concatenate([k_gain, ones], axis=1)
     for f in fellows:
         links.arrive(gain_blocks.at[f], gain_slot + f)
     for made in kept:
@@ -917,9 +964,10 @@
     row_loop(2, heads)
     plane.onward(1)
     plane.onward(2)
+    plane.forward(0)
     row_loop(2, heads, 2)
     plane.onward(3)
-    for k in range(3):
+    for k in range(1, 3):
         plane.forward(k)
 
     @pl.when(jnp.logical_not(jnp.logical_or(holds, relays)))
@@ -1014,7 +1062,7 @@
     gu_h, dn_h, dout_h, mid_h, middle_h, gains,
     gu_g, dn_pair, ffn_h, d_middle_h, branch_s, ffn_gain,
     gu_w, dn_w, dout, mid, hidden, d_proj, dn_g, from_x, stage,
-    part, from_core, to_y, from_y, middle, branch, send_sems, recv_sems, local_sems,
+    part, from_core, to_y, from_y, middle, d_norm, branch, send_sems, recv_sems, local_sems,
 ):
     place = Place()
     links = Links(place, send_sems, recv_sems, local_sems)
@@ -1080,10 +1128,14 @@
         columns = pl.ds(pl.multiple_of(rows * f, rows), rows)
         part[:, :, columns] = grad.astype(BF16).reshape(4, tokens, rows)
 
-    row_loop(shards, mid_grad)
     parts = halves(tokens)
-    dmid = ReduceCtx(links, place, part, parts, None, from_core, to_y, from_y)
-    dmid.begin()
+    sides = [(slice(None), side) for side in halves(width)]
+    dmid = ReduceCtx(links, place, part, sides, None, from_core, to_y, from_y)
+    row_loop(shards // 2, mid_grad)
+    dmid.begin(0)
+    row_loop(shards // 2, mid_grad, shards // 2)
+    dmid.begin(1)
+    dmid.cross(0)
 
     def gate_up_grad(z):
         for x in range(2):
@@ -1098,9 +1150,8 @@
         made.wait()
 
     row_loop(1, gate_up_grad)
-    for k in range(2):
-        dmid.cross(k)
-    lax.fori_loop(1, 4, lambda z, carry: (gate_up_grad(z), carry)[1], 0)
+    dmid.cross(1)
+    row_loop(3, gate_up_grad, 1)
     links.locals += 1
 
     def feed_out(index):
@@ -1114,9 +1165,11 @@
     row_loop(4, feed_out)
     later.append(links.local(mid, ffn_h))
     later[0].wait()
+    for k in range(2):
+        d_norm[sides[k]] = dmid.total(k)
     gain_sum = None
     for k, at in enumerate(parts):
-        grad, term = norm_back(dmid.total(k), middle[at], gains[1:2])
+        grad, term = norm_back(d_norm[at], middle[at], gains[1:2])
         gain_sum = term if gain_sum is None else gain_sum + term
         middle[at] = grad + dout[place.c, at].astype(F32)
         branch[at] = middle[at].astype(BF16)
@@ -1134,8 +1187,8 @@
 
 
 def backward_kernel(
-    gu_g, dn_pair, ffn_part, middle_h, d_middle_h, branch_s, x_h, keep, gains, ffn_gain,
-    cos_h, sin_h, head_gain, key_bias,
+    gu_g, dn_pair, ffn_part, middle_h, d_middle_h, branch_s, x_h, lengths, gains, ffn_gain,
+    angles, head_gain, key_bias,
     normed_h, qkv_raw_h, qkv_low_h, att_low_h, log_sums_h, qkv_wh, out_wh,
     gu_all, dn_all, layer_out, qkv_all, out_all, input_grad, stats,
     own, from_x, from_z, via,
@@ -1181,7 +1234,7 @@
     branch = SpreadCtx(links, place, branch_all, parts)
     for k, rows in enumerate(parts):
         branch.begin(k, branch_s.at[rows])
-    for k in (2, 3):
+    for k in range(summed, count - 1):
         plane.send_x(k)
     ffn = ReduceCtx(links, place, ffn_part, parts, ctx_own, from_core1, to_y1, from_y1)
     ffn.begin()
@@ -1192,10 +1245,11 @@
         for a, b in (
             (branch_s, branch_all.at[place.c]),
             (out_wh, out_w), (qkv_low_h, qkv_low), (att_low_h, att_low), (log_sums_h, log_sums),
-            (cos_h, cos), (sin_h, sin), (qkv_raw_h, qkv_raw), (qkv_wh, qkv_w),
+            (qkv_raw_h, qkv_raw), (qkv_wh, qkv_w),
             (middle_h, middle), (d_middle_h, d_middle), (x_h, x_s),
         )
     ]
+    turn_tables(angles, cos, sin)
     gain_g[...] = jnp.zeros_like(gain_g)
     d_keys[...] = jnp.zeros_like(d_keys)
     d_low[...] = jnp.zeros_like(d_low)
@@ -1237,8 +1291,7 @@
             out_g[b, :, columns] = jnp.dot(left, right, preferred_element_type=F32).astype(BF16)
     out_slot = links.slots(1)
     links.send(out_g.at[place.xo], out_x, out_slot, place.x_dev)
-    for k in range(4, count):
-        plane.send_x(k)
+    plane.send_x(count - 1)
     links.settle(branch.sends)
     normed_load = links.local(normed_h, branch_all)
     plane.middle(3)
@@ -1285,6 +1338,7 @@
     plane.combine(2)
     end(0)
     row_loop(2, heads, 2)
+    plane.middle(4)
     plane.combine(3)
     end(1)
     row_loop(seq // BLOCK, unturn_queries)
@@ -1326,18 +1380,6 @@
     qkv_outs = [SpreadCtx(links, place, qkv_all, [rows]) for rows in qkv_rows]
     for k in range(len(qkv_chunks)):
         qkv_plane.send_x(k)
-    plane.middle(4)
-    for k in range(2):
-        dnorm.cross(k)
-    end(2)
-    outs[0].forward(0)
-    outs[1].forward(0)
-    end(3)
-    for k, rows in enumerate(parts):
-        layer_out[rows] = (keep[rows] * (middle[rows] + ffn.total(k))).astype(BF16)
-    plane.middle(5)
-    plane.combine(4)
-    outs[2].forward(0)
     links.arrive(out_x, out_slot)
     root_slot, final_slot = links.slots(3), links.slots(1)
     holds = place.z == place.c
@@ -1355,6 +1397,20 @@
     def _():
         to_root.start()
 
+    for k in range(2):
+        dnorm.cross(k)
+    plane.combine(4)
+    end(2)
+    outs[0].forward(0)
+    outs[1].forward(0)
+    end(3)
+    for k, rows in enumerate(parts):
+        value = middle[rows] + ffn.total(k)
+        positions = lax.broadcasted_iota(jnp.int32, (value.shape[0], 1), 0)
+        positions += tokens * place.c + k * value.shape[0]
+        layer_out[rows] = jnp.where(positions < lengths[0], value, 0.0).astype(BF16)
+    plane.middle(5)
+    outs[2].forward(0)
     attn_gain = None
     for k, rows in enumerate(parts):
         grad, term = norm_back(dnorm.total(k), x_s[rows].astype(F32), gains[0:1])
@@ -1445,8 +1501,11 @@
             made.wait_send()
 
 
-def interleave_kernel(parts, out, pairs, sems):
-    rows = parts.shape[1]
+def finish_kernel(
+    gu_parts, dn_parts, out_s, qkv_parts, layer_s, input_s, stats,
+    out, dn_out, out_out, qkv_out, layer_out, input_out, attn_out, ffn_out, pairs, sems,
+):
+    rows = gu_parts.shape[1]
     first = pl.multiple_of(pl.program_id(0) * rows, rows)
     sent = []
     for c in range(4):
@@ -1454,7 +1513,7 @@
             b = 4 * f + c
             for side in range(2):
                 column = 1024 * side + 128 * f
-                block = parts[c, :, column : column + 128]
+                block = gu_parts[c, :, column : column + 128]
                 pairs[b, pl.ds(side, rows, stride=2), :] = block.astype(F32)
             made = pltpu.make_async_copy(
                 pairs.at[b].reshape(rows, 2, 128),
@@ -1463,6 +1522,24 @@
             )
             made.start()
             sent.append(made)
+    dn_out[...] = dn_parts[...].astype(F32)
+    out_out[...] = out_s[...].astype(F32)
+    layer_out[...] = layer_s[...]
+    input_out[...] = input_s[...]
+
+    @pl.when(pl.program_id(0) == 0)
+    def _():
+        attn_out[...] = stats[0:1]
+        ffn_out[...] = stats[1:2]
+        for c in range(4):
+            qkv_out[:, 256 * c : 256 * (c + 1)] = qkv_parts[c, 0:256].astype(F32).T
+        for y in range(2):
+            for j in range(2):
+                from_row = 256 + 64 * j
+                both = [qkv_parts[2 * y + core, from_row : from_row + 64] for core in range(2)]
+                column = 1024 + 256 * j + 128 * y
+                qkv_out[:, column : column + 128] = jnp.concatenate(both, axis=0).astype(F32).T
+
     for made in sent:
         made.wait()
 
@@ -1501,50 +1578,35 @@
 ):
     tokens, width = inputs.shape[1:]
     seq = tokens * 4
-    c = lax.axis_index("ctx")
-    length = lengths[0]
-    positions = c * tokens + jnp.arange(tokens, dtype=jnp.int32)
-    keep = (positions < length).astype(F32)[:, None]
-    all_positions = jnp.arange(seq, dtype=jnp.int32)
-    key_bias = jnp.broadcast_to(jnp.where(all_positions < length, 0.0, -1e30)[None], (8, seq))
     source = inputs[0]
-    d_out = (keep * cotangent[0].astype(F32)).astype(BF16)
-
-    query_cols, key_cols = HEADS * HEAD_DIM, KV_HEADS * HEAD_DIM
-    qkv_s = jnp.concatenate(
-        [
-            lax.dynamic_slice_in_dim(qkv_weight, c * 256, 256, 1),
-            lax.dynamic_slice_in_dim(qkv_weight, query_cols + c * 64, 64, 1),
-            lax.dynamic_slice_in_dim(qkv_weight, query_cols + key_cols + c * 64, 64, 1),
-        ],
-        axis=1,
-    )
     rows, parts, units = gate_up.shape
     down_rows = down_weight.shape[0] // 4
-    dn_s = lax.dynamic_slice_in_dim(down_weight, c * down_rows, down_rows, 0)
     gain_s = jnp.concatenate(
         [attn_gain[None], ffn_gain[None], jnp.zeros((6, rows), BF16)], axis=0
     ).astype(F32)
 
     half_dim = HEAD_DIM // 2
-    angles = np.arange(seq)[:, None] * 10000.0 ** (-2.0 * np.arange(half_dim) / HEAD_DIM)[None]
-    cos = jnp.tile(jnp.asarray(np.cos(angles), F32), (1, 4))
-    sine = jnp.asarray(np.sin(angles), F32)
-    sin = jnp.tile(jnp.concatenate([-sine, sine], axis=1), (1, 2))
-    q_gain = jnp.tile(qk_gain[0].astype(F32), 2)
-    k_gain = jnp.concatenate([qk_gain[1].astype(F32), jnp.ones((HEAD_DIM,), F32)])
-    head_gain = jnp.concatenate(
-        [q_gain[None], q_gain[None], k_gain[None], jnp.zeros((5, 128), F32)], axis=0
-    )
-
+    frequency = 10000.0 ** (-2.0 * np.arange(half_dim) / HEAD_DIM)
+    turns = [np.arange(0, seq, 64)[:, None] * frequency, np.arange(64)[:, None] * frequency]
+    signs = np.repeat([-1.0, 1.0, -1.0, 1.0], half_dim)
+    angles = jnp.asarray(
+        np.concatenate(
+            [part for t in turns for part in (np.tile(np.cos(t), 4), np.tile(np.sin(t), 4) * signs)]
+        ),
+        F32,
+    )
     table = pltpu.VMEM((seq, 128), F32)
     (
         qkv_w, out_w, gains, normed, qkv_raw, qkv_low, att_low, log_sums,
-        gu_w, dn_w, dout_all, middle, mid_all,
+        gu_w, dn_w, dout_all, middle, mid_all, head_gain, key_bias,
     ) = call(
         forward_kernel,
-        [(a, HBM) for a in (qkv_s, out_weight, gain_s, source, gate_up, dn_s, d_out, cos, sin)]
-        + [(head_gain, VMEM), (key_bias, VMEM)],
+        [(lengths, pl.BlockSpec(memory_space=pltpu.SMEM))]
+        + [
+            (a, HBM)
+            for a in (qkv_weight, out_weight, gain_s, source, gate_up, down_weight, cotangent[0])
+        ]
+        + [(angles, VMEM), (qk_gain, VMEM)],
         [
             (shaped((8, rows, 384)), HBM),
             (shaped((2, out_weight.shape[0], width)), HBM),
@@ -1559,8 +1621,13 @@
             (shaped((4, tokens, width)), HBM),
             (shaped((tokens, width), F32), VMEM),
             (shaped((4, tokens, width)), HBM),
+            (shaped((8, 128), F32), VMEM),
+            (shaped((8, seq), F32), VMEM),
         ],
         [
+            pltpu.VMEM((2, rows, 128), BF16),
+            pltpu.VMEM((rows, 128), BF16),
+            pltpu.VMEM((tokens, width), BF16),
             table,
             table,
             pltpu.VMEM((8, 8, rows), F32),
@@ -1617,6 +1684,7 @@
             block,
             block,
             pltpu.VMEM((tokens, width), F32),
+            pltpu.VMEM((tokens, width), F32),
             block,
         ],
         sems=(16, 16, 24),
@@ -1635,11 +1703,10 @@
             (d_middle, HBM),
             (branch_s, HBM),
             (source, HBM),
-            (keep, VMEM),
+            (lengths, pl.BlockSpec(memory_space=pltpu.SMEM)),
             (gains, VMEM),
             (ffn_gain_part, VMEM),
-            (cos, HBM),
-            (sin, HBM),
+            (angles, VMEM),
             (head_gain, VMEM),
             (key_bias, VMEM),
             (normed.reshape(4, tokens, width), HBM),
@@ -1693,36 +1760,59 @@
         sems=(120, 120, 50),
         number=1,
     )
-    qkv_grad = jnp.concatenate(
-        [
-            jnp.transpose(qkv_all[:, :256], (2, 0, 1)).reshape(rows, query_cols),
-            jnp.transpose(qkv_all[:, 256:320], (2, 0, 1)).reshape(rows, key_cols),
-            jnp.transpose(qkv_all[:, 320:], (2, 0, 1)).reshape(rows, key_cols),
+    some = 64
+    steps = rows // some
+    few = down_rows // steps
+    out_rows = out_weight.shape[0]
+    block_of = lambda n: pl.BlockSpec((n, width), lambda i: (i, 0))
+    fixed = lambda *shape: pl.BlockSpec(shape, lambda i: (0,) * len(shape))
+    gate_up_grad, down_grad, out_grad, qkv_grad, layer_out, input_grad, attn_g, ffn_g = pl.pallas_call(
+        finish_kernel,
+        grid=(steps,),
+        in_specs=[
+            pl.BlockSpec((4, some, width), lambda i: (0, i, 0)),
+            pl.BlockSpec((4, few, width), lambda i: (0, i, 0)),
+            block_of(out_rows // steps),
+            fixed(4, 384, rows),
+            block_of(tokens // steps),
+            block_of(tokens // steps),
+            fixed(8, rows),
         ],
-        axis=1,
-    ).astype(F32)
-    some = 64
-    gate_up_grad = pl.pallas_call(
-        interleave_kernel,
-        grid=(rows // some,),
-        in_specs=[pl.BlockSpec((4, some, width), lambda i: (0, i, 0))],
-        out_specs=HBM,
-        out_shape=shaped((rows, parts, units), F32),
+        out_specs=[
+            HBM,
+            pl.BlockSpec((4, few, width), lambda i: (0, i, 0)),
+            block_of(out_rows // steps),
+            fixed(rows, qkv_weight.shape[1]),
+            block_of(tokens // steps),
+            block_of(tokens // steps),
+            fixed(1, rows),
+            fixed(1, rows),
+        ],
+        out_shape=[
+            shaped((rows, parts, units), F32),
+            shaped((4, down_rows, width), F32),
+            shaped((out_rows, width), F32),
+            shaped((rows, qkv_weight.shape[1]), F32),
+            shaped((tokens, width)),
+            shaped((tokens, width)),
+            shaped((1, rows), F32),
+            shaped((1, rows), F32),
+        ],
         scratch_shapes=[
             pltpu.VMEM((32, 2 * some, 128), F32),
             pltpu.SemaphoreType.DMA((32,)),
         ],
         compiler_params=pltpu.CompilerParams(vmem_limit_bytes=VMEM_BYTES),
-    )(gu_all)
+    )(gu_all, dn_all, out_all, qkv_all, layer_out, input_grad, stats)
     return (
         layer_out[None],
         input_grad[None],
         qkv_grad,
-        out_all.astype(F32),
+        out_grad,
         gate_up_grad,
-        dn_all.reshape(4 * down_rows, width).astype(F32),
-        stats[0],
-        stats[1],
+        down_grad.reshape(4 * down_rows, width),
+        attn_g[0],
+        ffn_g[0],
         jnp.stack([stats[2, :64] + stats[2, 64:128], stats[2, 128:192]]),
     )
 

time: 490 us -> 454 us (0.927)
  Pallas kernels: 464 us -> 446 us
  local copies, waits for them, and re-layouts: 10.8 us -> 1.4 us
  other arithmetic: 10.5 us -> 2.07 us
    pallas_call x3, Pallas kernels: 457 us -> 435 us  [call(): pl.pallas_call(kernel, out_shape=tuple((shape for shape, _ in outs)), in_...]
    convert_element_type x6 -> x0, other arithmetic: 6.95 us -> none  [the longest x1 2.68 us: split_heads(): dn_all.reshape(4 * down_rows, width).astype(F32)]
where the time goes in v5:
time: 454 us; the launch traced here: 451 us
  Pallas kernels  446 us (98%)
    pallas_call x3, Pallas kernels, call(): pl.pallas_call(kernel, out_shape=tuple((shape for shape, _ in outs)), in_...  435 us
    pallas_call x1, Pallas kernels, split_heads(): pl.pallas_call(finish_kernel, grid=(steps,), in_specs=[pl.BlockSpec((4, s...  11.5 us

profile of v5, /device:TPU:13, one launch (start us, length us, event | category | flops | bytes accessed | tf_op | source)
XLA Modules:
  0.0 451.5 jit_solution(8565901739879212515)
XLA Ops:
  1.3 0.1 pad.4.clone
  1.4 0.7 broadcast_in_dim.15
  2.0 0.7 broadcast_in_dim.16
  2.7 0.7 maximum_convert_fusion.gain_s
  3.4 177.6 %shard_map.178 = (bf16[8,256,384]{2,1,0:T(8,128)(2,1)}, bf16[2,128,2048]{2,1,0:T(8,128)(2,1)}, f32[8,2048]{1,0:T(8,128)}, bf16[1024,2048]{1,0:T(8,128)(2,1)}, f3...) custom-call(s32[1]{0:T(128)S(6)} %copy.20.lengths, ...), custom_call_target="tpu_custom_call" | custom-call | tf_op jit(solution)/shard_map/pallas_call | solution.py:1557
  180.9 72.9 %shard_map.179 = (bf16[4,2,256,2048]{3,2,1,0:T(8,128)(2,1)}, bf16[4,128,2048]{2,1,0:T(8,128)(2,1)}, bf16[4,256,2048]{2,1,0:T(8,128)(2,1)}, f32[256,2048]{1,0:T(8...) custom-call(bf16[8,256,2048]{2,1,0:T(8,128)(2,1)} %get-tuple-element.45.gu_h, ...), custom_call_target="tpu_custom_call" | custom-call | tf_op jit(solution)/shard_map/pallas_call | solution.py:1557
  253.8 184.5 %shard_map.180 = (bf16[4,256,2048]{2,1,0:T(8,128)(2,1)}, bf16[4,128,2048]{2,1,0:T(8,128)(2,1)}, bf16[256,2048]{1,0:T(8,128)(2,1)}, bf16[4,384,256]{2,1,0:T(8,128...) custom-call(bf16[4,2,256,2048]{3,2,1,0:T(8,128)(2,1)} %get-tuple-element.51.gu_g, ...), custom_call_target="tpu_custom_call" | custom-call | tf_op jit(solution)/shard_map/pallas_call | solution.py:1557
  438.4 0.8 slice_add_fusion
  439.2 0.6 pad_maximum_fusion
  439.8 11.5 %shard_map.181 = (f32[256,2,4096]{2,1,0:T(2,128)}, f32[4,128,2048]{2,1,0:T(8,128)}, f32[128,2048]{1,0:T(8,128)}, f32[256,1536]{1,0:T(8,128)}, bf16[256,2048]{1,0...) custom-call(bf16[4,256,2048]{2,1,0:T(8,128)(2,1)} %get-tuple-element.66.gu_parts, ...), custom_call_target="tpu_custom_call" | custom-call | tf_op jit(solution)/shard_map/pallas_call | solution.py:1769
  (1 shorter events, 0.0 us)

commit v6 on v5

--- a/solution.py
+++ b/solution.py
@@ -452,17 +452,43 @@
 
 
 class SpreadTree(SpreadPlane):
-    def begin_z(self):
+    def __init__(self, links, place, chunks, crossed):
+        super().__init__(links, place, chunks)
+        self.plain = len(chunks) - crossed
+        self.passed = []
+
+    def begin_z(self, ahead=4):
         place = self.place
-        self.passed = []
+        self.near = {}
         for k, (src, dst) in enumerate(self.chunks):
             slot = self.z_slot + 4 * k + place.z
-            for other in place.others[:2]:
-                self.links.send(src, dst(place.f), slot, place.z_dev(other))
+            near = self.links.copy(src, dst(place.f), slot, place.z_dev(place.others[0]))
+            self.links.open.append(near)
+            if k < ahead:
+                near.start()
+            else:
+                pl.when(jnp.logical_not(place.inner))(near.start)
+                self.near[k - ahead] = near
+            self.links.send(src, dst(place.f), slot, place.z_dev(place.others[1]))
+
+    def cross_z(self, k):
+        place = self.place
+        block = self.chunks[k][1](place.z * 2 + place.xo)
+        slot = self.x_slot + 4 * k + place.z
+        self.links.arrive(block, slot)
+        for other in place.others[:2]:
+            self.links.send(block, block, slot, place.z_dev(other))
+
+    def blocks(self, k, other):
+        place, dst = self.place, self.chunks[k][1]
+        found = [(dst(other * 2 + place.x), self.z_slot + 4 * k + other)]
+        if k >= self.plain:
+            found.append((dst(other * 2 + place.xo), self.x_slot + 4 * k + other))
+        return found
 
     def onward(self, k):
-        place, dst = self.place, self.chunks[k][1]
-        blocks = [(dst(o * 2 + place.x), self.z_slot + 4 * k + o) for o in place.others[1:]]
+        place = self.place
+        blocks = [pair for other in place.others[1:] for pair in self.blocks(k, other)]
         made = [
             self.links.copy(block, block, slot, place.z_dev(place.others[0]))
             for block, slot in blocks
@@ -474,21 +500,33 @@
             for (block, slot), one in zip(blocks, made):
                 self.links.arrive(block, slot)
                 one.start()
+            if k in self.near:
+                self.near[k].start()
 
     def forward(self, k):
-        place, dst = self.place, self.chunks[k][1]
-        blocks = [(dst(o * 2 + place.x), self.z_slot + 4 * k + o) for o in place.others]
-        self.links.arrive(*blocks[0])
-        near = self.x_slot + 4 * k + place.others[0]
-        self.links.send(blocks[0][0], blocks[0][0], near, place.x_dev)
+        place = self.place
+        near, *far = [self.blocks(k, other) for other in place.others]
+        far = far[0] + far[1]
+        for pair in near:
+            self.links.arrive(*pair)
+        if k < self.plain:
+            slot = self.x_slot + 4 * k + place.others[0]
+            self.links.send(near[0][0], near[0][0], slot, place.x_dev)
 
         @pl.when(jnp.logical_not(place.inner))
         def _():
-            for block, slot in blocks[1:]:
-                self.links.arrive(block, slot)
-
-        for other, (block, _) in zip(place.others[1:], blocks[1:]):
-            self.links.send(block, block, self.x_slot + 4 * k + other, place.x_dev)
+            for pair in far:
+                self.links.arrive(*pair)
+
+        if k < self.plain:
+            for other, (block, _) in zip(place.others[1:], far):
+                self.links.send(block, block, self.x_slot + 4 * k + other, place.x_dev)
+
+    def end(self):
+        for k in range(self.plain):
+            for z in range(4):
+                block = self.chunks[k][1](z * 2 + self.place.xo)
+                self.links.arrive(block, self.x_slot + 4 * k + z)
 
     def finish(self):
         @pl.when(self.place.inner)
@@ -866,18 +904,22 @@
         for first in range(0, src.shape[0], step):
             rows = pl.ds(first, step)
             chunks.append((src.at[rows], lambda f, dst=dst, rows=rows: dst.at[f, rows]))
-    plane = SpreadTree(links, place, chunks)
+    plane = SpreadTree(links, place, chunks, 2)
     plane.begin_z()
     cot_load.wait()
     length = lengths[0]
     positions = tokens * place.c + lax.broadcasted_iota(jnp.int32, (tokens, 1), 0)
     dout_s[...] = jnp.where(positions < length, dout_s[...].astype(F32), 0.0).astype(BF16)
-    for k in range(4):
+    for k in range(plane.plain, len(chunks)):
+        plane.begin_x(k)
+    for k in range(3):
         plane.begin_x(k)
     qkv_plane.forward(0)
     qkv_plane.forward(1)
-    for k in range(4, len(chunks)):
+    for k in range(3, plane.plain):
         plane.begin_x(k)
+    for k in range(plane.plain, len(chunks)):
+        plane.cross_z(k)
     last = [
         links.local(gu_s, gu_w.at[place.f]),
         links.local(dn_s, dn_w.at[place.f]),
@@ -1015,13 +1057,15 @@
         mid_low[rows] = (value * row_factor(value) * gains[1:2]).astype(BF16)
         mid.begin(k, mid_low.at[rows])
         last.append(links.local(mid_low.at[rows], mid_all.at[place.c, rows]))
-    for k in range(9, len(chunks)):
-        plane.onward(k)
+    plane.onward(9)
     plane.forward(7)
     plane.forward(8)
     for k in range(2):
         mid.forward(k)
-    for k in range(9, len(chunks)):
+    plane.forward(9)
+    for k in range(plane.plain, len(chunks)):
+        plane.onward(k)
+    for k in range(plane.plain, len(chunks)):
         plane.forward(k)
     plane.end()
     mid.end()
@@ -1650,7 +1694,7 @@
             pltpu.VMEM((2 * rows, 128), F32),
             pltpu.VMEM((rows, width), BF16),
         ],
-        sems=(170, 170, 32),
+        sems=(180, 170, 32),
         number=0,
     )
     qkv_w = qkv_w.reshape(width, 384)

time: 454 us -> 435 us (0.958)
  Pallas kernels: 446 us -> 427 us
    pallas_call x3, Pallas kernels: 435 us -> 416 us  [call(): pl.pallas_call(kernel, out_shape=tuple((shape for shape, _ in outs)), in_...]
where the time goes in v6:
time: 435 us; the launch traced here: 432 us
  Pallas kernels  427 us (98%)
    pallas_call x3, Pallas kernels, call(): pl.pallas_call(kernel, out_shape=tuple((shape for shape, _ in outs)), in_...  416 us
    pallas_call x1, Pallas kernels, split_heads(): pl.pallas_call(finish_kernel, grid=(steps,), in_specs=[pl.BlockSpec((4, s...  11.5 us

profile of v6, /device:TPU:13, one launch (start us, length us, event | category | flops | bytes accessed | tf_op | source)
XLA Modules:
  0.0 432.0 jit_solution(12288522146638826781)
XLA Ops:
  1.3 0.1 pad.4.clone
  1.4 0.7 broadcast_in_dim.15
  2.0 0.7 broadcast_in_dim.16
  2.7 0.7 maximum_convert_fusion.gain_s
  3.4 173.0 %shard_map.178 = (bf16[8,256,384]{2,1,0:T(8,128)(2,1)}, bf16[2,128,2048]{2,1,0:T(8,128)(2,1)}, f32[8,2048]{1,0:T(8,128)}, bf16[1024,2048]{1,0:T(8,128)(2,1)}, f3...) custom-call(s32[1]{0:T(128)S(6)} %copy.20.lengths, ...), custom_call_target="tpu_custom_call" | custom-call | tf_op jit(solution)/shard_map/pallas_call | solution.py:1601
  176.4 66.5 %shard_map.179 = (bf16[4,2,256,2048]{3,2,1,0:T(8,128)(2,1)}, bf16[4,128,2048]{2,1,0:T(8,128)(2,1)}, bf16[4,256,2048]{2,1,0:T(8,128)(2,1)}, f32[256,2048]{1,0:T(8...) custom-call(bf16[8,256,2048]{2,1,0:T(8,128)(2,1)} %get-tuple-element.45.gu_h, ...), custom_call_target="tpu_custom_call" | custom-call | tf_op jit(solution)/shard_map/pallas_call | solution.py:1601
  242.8 176.1 %shard_map.180 = (bf16[4,256,2048]{2,1,0:T(8,128)(2,1)}, bf16[4,128,2048]{2,1,0:T(8,128)(2,1)}, bf16[256,2048]{1,0:T(8,128)(2,1)}, bf16[4,384,256]{2,1,0:T(8,128...) custom-call(bf16[4,2,256,2048]{3,2,1,0:T(8,128)(2,1)} %get-tuple-element.51.gu_g, ...), custom_call_target="tpu_custom_call" | custom-call | tf_op jit(solution)/shard_map/pallas_call | solution.py:1601
  418.9 0.8 slice_add_fusion
  419.8 0.6 pad_maximum_fusion
  420.3 11.5 %shard_map.181 = (f32[256,2,4096]{2,1,0:T(2,128)}, f32[4,128,2048]{2,1,0:T(8,128)}, f32[128,2048]{1,0:T(8,128)}, f32[256,1536]{1,0:T(8,128)}, bf16[256,2048]{1,0...) custom-call(bf16[4,256,2048]{2,1,0:T(8,128)(2,1)} %get-tuple-element.66.gu_parts, ...), custom_call_target="tpu_custom_call" | custom-call | tf_op jit(solution)/shard_map/pallas_call | solution.py:1813
  (1 shorter events, 0.0 us)

commit v7 on v6

--- a/solution.py
+++ b/solution.py
@@ -1135,7 +1135,8 @@
         gate_columns, up_columns = slice(256 * n, 256 * (n + 1)), slice(units + 256 * n, units + 256 * (n + 1))
 
         def activation(index, gate_columns=gate_columns, up_columns=up_columns, n=n):
-            low = mid[index]
+            two = pl.ds(2 * index, 2)
+            low = mid[two].reshape(2 * tokens, width)
             gate = jnp.dot(
                 low, gu_w[:, :, gate_columns].reshape(width, 256), preferred_element_type=F32
             )
@@ -1143,10 +1144,10 @@
                 low, gu_w[:, :, up_columns].reshape(width, 256), preferred_element_type=F32
             )
             d_hidden = lax.dot_general(
-                dout[index], dn_w[2 * n : 2 * n + 2].reshape(256, width), NT,
+                dout[two].reshape(2 * tokens, width), dn_w[2 * n : 2 * n + 2].reshape(256, width), NT,
                 preferred_element_type=F32,
             )
-            at = pl.ds(pl.multiple_of(index * tokens, tokens), tokens)
+            at = pl.ds(pl.multiple_of(index * 2 * tokens, 2 * tokens), 2 * tokens)
             sigmoid = 1.0 / (1.0 + jnp.exp(-gate))
             silu = gate * sigmoid
             hidden[at, gate_columns] = (silu * up).astype(BF16)
@@ -1154,7 +1155,7 @@
             d_proj[at, gate_columns] = d_gate.astype(BF16)
             d_proj[at, up_columns] = (d_hidden * silu).astype(BF16)
 
-        row_loop(4, activation)
+        row_loop(2, activation)
         left = hidden[:, gate_columns].T
 
         def down_grad(j, left=left, n=n):
@@ -1175,20 +1176,21 @@
     parts = halves(tokens)
     sides = [(slice(None), side) for side in halves(width)]
     dmid = ReduceCtx(links, place, part, sides, None, from_core, to_y, from_y)
-    row_loop(shards // 2, mid_grad)
+    quarter = shards // 4
+    row_loop(2 * quarter, mid_grad)
     dmid.begin(0)
-    row_loop(shards // 2, mid_grad, shards // 2)
+    row_loop(quarter, mid_grad, 2 * quarter)
+    dmid.cross(0)
+    row_loop(quarter, mid_grad, 3 * quarter)
     dmid.begin(1)
-    dmid.cross(0)
 
     def gate_up_grad(z):
-        for x in range(2):
-            columns = pl.ds(pl.multiple_of(2 * rows * z + rows * x, rows), rows)
-            left = mid[:, :, columns].reshape(seq, rows).T
-            for j in range(4):
-                wide = slice(512 * j, 512 * (j + 1))
-                grad = jnp.dot(left, d_proj[:, wide], preferred_element_type=F32)
-                stage[x, :, wide] = grad.astype(BF16)
+        columns = pl.ds(pl.multiple_of(2 * rows * z, 2 * rows), 2 * rows)
+        left = mid[:, :, columns].reshape(seq, 2 * rows).T
+        for j in range(4):
+            wide = slice(512 * j, 512 * (j + 1))
+            grad = jnp.dot(left, d_proj[:, wide], preferred_element_type=F32)
+            stage[:, :, wide] = grad.astype(BF16).reshape(2, rows, 512)
         made = pltpu.make_async_copy(stage, gu_g.at[z], local_sems.at[links.locals])
         made.start()
         made.wait()
@@ -1199,14 +1201,14 @@
     links.locals += 1
 
     def feed_out(index):
-        at = pl.ds(pl.multiple_of(index * tokens, tokens), tokens)
+        at = pl.ds(pl.multiple_of(index * 2 * tokens, 2 * tokens), 2 * tokens)
         for j in range(4):
             wide = slice(512 * j, 512 * (j + 1))
             right = dn_w[:, :, wide].reshape(units, 512)
             sums = jnp.dot(hidden[at], right, preferred_element_type=F32)
-            mid[index, :, wide] = sums.astype(BF16)
-
-    row_loop(4, feed_out)
+            mid[pl.ds(2 * index, 2), :, wide] = sums.astype(BF16).reshape(2, tokens, 512)
+
+    row_loop(2, feed_out)
     later.append(links.local(mid, ffn_h))
     later[0].wait()
     for k in range(2):

time: 435 us -> 431 us (level)
  no operation moved by 1% of the time
where the time goes in v7:
time: 431 us; the launch traced here: 429 us
  Pallas kernels  424 us (98%)
    pallas_call x3, Pallas kernels, call(): pl.pallas_call(kernel, out_shape=tuple((shape for shape, _ in outs)), in_...  412 us
    pallas_call x1, Pallas kernels, split_heads(): pl.pallas_call(finish_kernel, grid=(steps,), in_specs=[pl.BlockSpec((4, s...  11.5 us

profile of v7, /device:TPU:13, one launch (start us, length us, event | category | flops | bytes accessed | tf_op | source)
XLA Modules:
  0.0 428.8 jit_solution(6325862120459303591)
XLA Ops:
  1.3 0.1 pad.4.clone
  1.4 0.7 broadcast_in_dim.15
  2.0 0.7 broadcast_in_dim.16
  2.7 0.7 maximum_convert_fusion.gain_s
  3.4 173.0 %shard_map.178 = (bf16[8,256,384]{2,1,0:T(8,128)(2,1)}, bf16[2,128,2048]{2,1,0:T(8,128)(2,1)}, f32[8,2048]{1,0:T(8,128)}, bf16[1024,2048]{1,0:T(8,128)(2,1)}, f3...) custom-call(s32[1]{0:T(128)S(6)} %copy.20.lengths, ...), custom_call_target="tpu_custom_call" | custom-call | tf_op jit(solution)/shard_map/pallas_call | solution.py:1603
  176.4 64.6 %shard_map.179 = (bf16[4,2,256,2048]{3,2,1,0:T(8,128)(2,1)}, bf16[4,128,2048]{2,1,0:T(8,128)(2,1)}, bf16[4,256,2048]{2,1,0:T(8,128)(2,1)}, f32[256,2048]{1,0:T(8...) custom-call(bf16[8,256,2048]{2,1,0:T(8,128)(2,1)} %get-tuple-element.45.gu_h, ...), custom_call_target="tpu_custom_call" | custom-call | tf_op jit(solution)/shard_map/pallas_call | solution.py:1603
  241.0 174.6 %shard_map.180 = (bf16[4,256,2048]{2,1,0:T(8,128)(2,1)}, bf16[4,128,2048]{2,1,0:T(8,128)(2,1)}, bf16[256,2048]{1,0:T(8,128)(2,1)}, bf16[4,384,256]{2,1,0:T(8,128...) custom-call(bf16[4,2,256,2048]{3,2,1,0:T(8,128)(2,1)} %get-tuple-element.51.gu_g, ...), custom_call_target="tpu_custom_call" | custom-call | tf_op jit(solution)/shard_map/pallas_call | solution.py:1603
  415.6 0.8 slice_add_fusion
  416.5 0.6 pad_maximum_fusion
  417.0 11.5 %shard_map.181 = (f32[256,2,4096]{2,1,0:T(2,128)}, f32[4,128,2048]{2,1,0:T(8,128)}, f32[128,2048]{1,0:T(8,128)}, f32[256,1536]{1,0:T(8,128)}, bf16[256,2048]{1,0...) custom-call(bf16[4,256,2048]{2,1,0:T(8,128)(2,1)} %get-tuple-element.66.gu_parts, ...), custom_call_target="tpu_custom_call" | custom-call | tf_op jit(solution)/shard_map/pallas_call | solution.py:1815
  (1 shorter events, 0.0 us)

commit v8 on v7

--- a/solution.py
+++ b/solution.py
@@ -1280,7 +1280,7 @@
     branch = SpreadCtx(links, place, branch_all, parts)
     for k, rows in enumerate(parts):
         branch.begin(k, branch_s.at[rows])
-    for k in range(summed, count - 1):
+    for k in range(summed, count - 2):
         plane.send_x(k)
     ffn = ReduceCtx(links, place, ffn_part, parts, ctx_own, from_core1, to_y1, from_y1)
     ffn.begin()
@@ -1300,15 +1300,20 @@
     d_keys[...] = jnp.zeros_like(d_keys)
     d_low[...] = jnp.zeros_like(d_low)
     d_values[...] = jnp.zeros_like(d_values)
-    plane.middle(0)
-    plane.middle(1)
+    for k in (0, 1):
+        plane.middle(k)
+    for k in (2, 3):
+        plane.middle(k)
     for k in range(2):
         ffn.cross(k)
     branch.forward(0)
-    plane.combine(0)
+    for k in (0, 1):
+        plane.combine(k)
     branch.forward(1)
-    plane.middle(2)
-    plane.combine(1)
+    for k in (4, 5):
+        plane.middle(k)
+    for k in (2, 3):
+        plane.combine(k)
     branch.end()
     for made in late:
         made.wait()
@@ -1337,10 +1342,12 @@
             out_g[b, :, columns] = jnp.dot(left, right, preferred_element_type=F32).astype(BF16)
     out_slot = links.slots(1)
     links.send(out_g.at[place.xo], out_x, out_slot, place.x_dev)
-    plane.send_x(count - 1)
+    for k in range(count - 2, count):
+        plane.send_x(k)
     links.settle(branch.sends)
     normed_load = links.local(normed_h, branch_all)
-    plane.middle(3)
+    for k in (6, 7):
+        plane.middle(k)
 
     def unturn(row, rows, grads, block):
         back = grads * cos[rows] + partner(grads * sin[rows])
@@ -1381,12 +1388,17 @@
             gain_g[0:1] += gain_term
 
     row_loop(2, heads)
-    plane.combine(2)
-    end(0)
+    for k in (4, 5):
+        plane.combine(k)
+    for k in (0, 1):
+        end(k)
     row_loop(2, heads, 2)
-    plane.middle(4)
-    plane.combine(3)
-    end(1)
+    for k in (8, 9):
+        plane.middle(k)
+    for k in (6, 7):
+        plane.combine(k)
+    for k in (2, 3):
+        end(k)
     row_loop(seq // BLOCK, unturn_queries)
 
     def finish(index):
@@ -1445,18 +1457,25 @@
 
     for k in range(2):
         dnorm.cross(k)
-    plane.combine(4)
-    end(2)
-    outs[0].forward(0)
-    outs[1].forward(0)
-    end(3)
+    for k in (8, 9):
+        plane.combine(k)
+    for k in (4, 5):
+        end(k)
+    for k in (0, 1):
+        outs[k].forward(0)
+    for k in (2, 3):
+        outs[k].forward(0)
+    for k in (6, 7):
+        end(k)
     for k, rows in enumerate(parts):
         value = middle[rows] + ffn.total(k)
         positions = lax.broadcasted_iota(jnp.int32, (value.shape[0], 1), 0)
         positions += tokens * place.c + k * value.shape[0]
         layer_out[rows] = jnp.where(positions < lengths[0], value, 0.0).astype(BF16)
-    plane.middle(5)
-    outs[2].forward(0)
+    for k in (10, 11):
+        plane.middle(k)
+    for k in (4, 5):
+        outs[k].forward(0)
     attn_gain = None
     for k, rows in enumerate(parts):
         grad, term = norm_back(dnorm.total(k), x_s[rows].astype(F32), gains[0:1])
@@ -1473,12 +1492,16 @@
         links.send(mine.at[f], plane_stats.at[place.f], plane_slot + place.f, (f, place.c))
     plane_stats[place.f] = mine[place.f]
 
-    end(4)
-    outs[3].forward(0)
+    for k in (8, 9):
+        end(k)
+    for k in (6, 7):
+        outs[k].forward(0)
     for k in range(len(qkv_chunks)):
         qkv_plane.middle(k)
-    plane.combine(5)
-    end(5)
+    for k in (10, 11):
+        plane.combine(k)
+    for k in (10, 11):
+        end(k)
     for f in fellows:
         links.arrive(plane_stats.at[f], plane_slot + f)
     sums = plane_stats[0]
@@ -1508,7 +1531,7 @@
         total = qkv_plane.end(k)
         qkv_outs[k].begin(0, total)
         kept.append(links.local(total, qkv_all.at[place.c, qkv_rows[k]]))
-    for k in range(4, count):
+    for k in range(8, count):
         outs[k].forward(0)
     relays = place.c_y == place.z
 
@@ -1736,7 +1759,7 @@
         sems=(16, 16, 24),
         number=2,
     )
-    step = 64
+    step = 32
     count = (rows + down_rows) // step
     heads = pltpu.VMEM((seq, 128), BF16)
     gu_all, dn_all, layer_out, qkv_all, out_all, input_grad, stats = call(
@@ -1768,7 +1791,7 @@
             (shaped((8, rows), F32), VMEM),
         ],
         [
-            pltpu.VMEM((4, 4, step, width), BF16),
+            pltpu.VMEM((8, 4, step, width), BF16),
             pltpu.VMEM((rows // step, 4, step, width), BF16),
             pltpu.VMEM((count, 2, step, width), BF16),
             pltpu.VMEM((count, 2, step, width), BF16),
@@ -1803,7 +1826,7 @@
             pltpu.VMEM((8, 8, rows), F32),
             pltpu.VMEM((4, 8, rows), F32),
         ],
-        sems=(120, 120, 50),
+        sems=(190, 190, 70),
         number=1,
     )
     some = 64

time: 431 us -> 429 us (level)
  no operation moved by 1% of the time
where the time goes in v8:
time: 429 us; the launch traced here: 426 us
  Pallas kernels  421 us (98%)
    pallas_call x3, Pallas kernels, call(): pl.pallas_call(kernel, out_shape=tuple((shape for shape, _ in outs)), in_...  410 us
    pallas_call x1, Pallas kernels, split_heads(): pl.pallas_call(finish_kernel, grid=(steps,), in_specs=[pl.BlockSpec((4, s...  11.5 us

profile of v8, /device:TPU:13, one launch (start us, length us, event | category | flops | bytes accessed | tf_op | source)
XLA Modules:
  0.0 426.3 jit_solution(1838509044227259792)
XLA Ops:
  1.3 0.1 pad.4.clone
  1.4 0.7 broadcast_in_dim.15
  2.0 0.7 broadcast_in_dim.16
  2.7 0.7 maximum_convert_fusion.gain_s
  3.4 173.0 %shard_map.178 = (bf16[8,256,384]{2,1,0:T(8,128)(2,1)}, bf16[2,128,2048]{2,1,0:T(8,128)(2,1)}, f32[8,2048]{1,0:T(8,128)}, bf16[1024,2048]{1,0:T(8,128)(2,1)}, f3...) custom-call(s32[1]{0:T(128)S(6)} %copy.20.lengths, ...), custom_call_target="tpu_custom_call" | custom-call | tf_op jit(solution)/shard_map/pallas_call | solution.py:1626
  176.4 64.6 %shard_map.179 = (bf16[4,2,256,2048]{3,2,1,0:T(8,128)(2,1)}, bf16[4,128,2048]{2,1,0:T(8,128)(2,1)}, bf16[4,256,2048]{2,1,0:T(8,128)(2,1)}, f32[256,2048]{1,0:T(8...) custom-call(bf16[8,256,2048]{2,1,0:T(8,128)(2,1)} %get-tuple-element.45.gu_h, ...), custom_call_target="tpu_custom_call" | custom-call | tf_op jit(solution)/shard_map/pallas_call | solution.py:1626
  241.0 172.1 %shard_map.180 = (bf16[4,256,2048]{2,1,0:T(8,128)(2,1)}, bf16[4,128,2048]{2,1,0:T(8,128)(2,1)}, bf16[256,2048]{1,0:T(8,128)(2,1)}, bf16[4,384,256]{2,1,0:T(8,128...) custom-call(bf16[4,2,256,2048]{3,2,1,0:T(8,128)(2,1)} %get-tuple-element.51.gu_g, ...), custom_call_target="tpu_custom_call" | custom-call | tf_op jit(solution)/shard_map/pallas_call | solution.py:1626
  413.1 0.8 slice_add_fusion
  414.0 0.6 pad_maximum_fusion
  414.5 11.5 %shard_map.181 = (f32[256,2,4096]{2,1,0:T(2,128)}, f32[4,128,2048]{2,1,0:T(8,128)}, f32[128,2048]{1,0:T(8,128)}, f32[256,1536]{1,0:T(8,128)}, bf16[256,2048]{1,0...) custom-call(bf16[4,256,2048]{2,1,0:T(8,128)(2,1)} %get-tuple-element.66.gu_parts, ...), custom_call_target="tpu_custom_call" | custom-call | tf_op jit(solution)/shard_map/pallas_call | solution.py:1838
  (1 shorter events, 0.0 us)

commit v9 on v8

--- a/solution.py
+++ b/solution.py
@@ -1492,14 +1492,14 @@
         links.send(mine.at[f], plane_stats.at[place.f], plane_slot + place.f, (f, place.c))
     plane_stats[place.f] = mine[place.f]
 
+    qkv_plane.middle(0)
+    for k in (10, 11):
+        plane.combine(k)
+    qkv_plane.middle(1)
     for k in (8, 9):
         end(k)
     for k in (6, 7):
         outs[k].forward(0)
-    for k in range(len(qkv_chunks)):
-        qkv_plane.middle(k)
-    for k in (10, 11):
-        plane.combine(k)
     for k in (10, 11):
         end(k)
     for f in fellows:

time: 429 us -> 424 us (0.988)
  Pallas kernels: 421 us -> 416 us
    pallas_call x3, Pallas kernels: 410 us -> 404 us  [call(): pl.pallas_call(kernel, out_shape=tuple((shape for shape, _ in outs)), in_...]
where the time goes in v9:
time: 424 us; the launch traced here: 421 us
  Pallas kernels  416 us (98%)
    pallas_call x3, Pallas kernels, call(): pl.pallas_call(kernel, out_shape=tuple((shape for shape, _ in outs)), in_...  404 us
    pallas_call x1, Pallas kernels, split_heads(): pl.pallas_call(finish_kernel, grid=(steps,), in_specs=[pl.BlockSpec((4, s...  11.5 us

profile of v9, /device:TPU:13, one launch (start us, length us, event | category | flops | bytes accessed | tf_op | source)
XLA Modules:
  0.0 420.7 jit_solution(5789459433160179153)
XLA Ops:
  1.3 0.1 pad.4.clone
  1.4 0.7 broadcast_in_dim.15
  2.0 0.7 broadcast_in_dim.16
  2.7 0.7 maximum_convert_fusion.gain_s
  3.4 173.0 %shard_map.178 = (bf16[8,256,384]{2,1,0:T(8,128)(2,1)}, bf16[2,128,2048]{2,1,0:T(8,128)(2,1)}, f32[8,2048]{1,0:T(8,128)}, bf16[1024,2048]{1,0:T(8,128)(2,1)}, f3...) custom-call(s32[1]{0:T(128)S(6)} %copy.20.lengths, ...), custom_call_target="tpu_custom_call" | custom-call | tf_op jit(solution)/shard_map/pallas_call | solution.py:1626
  176.4 64.6 %shard_map.179 = (bf16[4,2,256,2048]{3,2,1,0:T(8,128)(2,1)}, bf16[4,128,2048]{2,1,0:T(8,128)(2,1)}, bf16[4,256,2048]{2,1,0:T(8,128)(2,1)}, f32[256,2048]{1,0:T(8...) custom-call(bf16[8,256,2048]{2,1,0:T(8,128)(2,1)} %get-tuple-element.45.gu_h, ...), custom_call_target="tpu_custom_call" | custom-call | tf_op jit(solution)/shard_map/pallas_call | solution.py:1626
  241.0 166.5 %shard_map.180 = (bf16[4,256,2048]{2,1,0:T(8,128)(2,1)}, bf16[4,128,2048]{2,1,0:T(8,128)(2,1)}, bf16[256,2048]{1,0:T(8,128)(2,1)}, bf16[4,384,256]{2,1,0:T(8,128...) custom-call(bf16[4,2,256,2048]{3,2,1,0:T(8,128)(2,1)} %get-tuple-element.51.gu_g, ...), custom_call_target="tpu_custom_call" | custom-call | tf_op jit(solution)/shard_map/pallas_call | solution.py:1626
  407.5 0.8 slice_add_fusion
  408.4 0.6 pad_maximum_fusion
  408.9 11.5 %shard_map.181 = (f32[256,2,4096]{2,1,0:T(2,128)}, f32[4,128,2048]{2,1,0:T(8,128)}, f32[128,2048]{1,0:T(8,128)}, f32[256,1536]{1,0:T(8,128)}, bf16[256,2048]{1,0...) custom-call(bf16[4,256,2048]{2,1,0:T(8,128)(2,1)} %get-tuple-element.66.gu_parts, ...), custom_call_target="tpu_custom_call" | custom-call | tf_op jit(solution)/shard_map/pallas_call | solution.py:1838
  (1 shorter events, 0.0 us)
